TPU v7x, 32 devices: a whole 2x2x4 slice. The times are simulated.
32 devices in a mesh: groups: 2 (over x), ha: 16 (over z, y, core).
Axes of the slice: x: 2, y: 2, z: 4, core: 2. Of those that a mesh axis runs over, the one named last changes fastest.
Arguments:
- video: bfloat16 [8, 64, 192, 192], P('groups', 'ha'), parts along dimension 0, may hold values from -6 to 6
- s1_weight: bfloat16 [3, 3, 192, 128], replicated, may hold values from -0.15625 to 0.15625
- t1_weight: bfloat16 [3, 128, 128], replicated, may hold values from -0.3125 to 0.3125
- r1_weight: bfloat16 [2, 2, 128, 256], replicated, may hold values from -0.25 to 0.25
- s2_weight: bfloat16 [3, 3, 256, 256], replicated, may hold values from -0.125 to 0.125
- t2_weight: bfloat16 [3, 256, 256], replicated, may hold values from -0.21875 to 0.21875
- r2_weight: bfloat16 [2, 2, 256, 512], replicated, may hold values from -0.1875 to 0.1875
- attn_gain: bfloat16 [512], replicated, may hold values from 0.5 to 1.5
- w_query: bfloat16 [512, 512], replicated, may hold values from -2.5 to 2.5
- w_key: bfloat16 [512, 512], replicated, may hold values from -0.27 to 0.27
- w_value: bfloat16 [512, 512], replicated, may hold values from -0.25 to 0.25
- w_out: bfloat16 [512, 512], replicated, may hold values from -1 to 1
Outputs:
- encoded: bfloat16 [8, 16, 48, 512], P('groups', 'ha'), parts along dimension 0
There are 2 independent parts, one for each index of `groups`. A program takes and returns all parts, laid end to end along the dimension named above; an argument that names none is the same for every part. Nothing has to cross between parts.
All inputs are finite; a program needn't handle non-finite values.
Results may differ from a plain program's by a relative error of at most 0.018.
Values may be sent and summed in bfloat16 or wider, within the bound.
No kernel may reach another device: no remote copies, remote signals or barrier semaphores. Data moves between devices by JAX's collectives and lax.ppermute only.
A program may use at most 128 MiB of HBM per device.

v0:
```python
import math

import jax
import jax.numpy as jnp
from jax import lax
from jax.sharding import PartitionSpec as P


def padded_2(block, sides, width):
    for axis, dim in sides:
        count = lax.axis_size(axis)
        forward = [(i, i + 1) for i in range(count - 1)]
        backward = [(target, source) for source, target in forward]
        low = lax.ppermute(
            lax.slice_in_dim(block, block.shape[dim] - width, None, axis=dim), axis, forward
        )
        high = lax.ppermute(lax.slice_in_dim(block, 0, width, axis=dim), axis, backward)
        block = jnp.concatenate([low, block, high], axis=dim)
    return block


def spatial(volume, weight):
    row_count = volume.shape[1] - 2
    col_count = volume.shape[2]
    padded = jnp.pad(volume, ((0, 0), (0, 0), (1, 1), (0, 0)))
    summed = None
    for tap_row in range(3):
        for tap_col in range(3):
            tap_term = jnp.einsum(
                "tywc,co->tywo",
                padded[:, tap_row : tap_row + row_count, tap_col : tap_col + col_count],
                weight[tap_row, tap_col],
                preferred_element_type=jnp.float32,
            )
            summed = tap_term if summed is None else summed + tap_term
    return summed


def temporal(volume, weight):
    frame_count = volume.shape[0]
    padded = jnp.pad(volume, ((2, 0), (0, 0), (0, 0), (0, 0)))
    summed = None
    for tap_time in range(3):
        tap_term = jnp.einsum(
            "tywc,co->tywo",
            padded[tap_time : tap_time + frame_count],
            weight[tap_time],
            preferred_element_type=jnp.float32,
        )
        summed = tap_term if summed is None else summed + tap_term
    return summed


def reduce_pairs(volume, weight):
    frame_count, row_count, col_count, channels = volume.shape
    grouped = volume.reshape(frame_count, row_count // 2, 2, col_count // 2, 2, channels)
    return jnp.einsum("tyixjc,ijco->tyxo", grouped, weight, preferred_element_type=jnp.float32)


def project(normed, weight):
    return jnp.einsum("...c,co->...o", normed, weight, preferred_element_type=jnp.float32).astype(
        jnp.bfloat16
    )


def frame_attention(queries, key_rows, value_rows, score_scale):
    scores = (
        jnp.einsum("qc,kc->qk", queries, key_rows, preferred_element_type=jnp.float32) * score_scale
    )
    top_score = jnp.max(scores, axis=-1, keepdims=True)
    weights = jnp.exp(scores - top_score)
    totals = jnp.sum(weights, axis=-1, keepdims=True)
    attended = (
        jnp.einsum(
            "qk,kc->qc",
            weights.astype(jnp.bfloat16),
            value_rows,
            preferred_element_type=jnp.float32,
        )
        / totals
    )
    return attended.astype(jnp.bfloat16)


def per_device(
    video,
    s1_weight,
    t1_weight,
    r1_weight,
    s2_weight,
    t2_weight,
    r2_weight,
    attn_gain,
    w_query,
    w_key,
    w_value,
    w_out,
):
    video_rows = padded_2(video, (("ha", 1),), 1)
    a_first = spatial(video_rows, s1_weight).astype(jnp.bfloat16)
    h_first = jax.nn.silu(temporal(a_first, t1_weight)).astype(jnp.bfloat16)
    d_first = reduce_pairs(h_first, r1_weight).astype(jnp.bfloat16)
    middle_halo = padded_2(d_first, (("ha", 1),), 1)
    a_second = spatial(middle_halo, s2_weight).astype(jnp.bfloat16)
    h_second = (d_first.astype(jnp.float32) + jax.nn.silu(temporal(a_second, t2_weight))).astype(
        jnp.bfloat16
    )
    h_third = reduce_pairs(h_second, r2_weight).astype(jnp.bfloat16)
    frame_count, row_count, col_count, channels = h_third.shape
    score_scale = 1.0 / math.sqrt(channels)
    residual = h_third.astype(jnp.float32)
    mean_square = jnp.mean(residual * residual, axis=-1, keepdims=True)
    inverse_norm = lax.rsqrt(mean_square + 1e-06)
    normed = (residual * inverse_norm * attn_gain.astype(jnp.float32)).astype(jnp.bfloat16)
    device_count = lax.axis_size("ha")
    group_size = device_count // frame_count
    block_cols = col_count // group_size
    normed_out = jnp.broadcast_to(
        normed[:, None], (frame_count, group_size, row_count, col_count, channels)
    ).reshape(device_count, row_count, col_count, channels)
    normed_in = lax.all_to_all(normed_out, "ha", split_axis=0, concat_axis=0, tiled=True)
    column = lax.axis_index("ha") % group_size * block_cols
    own_sites = lax.dynamic_slice_in_dim(normed_in, column, block_cols, 2)
    queries = project(own_sites.reshape(-1, channels), w_query)
    whole_frame = normed_in.reshape(-1, channels)
    key_rows = project(whole_frame, w_key)
    value_rows = project(whole_frame, w_value)
    attended = frame_attention(queries, key_rows, value_rows, score_scale)
    returned = lax.all_to_all(
        attended.reshape(device_count, row_count, block_cols, channels),
        "ha",
        split_axis=0,
        concat_axis=0,
        tiled=True,
    )
    mixed_rows = jnp.transpose(
        returned.reshape(frame_count, group_size, row_count, block_cols, channels), (0, 2, 1, 3, 4)
    ).reshape(frame_count, row_count, col_count, channels)
    encoded = residual + jnp.einsum(
        "tywc,co->tywo", mixed_rows, w_out, preferred_element_type=jnp.float32
    )
    return encoded.astype(jnp.bfloat16)


def solution(mesh):
    placed = (P("groups", "ha", None, None), P(), P(), P(), P(), P(), P(), P(), P(), P(), P(), P())
    return jax.shard_map(
        per_device,
        mesh=mesh,
        in_specs=placed,
        out_specs=P("groups", "ha", None, None),
        check_vma=False,
    )
```

profile of v0, /device:TPU:0, one launch (start us, length us, event | category | flops | bytes accessed | tf_op | source)
XLA Modules:
  0.0 83.5 jit_solution(14285778196066986101)
XLA Ops:
  0.0 1.3 %fusion.129 = (bf16[4,1,192,192]{3,2,1,0:T(8,128)(2,1)S(1)}, bf16[4,1,192,192]{3,2,1,0:T(8,128)(2,1)S(1)}) fusion(bf16[4,4,192,192]{3,2,1,0:T(8,128)(2,1)} %param.12), kind=kLoop, calls=%fused_computation.150 | loop fusion | bytes 1179648 | tf_op jit(solution)/shard_map/slice | solution.py:15
  1.3 2.4 %collective-permute-start = (bf16[4,1,192,192]{3,2,1,0:T(8,128)(2,1)S(1)}, bf16[4,1,192,192]{3,2,1,0:T(8,128)(2,1)S(1)}, u32[]{:S(2)}, u32[]{:S(2)}) collective-permute-start(bf16[4,1,192,192]{3,2,1,0:T(8,128)(2,1)S(1)} %get-tuple-element.5), channel_id=1, source_target_pairs={{0,1},{1,2},{2,3},{3,4},{4,5},{5,6},{6,7},{7,8},{8,9},{9,10},{10,1... | collective-permute-start | bytes 884744 | tf_op jit(solution)/shard_map/ppermute | solution.py:14
  3.8 1.3 %collective-permute-start.1 = (bf16[4,1,192,192]{3,2,1,0:T(8,128)(2,1)S(1)}, bf16[4,1,192,192]{3,2,1,0:T(8,128)(2,1)S(1)}, u32[]{:S(2)}, u32[]{:S(2)}) collective-permute-start(bf16[4,1,192,192]{3,2,1,0:T(8,128)(2,1)S(1)} %get-tuple-element.6), channel_id=1, source_target_pairs={{1,0},{2,1},{3,2},{4,3},{5,4},{6,5},{7,6},{8,7},{9,8},{10,9},{11,1... | collective-permute-start | bytes 884744 | tf_op jit(solution)/shard_map/ppermute | solution.py:17
  5.1 1.3 %fusion.102 = f32[4,4,192,128]{3,2,1,0:T(8,128)S(1)} fusion(bf16[4,4,192,192]{3,2,1,0:T(8,128)(2,1)S(1)} %copy-done.1, bf16[3,3,192,128]{3,2,1,0:T(8,128)(2,1)} %param.13), kind=kOutput, calls=%fused_computation.121 | convolution fusion | flops 150994944 | bytes 2801664 | tf_op jit(solution)/shard_map/tywc,co->tywo/dot_general | solution.py:29
  6.4 3.0 %collective-permute-done.1 = bf16[4,1,192,192]{3,2,1,0:T(8,128)(2,1)S(1)} collective-permute-done((bf16[4,1,192,192]{3,2,1,0:T(8,128)(2,1)S(1)}, bf16[4,1,192,192]{3,2,1,0:T(8,128)(2,1)S(1)}, u32[]{:S(2)}, u32[]{:S(2)}) %collective-permute-start.1) | collective-permute-done | bytes 294944 | tf_op jit(solution)/shard_map/ppermute | solution.py:17
  9.5 1.0 %fusion.5 = bf16[4,6,194,192]{3,2,1,0:T(8,128)(2,1)S(1)} fusion(bf16[4,1,192,192]{3,2,1,0:T(8,128)(2,1)S(1)} %collective-permute-done.1, bf16[4,4,192,192]{3,2,1,0:T(8,128)(2,1)S(1)} %copy-done.1, bf16[4,1,192,192]{3,2,1,0:T(8,128)(2,1)S(1)} %collective-permute-done), kind=kLoop, calls=%fused_computation.9 | loop fusion | flops 10727424 | bytes 3557376 | tf_op jit(solution)/shard_map/concatenate | solution.py:18
  10.4 0.5 fusion.17
  11.0 0.6 fusion.19
  11.6 0.6 fusion.21
  12.1 0.6 fusion.23
  12.7 0.5 fusion.25
  13.3 0.6 fusion.10
  13.8 0.6 fusion.6
  14.4 0.9 %add_convert_fusion = bf16[4,4,192,128]{3,2,1,0:T(8,128)(2,1)S(1)} fusion(f32[4,4,192,128]{3,2,1,0:T(8,128)S(1)} %fusion.10, f32[4,4,192,128]{3,2,1,0:T(8,128)S(1)} %fusion.17, f32[4,4,192,128]{3,2,1,0:T(8,128)S(1)} %fusion.19, f32[4,4,192,128]{3,2,1,0:T(8,128)S(1)} %fusion.102, f32[4,4,192,128]{3,2,1,0:T(8,128)S(1)} %fusion.21, ...), kind=kOutput, calls=%fused_computation.32 | convolution fusion | flops 154533888 | bytes 14991360 | tf_op jit(solution)/shard_map/tywc,co->tywo/dot_general | solution.py:29
  15.4 0.3 fusion.117
  15.7 0.3 fusion.120
  16.1 0.6 multiply_convert_fusion
  17.0 0.4 fusion.33
  17.4 8.0 %collective-permute-start.2 = (bf16[4,1,96,256]{3,2,1,0:T(8,128)(2,1)S(1)}, bf16[4,1,96,256]{3,2,1,0:T(8,128)(2,1)S(1)}, u32[]{:S(2)}, u32[]{:S(2)}) collective-permute-start(bf16[4,1,96,256]{3,2,1,0:T(8,128)(2,1)S(1)} %get-tuple-element.7), channel_id=1, source_target_pairs={{0,1},{1,2},{2,3},{3,4},{4,5},{5,6},{6,7},{7,8},{8,9},{9,10},{10,1... | collective-permute-start | bytes 589832 | tf_op jit(solution)/shard_map/ppermute | solution.py:14
  25.5 1.3 %collective-permute-start.3 = (bf16[4,1,96,256]{3,2,1,0:T(8,128)(2,1)S(1)}, bf16[4,1,96,256]{3,2,1,0:T(8,128)(2,1)S(1)}, u32[]{:S(2)}, u32[]{:S(2)}) collective-permute-start(bf16[4,1,96,256]{3,2,1,0:T(8,128)(2,1)S(1)} %get-tuple-element.8), channel_id=1, source_target_pairs={{1,0},{2,1},{3,2},{4,3},{5,4},{6,5},{7,6},{8,7},{9,8},{10,9},{11,1... | collective-permute-start | bytes 589832 | tf_op jit(solution)/shard_map/ppermute | solution.py:17
  26.8 2.0 %collective-permute-done.3 = bf16[4,1,96,256]{3,2,1,0:T(8,128)(2,1)S(1)} collective-permute-done((bf16[4,1,96,256]{3,2,1,0:T(8,128)(2,1)S(1)}, bf16[4,1,96,256]{3,2,1,0:T(8,128)(2,1)S(1)}, u32[]{:S(2)}, u32[]{:S(2)}) %collective-permute-start.3) | collective-permute-done | bytes 196640 | tf_op jit(solution)/shard_map/ppermute | solution.py:17
  28.8 0.3 fusion.45
  31.6 0.7 copy-done.5
  32.8 0.4 add_convert_fusion.1
  33.4 0.5 multiply_reduce_fusion
  34.0 1.0 %broadcast_in_dim.4 = bf16[4,4,48,512]{3,2,1,0:T(8,128)(2,1)} broadcast(bf16[4,48,512]{2,1,0:T(8,128)(2,1)S(1)} %multiply_convert_fusion.1), dimensions={0,2,3} | broadcast | bytes 983040 | tf_op jit(solution)/shard_map/broadcast_in_dim | solution.py:118
  35.0 10.0 %all-to-all-start = ((bf16[16,1,48,512]{3,2,1,0:T(8,128)(2,1)}), bf16[16,1,48,512]{3,2,1,0:T(8,128)(2,1)S(1)}, u32[]{:S(2)}, u32[]{:S(2)}) async-start(bf16[16,1,48,512]{3,2,1,0:T(8,128)(2,1)} %bitcast.80), calls=%async_computation | async-start | bytes 1572864 | tf_op jit(solution)/shard_map/all_to_all | solution.py:121
  45.0 18.7 %all-to-all-done = bf16[16,1,48,512]{3,2,1,0:T(8,128)(2,1)S(1)} async-done(((bf16[16,1,48,512]{3,2,1,0:T(8,128)(2,1)}), bf16[16,1,48,512]{3,2,1,0:T(8,128)(2,1)S(1)}, u32[]{:S(2)}, u32[]{:S(2)}) %all-to-all-start) | async-done | bytes 786464 | tf_op jit(solution)/shard_map/all_to_all | solution.py:121
  64.1 2.0 %fusion.131 = (f32[192]{0:T(256)S(1)}, f32[192,768]{1,0:T(8,128)S(1)}) fusion(bf16[192,512]{1,0:T(8,128)(2,1)S(1)} %convolution_convert_fusion.2, bf16[768,512]{1,0:T(8,128)(2,1)S(1)} %bitcast.223, bf16[512,512]{1,0:T(8,128)(2,1)} %param.21), kind=kOutput, calls=%fused_computation.152 | convolution fusion | flops 554336064 | bytes 2097920 | tf_op jit(solution)/shard_map/qc,kc->qk/dot_general | solution.py:68
  66.4 0.7 fusion.35
  67.2 15.3 %all_to_all.10 = bf16[16,1,12,512]{3,2,1,0:T(8,128)(2,1)S(1)} all-to-all(bf16[16,1,12,512]{3,2,1,0:T(8,128)(2,1)S(1)} %bitcast.225), channel_id=1, replica_groups=mesh['groups'=2,'ha'=16] {'ha'}, dimensions={0} | all-to-all | bytes 393216 | tf_op jit(solution)/shard_map/all_to_all | solution.py:129
  82.6 1.0 %fusion.39 = bf16[4,1,48,512]{3,2,1,0:T(8,128)(2,1)} fusion(f32[4,48,512]{2,1,0:T(8,128)S(1)} %get-tuple-element.10, bf16[4,48,512]{2,1,0:T(8,128)(2,1)S(1)} %reshape.62, bf16[512,512]{1,0:T(8,128)(2,1)S(1)} %copy-done.4), kind=kOutput, calls=%fused_computation.59 | convolution fusion | flops 100859904 | bytes 1310720 | tf_op jit(solution)/shard_map/tywc,co->tywo/dot_general | solution.py:139
  (45 shorter events, 4.3 us)
Async XLA Ops:
  0.0 33.4 %copy-start = (bf16[2,2,256,512]{3,2,1,0:T(8,128)(2,1)S(1)}, bf16[2,2,256,512]{3,2,1,0:T(8,128)(2,1)}, u32[]{:S(2)}) copy-start(bf16[2,2,256,512]{3,2,1,0:T(8,128)(2,1)} %param.18) | copy-start | bytes 3145732
  0.0 5.1 %copy-start.1 = (bf16[4,4,192,192]{3,2,1,0:T(8,128)(2,1)S(1)}, bf16[4,4,192,192]{3,2,1,0:T(8,128)(2,1)}, u32[]{:S(2)}) copy-start(bf16[4,4,192,192]{3,2,1,0:T(8,128)(2,1)} %param.12) | copy-start | bytes 3538948
  1.3 5.1 %collective-permute-start = (bf16[4,1,192,192]{3,2,1,0:T(8,128)(2,1)S(1)}, bf16[4,1,192,192]{3,2,1,0:T(8,128)(2,1)S(1)}, u32[]{:S(2)}, u32[]{:S(2)}) collective-permute-start(bf16[4,1,192,192]{3,2,1,0:T(8,128)(2,1)S(1)} %get-tuple-element.5), channel_id=1, source_target_pairs={{0,1},{1,2},{2,3},{3,4},{4,5},{5,6},{6,7},{7,8},{8,9},{9,10},{10,1... | collective-permute-start | bytes 884744 | tf_op jit(solution)/shard_map/ppermute | solution.py:14
  3.8 5.7 %collective-permute-start.1 = (bf16[4,1,192,192]{3,2,1,0:T(8,128)(2,1)S(1)}, bf16[4,1,192,192]{3,2,1,0:T(8,128)(2,1)S(1)}, u32[]{:S(2)}, u32[]{:S(2)}) collective-permute-start(bf16[4,1,192,192]{3,2,1,0:T(8,128)(2,1)S(1)} %get-tuple-element.6), channel_id=1, source_target_pairs={{1,0},{2,1},{3,2},{4,3},{5,4},{6,5},{7,6},{8,7},{9,8},{10,9},{11,1... | collective-permute-start | bytes 884744 | tf_op jit(solution)/shard_map/ppermute | solution.py:17
  6.4 4.0 %copy-start.6 = (bf16[3,3,192,128]{3,2,1,0:T(8,128)(2,1)S(1)}, bf16[3,3,192,128]{3,2,1,0:T(8,128)(2,1)}, u32[]{:S(2)}) copy-start(bf16[3,3,192,128]{3,2,1,0:T(8,128)(2,1)} %param.13) | copy-start | bytes 1327108
  14.4 0.9 %copy-start.7 = (bf16[3,128,128]{2,1,0:T(8,128)(2,1)S(1)}, bf16[3,128,128]{2,1,0:T(8,128)(2,1)}, u32[]{:S(2)}) copy-start(bf16[3,128,128]{2,1,0:T(8,128)(2,1)} %param.14) | copy-start | bytes 294916
  16.0 1.0 %copy-start.10 = (bf16[2,2,128,256]{3,2,1,0:T(8,128)(2,1)S(1)}, bf16[2,2,128,256]{3,2,1,0:T(8,128)(2,1)}, u32[]{:S(2)}) copy-start(bf16[2,2,128,256]{3,2,1,0:T(8,128)(2,1)} %param.15) | copy-start | bytes 786436
  16.7 10.1 %copy-start.8 = (bf16[512]{0:T(512)(128)(2,1)S(1)}, bf16[512]{0:T(512)(128)(2,1)}, u32[]{:S(2)}) copy-start(bf16[512]{0:T(512)(128)(2,1)} %param.19) | copy-start | bytes 3076
  17.4 11.7 %copy-start.2 = (bf16[3,3,256,256]{3,2,1,0:T(8,128)(2,1)S(1)}, bf16[3,3,256,256]{3,2,1,0:T(8,128)(2,1)}, u32[]{:S(2)}) copy-start(bf16[3,3,256,256]{3,2,1,0:T(8,128)(2,1)} %param.16) | copy-start | bytes 3538948
  17.4 9.4 %collective-permute-start.2 = (bf16[4,1,96,256]{3,2,1,0:T(8,128)(2,1)S(1)}, bf16[4,1,96,256]{3,2,1,0:T(8,128)(2,1)S(1)}, u32[]{:S(2)}, u32[]{:S(2)}) collective-permute-start(bf16[4,1,96,256]{3,2,1,0:T(8,128)(2,1)S(1)} %get-tuple-element.7), channel_id=1, source_target_pairs={{0,1},{1,2},{2,3},{3,4},{4,5},{5,6},{6,7},{7,8},{8,9},{9,10},{10,1... | collective-permute-start | bytes 589832 | tf_op jit(solution)/shard_map/ppermute | solution.py:14
  25.5 3.3 %collective-permute-start.3 = (bf16[4,1,96,256]{3,2,1,0:T(8,128)(2,1)S(1)}, bf16[4,1,96,256]{3,2,1,0:T(8,128)(2,1)S(1)}, u32[]{:S(2)}, u32[]{:S(2)}) collective-permute-start(bf16[4,1,96,256]{3,2,1,0:T(8,128)(2,1)S(1)} %get-tuple-element.8), channel_id=1, source_target_pairs={{1,0},{2,1},{3,2},{4,3},{5,4},{6,5},{7,6},{8,7},{9,8},{10,9},{11,1... | collective-permute-start | bytes 589832 | tf_op jit(solution)/shard_map/ppermute | solution.py:17
  31.3 1.0 %copy-start.5 = (bf16[3,256,256]{2,1,0:T(8,128)(2,1)S(1)}, bf16[3,256,256]{2,1,0:T(8,128)(2,1)}, u32[]{:S(2)}) copy-start(bf16[3,256,256]{2,1,0:T(8,128)(2,1)} %param.17) | copy-start | bytes 1179652
  34.0 29.8 %copy-start.3 = (bf16[512,512]{1,0:T(8,128)(2,1)S(1)}, bf16[512,512]{1,0:T(8,128)(2,1)}, u32[]{:S(2)}) copy-start(bf16[512,512]{1,0:T(8,128)(2,1)} %param.20) | copy-start | bytes 1572868
  35.0 28.6 %all-to-all-start = ((bf16[16,1,48,512]{3,2,1,0:T(8,128)(2,1)}), bf16[16,1,48,512]{3,2,1,0:T(8,128)(2,1)S(1)}, u32[]{:S(2)}, u32[]{:S(2)}) async-start(bf16[16,1,48,512]{3,2,1,0:T(8,128)(2,1)} %bitcast.80), calls=%async_computation | async-start | bytes 1572864 | tf_op jit(solution)/shard_map/all_to_all | solution.py:121
  64.1 2.3 %copy-start.9 = (bf16[512,512]{1,0:T(8,128)(2,1)S(1)}, bf16[512,512]{1,0:T(8,128)(2,1)}, u32[]{:S(2)}) copy-start(bf16[512,512]{1,0:T(8,128)(2,1)} %param.22) | copy-start | bytes 1572868
  67.1 15.5 %copy-start.4 = (bf16[512,512]{1,0:T(8,128)(2,1)S(1)}, bf16[512,512]{1,0:T(8,128)(2,1)}, u32[]{:S(2)}) copy-start(bf16[512,512]{1,0:T(8,128)(2,1)} %param.23) | copy-start | bytes 1572868
where the time goes:
time: 84 us; the launch traced here: 83.5 us
  waiting for transfers between devices  23.7 us (28%)
  starting transfers between devices  23 us (27%)
  matrix products  15.6 us (19%)
  blocking collectives  15.3 us (18%)
  local copies, waits for them, and re-layouts  3.77 us (4%)
  other arithmetic  1.65 us (2%)
    all_to_all x1, waiting for transfers between devices, per_device(): lax.all_to_all(normed_out, 'ha', split_axis=0, concat_axis=0, tiled=True)  18.7 us
    all_to_all x1, blocking collectives, per_device(): lax.all_to_all(attended.reshape(device_count, row_count, block_cols, chan...  15.3 us
    ppermute x2, starting transfers between devices, padded_2(): lax.ppermute(lax.slice_in_dim(block, block.shape[dim] - width, None, axis...  10.5 us
    all_to_all x1, starting transfers between devices, per_device(): lax.all_to_all(normed_out, 'ha', split_axis=0, concat_axis=0, tiled=True)  9.97 us
    dot_general x18, matrix products, spatial(): jnp.einsum('tywc,co->tywo', padded[:, tap_row:tap_row + row_count, tap_co...  8.57 us
    ppermute x2, waiting for transfers between devices, padded_2(): lax.ppermute(lax.slice_in_dim(block, 0, width, axis=dim), axis, backward)  5.04 us
    ppermute x2, starting transfers between devices, padded_2(): lax.ppermute(lax.slice_in_dim(block, 0, width, axis=dim), axis, backward)  2.58 us
    dot_general x6, matrix products, temporal(): jnp.einsum('tywc,co->tywo', padded[tap_time:tap_time + frame_count], weig...  2.25 us
  transfers between devices with their start and end apart: 5, of which 3 were waited for; matrix products, arithmetic and copies ran while one was open for 2% of the time, Pallas kernels for 0%

commit v1 on v0

v1 whole, which is shorter than its diff:
```python
import math

import jax
import jax.numpy as jnp
from jax import lax
from jax.sharding import PartitionSpec as P


def pair_halo(block, axis, dim, width):
    count = lax.axis_size(axis)
    parity = lax.axis_index(axis) % 2
    top = lax.slice_in_dim(block, 0, width, axis=dim)
    low = lax.slice_in_dim(block, block.shape[dim] - width, None, axis=dim)
    inner = [(i, i ^ 1) for i in range(count)]
    outer = [(i, i + 1) for i in range(1, count - 1, 2)]
    outer = outer + [(target, source) for source, target in outer]
    is_even = parity == 0
    far = lax.ppermute(jnp.where(is_even, top, low), axis, outer)
    near = lax.ppermute(jnp.where(is_even, low, top), axis, inner)
    above = jnp.where(is_even, far, near)
    below = jnp.where(is_even, near, far)
    return jnp.concatenate([above, block, below], axis=dim)


def spatial(volume, weight):
    row_count = volume.shape[1] - 2
    col_count = volume.shape[2]
    padded = jnp.pad(volume, ((0, 0), (0, 0), (1, 1), (0, 0)))
    summed = None
    for tap_row in range(3):
        for tap_col in range(3):
            tap_term = jnp.einsum(
                "tywc,co->tywo",
                padded[:, tap_row : tap_row + row_count, tap_col : tap_col + col_count],
                weight[tap_row, tap_col],
                preferred_element_type=jnp.float32,
            )
            summed = tap_term if summed is None else summed + tap_term
    return summed


def temporal(volume, weight):
    frame_count = volume.shape[0]
    padded = jnp.pad(volume, ((2, 0), (0, 0), (0, 0), (0, 0)))
    summed = None
    for tap_time in range(3):
        tap_term = jnp.einsum(
            "tywc,co->tywo",
            padded[tap_time : tap_time + frame_count],
            weight[tap_time],
            preferred_element_type=jnp.float32,
        )
        summed = tap_term if summed is None else summed + tap_term
    return summed


def reduce_pairs(volume, weight):
    frame_count, row_count, col_count, channels = volume.shape
    grouped = volume.reshape(frame_count, row_count // 2, 2, col_count // 2, 2, channels)
    return jnp.einsum("tyixjc,ijco->tyxo", grouped, weight, preferred_element_type=jnp.float32)


def project(normed, weight):
    return jnp.einsum("...c,co->...o", normed, weight, preferred_element_type=jnp.float32).astype(
        jnp.bfloat16
    )


def frame_attention(own, sites, w_query, w_key, w_value, w_out, score_scale):
    queries = project(own, w_query)
    mapped = jnp.einsum(
        "qc,dc->qd", queries, w_key, preferred_element_type=jnp.float32
    ).astype(jnp.bfloat16)
    scores = (
        jnp.einsum("qc,kc->qk", mapped, sites, preferred_element_type=jnp.float32) * score_scale
    )
    top_score = jnp.max(scores, axis=-1, keepdims=True)
    weights = jnp.exp(scores - top_score)
    totals = jnp.sum(weights, axis=-1, keepdims=True)
    mixed = (
        jnp.einsum(
            "qk,kc->qc", weights.astype(jnp.bfloat16), sites, preferred_element_type=jnp.float32
        )
        / totals
    ).astype(jnp.bfloat16)
    return project(project(mixed, w_value), w_out)


def per_device(
    video,
    s1_weight,
    t1_weight,
    r1_weight,
    s2_weight,
    t2_weight,
    r2_weight,
    attn_gain,
    w_query,
    w_key,
    w_value,
    w_out,
):
    video_rows = pair_halo(video, "ha", 1, 1)
    a_first = spatial(video_rows, s1_weight).astype(jnp.bfloat16)
    h_first = jax.nn.silu(temporal(a_first, t1_weight)).astype(jnp.bfloat16)
    d_first = reduce_pairs(h_first, r1_weight).astype(jnp.bfloat16)
    middle_halo = pair_halo(d_first, "ha", 1, 1)
    a_second = spatial(middle_halo, s2_weight).astype(jnp.bfloat16)
    h_second = (d_first.astype(jnp.float32) + jax.nn.silu(temporal(a_second, t2_weight))).astype(
        jnp.bfloat16
    )
    h_third = reduce_pairs(h_second, r2_weight).astype(jnp.bfloat16)
    frame_count, row_count, col_count, channels = h_third.shape
    score_scale = 1.0 / math.sqrt(channels)
    residual = h_third.astype(jnp.float32)
    mean_square = jnp.mean(residual * residual, axis=-1, keepdims=True)
    inverse_norm = lax.rsqrt(mean_square + 1e-06)
    normed = (residual * inverse_norm * attn_gain.astype(jnp.float32)).astype(jnp.bfloat16)
    device_count = lax.axis_size("ha")
    group_size = device_count // frame_count
    own_frame = lax.axis_index("ha") // group_size
    steps = range(frame_count)
    flat = normed.reshape(frame_count, row_count * col_count, channels)
    turns = [
        [(d, (d // group_size ^ k) * group_size + d % group_size) for d in range(device_count)]
        for k in steps
    ]
    picked = [lax.dynamic_index_in_dim(flat, own_frame ^ k, 0, keepdims=False) for k in steps]
    own = jnp.concatenate(
        [picked[0]] + [lax.ppermute(picked[k], "ha", turns[k]) for k in steps if k], axis=0
    )
    sites = own
    bit = group_size // 2
    while bit:
        sites = jnp.concatenate(
            [sites, lax.ppermute(sites, "ha", [(d, d ^ bit) for d in range(device_count)])], axis=0
        )
        bit //= 2
    mixed = frame_attention(own, sites, w_query, w_key, w_value, w_out, score_scale)
    mixed = mixed.reshape(frame_count, row_count * col_count, channels)
    back = jnp.stack([mixed[0]] + [lax.ppermute(mixed[k], "ha", turns[k]) for k in steps if k])
    back = jnp.stack(
        [lax.dynamic_index_in_dim(back, own_frame ^ t, 0, keepdims=False) for t in steps]
    )
    encoded = residual + back.reshape(residual.shape).astype(jnp.float32)
    return encoded.astype(jnp.bfloat16)


def solution(mesh):
    placed = (P("groups", "ha", None, None), P(), P(), P(), P(), P(), P(), P(), P(), P(), P(), P())
    return jax.shard_map(
        per_device,
        mesh=mesh,
        in_specs=placed,
        out_specs=P("groups", "ha", None, None),
        check_vma=False,
    )
```

time: 84 us -> 67.2 us (0.80)
  blocking collectives: 15.3 us -> 0 us
  waiting for transfers between devices: 23.7 us -> 15 us
  starting transfers between devices: 23 us -> 28.6 us
  other arithmetic: 1.65 us -> 5.64 us
  local copies, waits for them, and re-layouts: 3.77 us -> 1.42 us
    all_to_all x1 -> x0, waiting for transfers between devices: 18.7 us -> none  [per_device(): lax.all_to_all(normed_out, 'ha', split_axis=0, concat_axis=0, tiled=True)]
    ppermute x4 -> x12, starting transfers between devices: 13 us -> 28.6 us  [the longest x2 15.8 us: pair_halo(): near = lax.ppermute(jnp.where(is_even, low, top), axis, inner)]
    all_to_all x1 -> x0, blocking collectives: 15.3 us -> none  [per_device(): lax.all_to_all(attended.reshape(device_count, row_count, block_cols, chan...]
    all_to_all x1 -> x0, starting transfers between devices: 9.97 us -> none  [per_device(): lax.all_to_all(normed_out, 'ha', split_axis=0, concat_axis=0, tiled=True)]
    ppermute x4 -> x12, waiting for transfers between devices: 5.04 us -> 15 us  [the longest x3 5.64 us: per_device(): lax.ppermute(picked[k], 'ha', turns[k])]
    select_n x0 -> x4, other arithmetic: none -> 3.19 us  [the longest x2 2.11 us: pair_halo(): far = lax.ppermute(jnp.where(is_even, top, low), axis, outer)]
    dot_general x1 -> x2, matrix products: 0.26 us -> 1.96 us  [project(): jnp.einsum('...c,co->...o', normed, weight, preferred_element_type=jnp.fl...]
    dot_general x3 -> x2, matrix products: 3.69 us -> 2.19 us  [the longest x1 1.68 us: frame_attention(): jnp.einsum('qc,dc->qd', queries, w_key, preferred_element_type=jnp.float32)]
  transfers between devices with their start and end apart: 5 -> 12, of which waited for: 3 -> 7; matrix products, arithmetic and copies ran while one was open for 2% -> 5% of each run, Pallas kernels for 0% -> 0%
where the time goes in v1:
time: 67.2 us; the launch traced here: 66.9 us
  starting transfers between devices  28.6 us (43%)
  matrix products  15.8 us (24%)
  waiting for transfers between devices  15 us (22%)
  other arithmetic  5.64 us (8%)
  local copies, waits for them, and re-layouts  1.42 us (2%)
    ppermute x2, starting transfers between devices, pair_halo(): near = lax.ppermute(jnp.where(is_even, low, top), axis, inner)  15.8 us
    dot_general x18, matrix products, spatial(): jnp.einsum('tywc,co->tywo', padded[:, tap_row:tap_row + row_count, tap_co...  8.66 us
    ppermute x3, waiting for transfers between devices, per_device(): lax.ppermute(picked[k], 'ha', turns[k])  5.64 us
    ppermute x2, waiting for transfers between devices, per_device(): lax.ppermute(sites, 'ha', [(d, d ^ bit) for d in range(device_count)])  4.86 us
    ppermute x3, starting transfers between devices, per_device(): lax.ppermute(picked[k], 'ha', turns[k])  4.45 us
    ppermute x3, starting transfers between devices, per_device(): lax.ppermute(mixed[k], 'ha', turns[k])  4.44 us
    ppermute x3, waiting for transfers between devices, per_device(): lax.ppermute(mixed[k], 'ha', turns[k])  3.54 us
    ppermute x2, starting transfers between devices, per_device(): lax.ppermute(sites, 'ha', [(d, d ^ bit) for d in range(device_count)])  2.57 us
  transfers between devices with their start and end apart: 12, of which 7 were waited for; matrix products, arithmetic and copies ran while one was open for 5% of the time, Pallas kernels for 0%

profile of v1, /device:TPU:0, one launch (start us, length us, event | category | flops | bytes accessed | tf_op | source)
XLA Modules:
  0.0 66.9 jit_solution(11907390746806560787)
XLA Ops:
  0.0 2.1 %broadcast_select_fusion.3 = (bf16[4,1,192,192]{3,2,1,0:T(8,128)(2,1)}, bf16[4,1,192,192]{3,2,1,0:T(8,128)(2,1)S(1)}) fusion(pred[]{:T(512)S(6)} %eq.7, bf16[4,4,192,192]{3,2,1,0:T(8,128)(2,1)} %param.12), kind=kLoop, calls=%fused_computation.92 | loop fusion | flops 294912 | bytes 1179649 | tf_op jit(solution)/shard_map/jit(_where)/select_n | solution.py:18
  2.1 0.7 %collective-permute-start = (bf16[4,1,192,192]{3,2,1,0:T(8,128)(2,1)}, bf16[4,1,192,192]{3,2,1,0:T(8,128)(2,1)S(1)}, u32[]{:S(2)}, u32[]{:S(2)}) collective-permute-start(bf16[4,1,192,192]{3,2,1,0:T(8,128)(2,1)} %get-tuple-element.7), channel_id=1, source_target_pairs={{1,2},{3,4},{5,6},{7,8},{9,10},{11,12},{13,14},{2,1},{4,3},{6,5},{... | collective-permute-start | bytes 884744 | tf_op jit(solution)/shard_map/ppermute | solution.py:18
  2.8 4.4 %collective-permute-start.1 = (bf16[4,1,192,192]{3,2,1,0:T(8,128)(2,1)S(1)}, bf16[4,1,192,192]{3,2,1,0:T(8,128)(2,1)}, u32[]{:S(2)}, u32[]{:S(2)}) collective-permute-start(bf16[4,1,192,192]{3,2,1,0:T(8,128)(2,1)S(1)} %get-tuple-element.8), channel_id=1, source_target_pairs={{0,1},{1,0},{2,3},{3,2},{4,5},{5,4},{6,7},{7,6},{8,9},{9,8},{10,11... | collective-permute-start | bytes 884744 | tf_op jit(solution)/shard_map/ppermute | solution.py:19
  7.2 1.3 %fusion.109 = f32[4,4,192,128]{3,2,1,0:T(8,128)S(1)} fusion(bf16[4,4,192,192]{3,2,1,0:T(8,128)(2,1)S(1)} %copy-done.1, bf16[3,3,192,128]{3,2,1,0:T(8,128)(2,1)} %param.13), kind=kOutput, calls=%fused_computation.135 | convolution fusion | flops 150994944 | bytes 2801664 | tf_op jit(solution)/shard_map/tywc,co->tywo/dot_general | solution.py:32
  8.7 1.1 %broadcast_select_fusion.1 = (bf16[4,1,192,192]{3,2,1,0:T(8,128)(2,1)S(1)}, bf16[4,1,192,192]{3,2,1,0:T(8,128)(2,1)S(1)}) fusion(bf16[4,1,192,192]{3,2,1,0:T(8,128)(2,1)S(1)} %collective-permute-done, bf16[4,1,192,192]{3,2,1,0:T(8,128)(2,1)} %collective-permute-done.1, pred[]{:T(512)S(6)} %eq.7), kind=kLoop, calls=%fused_computation.90 | loop fusion | flops 294912 | bytes 1179649 | tf_op jit(solution)/shard_map/jit(_where)/select_n | solution.py:20
  9.7 1.0 %fusion.5 = bf16[4,6,194,192]{3,2,1,0:T(8,128)(2,1)S(1)} fusion(bf16[4,1,192,192]{3,2,1,0:T(8,128)(2,1)S(1)} %get-tuple-element.10, bf16[4,4,192,192]{3,2,1,0:T(8,128)(2,1)S(1)} %copy-done.1, bf16[4,1,192,192]{3,2,1,0:T(8,128)(2,1)S(1)} %get-tuple-element.9), kind=kLoop, calls=%fused_computation.9 | loop fusion | flops 10727424 | bytes 3557376 | tf_op jit(solution)/shard_map/concatenate | solution.py:22
  10.7 0.5 fusion.17
  11.3 0.6 fusion.19
  11.9 0.6 fusion.21
  12.4 0.6 fusion.23
  13.0 0.5 fusion.25
  13.6 0.6 fusion.10
  14.1 0.6 fusion.6
  14.7 0.9 %add_convert_fusion = bf16[4,4,192,128]{3,2,1,0:T(8,128)(2,1)S(1)} fusion(f32[4,4,192,128]{3,2,1,0:T(8,128)S(1)} %fusion.10, f32[4,4,192,128]{3,2,1,0:T(8,128)S(1)} %fusion.17, f32[4,4,192,128]{3,2,1,0:T(8,128)S(1)} %fusion.19, f32[4,4,192,128]{3,2,1,0:T(8,128)S(1)} %fusion.109, f32[4,4,192,128]{3,2,1,0:T(8,128)S(1)} %fusion.21, ...), kind=kOutput, calls=%fused_computation.32 | convolution fusion | flops 154533888 | bytes 14991360 | tf_op jit(solution)/shard_map/tywc,co->tywo/dot_general | solution.py:32
  16.3 0.6 multiply_convert_fusion
  17.7 0.7 %collective-permute-start.2 = (bf16[4,1,96,256]{3,2,1,0:T(8,128)(2,1)S(1)}, bf16[4,1,96,256]{3,2,1,0:T(8,128)(2,1)S(1)}, u32[]{:S(2)}, u32[]{:S(2)}) collective-permute-start(bf16[4,1,96,256]{3,2,1,0:T(8,128)(2,1)S(1)} %get-tuple-element.13), channel_id=1, source_target_pairs={{1,2},{3,4},{5,6},{7,8},{9,10},{11,12},{13,14},{2,1},{4,3},{6,5},{... | collective-permute-start | bytes 589832 | tf_op jit(solution)/shard_map/ppermute | solution.py:18
  18.4 11.4 %collective-permute-start.3 = (bf16[4,1,96,256]{3,2,1,0:T(8,128)(2,1)S(1)}, bf16[4,1,96,256]{3,2,1,0:T(8,128)(2,1)S(1)}, u32[]{:S(2)}, u32[]{:S(2)}) collective-permute-start(bf16[4,1,96,256]{3,2,1,0:T(8,128)(2,1)S(1)} %get-tuple-element.14), channel_id=1, source_target_pairs={{0,1},{1,0},{2,3},{3,2},{4,5},{5,4},{6,7},{7,6},{8,9},{9,8},{10,11... | collective-permute-start | bytes 589832 | tf_op jit(solution)/shard_map/ppermute | solution.py:19
  30.0 0.8 %collective-permute-done.3 = bf16[4,1,96,256]{3,2,1,0:T(8,128)(2,1)S(1)} collective-permute-done((bf16[4,1,96,256]{3,2,1,0:T(8,128)(2,1)S(1)}, bf16[4,1,96,256]{3,2,1,0:T(8,128)(2,1)S(1)}, u32[]{:S(2)}, u32[]{:S(2)}) %collective-permute-start.3) | collective-permute-done | bytes 196640 | tf_op jit(solution)/shard_map/ppermute | solution.py:19
  33.4 0.7 %copy-done.4 = bf16[3,256,256]{2,1,0:T(8,128)(2,1)S(1)} copy-done((bf16[3,256,256]{2,1,0:T(8,128)(2,1)S(1)}, bf16[3,256,256]{2,1,0:T(8,128)(2,1)}, u32[]{:S(2)}) %copy-start.4) | copy-done | bytes 393240
  35.9 1.7 %collective-permute-start.4 = (bf16[48,512]{1,0:T(8,128)(2,1)S(1)}, bf16[48,512]{1,0:T(8,128)(2,1)S(1)}, u32[]{:S(2)}, u32[]{:S(2)}) collective-permute-start(bf16[48,512]{1,0:T(8,128)(2,1)S(1)} %get-tuple-element.27), channel_id=1, source_target_pairs={{0,4},{1,5},{2,6},{3,7},{4,0},{5,1},{6,2},{7,3},{8,12},{9,13},{10,... | collective-permute-start | bytes 147464 | tf_op jit(solution)/shard_map/ppermute | solution.py:130
  37.6 2.6 %collective-permute-start.5 = (bf16[48,512]{1,0:T(8,128)(2,1)S(1)}, bf16[48,512]{1,0:T(8,128)(2,1)S(1)}, u32[]{:S(2)}, u32[]{:S(2)}) collective-permute-start(bf16[48,512]{1,0:T(8,128)(2,1)S(1)} %get-tuple-element.26), channel_id=1, source_target_pairs={{0,8},{1,9},{2,10},{3,11},{4,12},{5,13},{6,14},{7,15},{8,0},{9,1},... | collective-permute-start | bytes 147464 | tf_op jit(solution)/shard_map/ppermute | solution.py:130
  40.4 2.8 %collective-permute-done.5 = bf16[48,512]{1,0:T(8,128)(2,1)S(1)} collective-permute-done((bf16[48,512]{1,0:T(8,128)(2,1)S(1)}, bf16[48,512]{1,0:T(8,128)(2,1)S(1)}, u32[]{:S(2)}, u32[]{:S(2)}) %collective-permute-start.5) | collective-permute-done | bytes 49184 | tf_op jit(solution)/shard_map/ppermute | solution.py:130
  43.2 2.9 %collective-permute-done.6 = bf16[48,512]{1,0:T(8,128)(2,1)S(1)} collective-permute-done((bf16[48,512]{1,0:T(8,128)(2,1)S(1)}, bf16[48,512]{1,0:T(8,128)(2,1)S(1)}, u32[]{:S(2)}, u32[]{:S(2)}) %collective-permute-start.6) | collective-permute-done | bytes 49184 | tf_op jit(solution)/shard_map/ppermute | solution.py:130
  46.0 2.5 %collective-permute-start.7 = (bf16[192,512]{1,0:T(8,128)(2,1)S(1)}, bf16[192,512]{1,0:T(8,128)(2,1)S(1)}, u32[]{:S(2)}, u32[]{:S(2)}) collective-permute-start(bf16[192,512]{1,0:T(8,128)(2,1)S(1)} %pad_maximum_fusion), channel_id=1, source_target_pairs={{0,2},{1,3},{2,0},{3,1},{4,6},{5,7},{6,4},{7,5},{8,10},{9,11},{10,... | collective-permute-start | bytes 589832 | tf_op jit(solution)/shard_map/ppermute | solution.py:136
  48.6 4.8 %collective-permute-done.7 = bf16[192,512]{1,0:T(8,128)(2,1)S(1)} collective-permute-done((bf16[192,512]{1,0:T(8,128)(2,1)S(1)}, bf16[192,512]{1,0:T(8,128)(2,1)S(1)}, u32[]{:S(2)}, u32[]{:S(2)}) %collective-permute-start.7) | collective-permute-done | bytes 196640 | tf_op jit(solution)/shard_map/ppermute | solution.py:136
  53.5 1.7 %convolution_convert_fusion.2 = bf16[192,512]{1,0:T(8,128)(2,1)S(1)} fusion(bf16[512,512]{1,0:T(8,128)(2,1)} %param.21, bf16[512,512]{1,0:T(8,128)(2,1)} %param.20, bf16[48,512]{1,0:T(8,128)(2,1)S(1)} %collective-permute-done.6, bf16[48,512]{1,0:T(8,128)(2,1)S(1)} %collective-permute-done.5, bf16[48,512]{1,0:T(8,128)(2,1)S(1)} %collective-permute-done.4, ...), kind=kOutput, calls=%fused_computation.52 | convolution fusion | flops 202309632 | bytes 1441792 | tf_op jit(solution)/shard_map/qc,dc->qd/dot_general | solution.py:71
  56.1 1.7 %convolution_convert_fusion.1 = bf16[192,512]{1,0:T(8,128)(2,1)S(1)} fusion(bf16[512,512]{1,0:T(8,128)(2,1)} %param.22, bf16[768,512]{1,0:T(8,128)(2,1)S(1)} %constant_dynamic-update-slice_fusion.5, f32[192,768]{1,0:T(8,128)S(1)} %get-tuple-element.37, f32[192]{0:T(256)S(1)} %get-tuple-element.36, f32[192]{0:T(256)S(1)} %fusion.52), kind=kOutput, calls=%fused_computation.51 | convolution fusion | flops 252248064 | bytes 2098688 | tf_op jit(solution)/shard_map/...c,co->...o/dot_general | solution.py:64
  58.1 2.0 %collective-permute-start.10 = (bf16[48,512]{1,0:T(8,128)(2,1)S(1)}, bf16[48,512]{1,0:T(8,128)(2,1)S(1)}, u32[]{:S(2)}, u32[]{:S(2)}) collective-permute-start(bf16[48,512]{1,0:T(8,128)(2,1)S(1)} %get-tuple-element.21), channel_id=1, source_target_pairs={{0,8},{1,9},{2,10},{3,11},{4,12},{5,13},{6,14},{7,15},{8,0},{9,1},... | collective-permute-start | bytes 147464 | tf_op jit(solution)/shard_map/ppermute | solution.py:141
  60.2 2.3 %collective-permute-start.11 = (bf16[48,512]{1,0:T(8,128)(2,1)S(1)}, bf16[48,512]{1,0:T(8,128)(2,1)S(1)}, u32[]{:S(2)}, u32[]{:S(2)}) collective-permute-start(bf16[48,512]{1,0:T(8,128)(2,1)S(1)} %get-tuple-element.20), channel_id=1, source_target_pairs={{0,12},{1,13},{2,14},{3,15},{4,8},{5,9},{6,10},{7,11},{8,4},{9,5},... | collective-permute-start | bytes 147464 | tf_op jit(solution)/shard_map/ppermute | solution.py:141
  62.5 0.8 %collective-permute-done.10 = bf16[48,512]{1,0:T(8,128)(2,1)S(1)} collective-permute-done((bf16[48,512]{1,0:T(8,128)(2,1)S(1)}, bf16[48,512]{1,0:T(8,128)(2,1)S(1)}, u32[]{:S(2)}, u32[]{:S(2)}) %collective-permute-start.10) | collective-permute-done | bytes 49184 | tf_op jit(solution)/shard_map/ppermute | solution.py:141
  63.3 2.8 %collective-permute-done.11 = bf16[48,512]{1,0:T(8,128)(2,1)S(1)} collective-permute-done((bf16[48,512]{1,0:T(8,128)(2,1)S(1)}, bf16[48,512]{1,0:T(8,128)(2,1)S(1)}, u32[]{:S(2)}, u32[]{:S(2)}) %collective-permute-start.11) | collective-permute-done | bytes 49184 | tf_op jit(solution)/shard_map/ppermute | solution.py:141
  66.1 0.7 %fusion.72 = bf16[4,1,48,512]{3,2,1,0:T(8,128)(2,1)} fusion(f32[4,48,512]{2,1,0:T(8,128)S(1)} %get-tuple-element.35, bf16[1,48,512]{2,1,0:T(8,128)(2,1)S(1)} %get-tuple-element.16, bf16[1,48,512]{2,1,0:T(8,128)(2,1)S(1)} %get-tuple-element.17, bf16[1,48,512]{2,1,0:T(8,128)(2,1)S(1)} %get-tuple-element.18, bf16[1,48,512]{2,1,0:T(8,128)(2,1)S(1)} %get-tuple-element.15), kind=kLoop, calls=%fused_computation.95 | loop fusion | flops 589824 | bytes 786432 | tf_op jit(solution)/shard_map/convert_element_type | solution.py:146
  (64 shorter events, 7.7 us)
Async XLA Ops:
  0.0 35.3 %copy-start = (bf16[2,2,256,512]{3,2,1,0:T(8,128)(2,1)S(1)}, bf16[2,2,256,512]{3,2,1,0:T(8,128)(2,1)}, u32[]{:S(2)}) copy-start(bf16[2,2,256,512]{3,2,1,0:T(8,128)(2,1)} %param.18) | copy-start | bytes 3145732
  0.0 7.2 %copy-start.1 = (bf16[4,4,192,192]{3,2,1,0:T(8,128)(2,1)S(1)}, bf16[4,4,192,192]{3,2,1,0:T(8,128)(2,1)}, u32[]{:S(2)}) copy-start(bf16[4,4,192,192]{3,2,1,0:T(8,128)(2,1)} %param.12) | copy-start | bytes 3538948
  0.0 7.2 %copy-start.7 = (bf16[512]{0:T(512)(128)(2,1)S(1)}, bf16[512]{0:T(512)(128)(2,1)}, u32[]{:S(2)}) copy-start(bf16[512]{0:T(512)(128)(2,1)} %param.19) | copy-start | bytes 3076
  2.1 6.5 %collective-permute-start = (bf16[4,1,192,192]{3,2,1,0:T(8,128)(2,1)}, bf16[4,1,192,192]{3,2,1,0:T(8,128)(2,1)S(1)}, u32[]{:S(2)}, u32[]{:S(2)}) collective-permute-start(bf16[4,1,192,192]{3,2,1,0:T(8,128)(2,1)} %get-tuple-element.7), channel_id=1, source_target_pairs={{1,2},{3,4},{5,6},{7,8},{9,10},{11,12},{13,14},{2,1},{4,3},{6,5},{... | collective-permute-start | bytes 884744 | tf_op jit(solution)/shard_map/ppermute | solution.py:18
  2.8 5.9 %collective-permute-start.1 = (bf16[4,1,192,192]{3,2,1,0:T(8,128)(2,1)S(1)}, bf16[4,1,192,192]{3,2,1,0:T(8,128)(2,1)}, u32[]{:S(2)}, u32[]{:S(2)}) collective-permute-start(bf16[4,1,192,192]{3,2,1,0:T(8,128)(2,1)S(1)} %get-tuple-element.8), channel_id=1, source_target_pairs={{0,1},{1,0},{2,3},{3,2},{4,5},{5,4},{6,7},{7,6},{8,9},{9,8},{10,11... | collective-permute-start | bytes 884744 | tf_op jit(solution)/shard_map/ppermute | solution.py:19
  9.7 1.0 %copy-start.5 = (bf16[3,3,192,128]{3,2,1,0:T(8,128)(2,1)S(1)}, bf16[3,3,192,128]{3,2,1,0:T(8,128)(2,1)}, u32[]{:S(2)}) copy-start(bf16[3,3,192,128]{3,2,1,0:T(8,128)(2,1)} %param.13) | copy-start | bytes 1327108
  14.7 0.9 %copy-start.6 = (bf16[3,128,128]{2,1,0:T(8,128)(2,1)S(1)}, bf16[3,128,128]{2,1,0:T(8,128)(2,1)}, u32[]{:S(2)}) copy-start(bf16[3,128,128]{2,1,0:T(8,128)(2,1)} %param.14) | copy-start | bytes 294916
  16.3 1.0 %copy-start.8 = (bf16[2,2,128,256]{3,2,1,0:T(8,128)(2,1)S(1)}, bf16[2,2,128,256]{3,2,1,0:T(8,128)(2,1)}, u32[]{:S(2)}) copy-start(bf16[2,2,128,256]{3,2,1,0:T(8,128)(2,1)} %param.15) | copy-start | bytes 786436
  16.9 12.8 %copy-start.2 = (bf16[3,3,256,256]{3,2,1,0:T(8,128)(2,1)S(1)}, bf16[3,3,256,256]{3,2,1,0:T(8,128)(2,1)}, u32[]{:S(2)}) copy-start(bf16[3,3,256,256]{3,2,1,0:T(8,128)(2,1)} %param.16) | copy-start | bytes 3538948
  17.7 12.3 %collective-permute-start.2 = (bf16[4,1,96,256]{3,2,1,0:T(8,128)(2,1)S(1)}, bf16[4,1,96,256]{3,2,1,0:T(8,128)(2,1)S(1)}, u32[]{:S(2)}, u32[]{:S(2)}) collective-permute-start(bf16[4,1,96,256]{3,2,1,0:T(8,128)(2,1)S(1)} %get-tuple-element.13), channel_id=1, source_target_pairs={{1,2},{3,4},{5,6},{7,8},{9,10},{11,12},{13,14},{2,1},{4,3},{6,5},{... | collective-permute-start | bytes 589832 | tf_op jit(solution)/shard_map/ppermute | solution.py:18
  18.4 12.4 %collective-permute-start.3 = (bf16[4,1,96,256]{3,2,1,0:T(8,128)(2,1)S(1)}, bf16[4,1,96,256]{3,2,1,0:T(8,128)(2,1)S(1)}, u32[]{:S(2)}, u32[]{:S(2)}) collective-permute-start(bf16[4,1,96,256]{3,2,1,0:T(8,128)(2,1)S(1)} %get-tuple-element.14), channel_id=1, source_target_pairs={{0,1},{1,0},{2,3},{3,2},{4,5},{5,4},{6,7},{7,6},{8,9},{9,8},{10,11... | collective-permute-start | bytes 589832 | tf_op jit(solution)/shard_map/ppermute | solution.py:19
  33.2 1.0 %copy-start.4 = (bf16[3,256,256]{2,1,0:T(8,128)(2,1)S(1)}, bf16[3,256,256]{2,1,0:T(8,128)(2,1)}, u32[]{:S(2)}) copy-start(bf16[3,256,256]{2,1,0:T(8,128)(2,1)} %param.17) | copy-start | bytes 1179652
  35.9 4.5 %collective-permute-start.4 = (bf16[48,512]{1,0:T(8,128)(2,1)S(1)}, bf16[48,512]{1,0:T(8,128)(2,1)S(1)}, u32[]{:S(2)}, u32[]{:S(2)}) collective-permute-start(bf16[48,512]{1,0:T(8,128)(2,1)S(1)} %get-tuple-element.27), channel_id=1, source_target_pairs={{0,4},{1,5},{2,6},{3,7},{4,0},{5,1},{6,2},{7,3},{8,12},{9,13},{10,... | collective-permute-start | bytes 147464 | tf_op jit(solution)/shard_map/ppermute | solution.py:130
  37.6 5.6 %collective-permute-start.5 = (bf16[48,512]{1,0:T(8,128)(2,1)S(1)}, bf16[48,512]{1,0:T(8,128)(2,1)S(1)}, u32[]{:S(2)}, u32[]{:S(2)}) collective-permute-start(bf16[48,512]{1,0:T(8,128)(2,1)S(1)} %get-tuple-element.26), channel_id=1, source_target_pairs={{0,8},{1,9},{2,10},{3,11},{4,12},{5,13},{6,14},{7,15},{8,0},{9,1},... | collective-permute-start | bytes 147464 | tf_op jit(solution)/shard_map/ppermute | solution.py:130
  40.1 5.9 %collective-permute-start.6 = (bf16[48,512]{1,0:T(8,128)(2,1)S(1)}, bf16[48,512]{1,0:T(8,128)(2,1)S(1)}, u32[]{:S(2)}, u32[]{:S(2)}) collective-permute-start(bf16[48,512]{1,0:T(8,128)(2,1)S(1)} %get-tuple-element.25), channel_id=1, source_target_pairs={{0,12},{1,13},{2,14},{3,15},{4,8},{5,9},{6,10},{7,11},{8,4},{9,5},... | collective-permute-start | bytes 147464 | tf_op jit(solution)/shard_map/ppermute | solution.py:130
  46.0 7.4 %collective-permute-start.7 = (bf16[192,512]{1,0:T(8,128)(2,1)S(1)}, bf16[192,512]{1,0:T(8,128)(2,1)S(1)}, u32[]{:S(2)}, u32[]{:S(2)}) collective-permute-start(bf16[192,512]{1,0:T(8,128)(2,1)S(1)} %pad_maximum_fusion), channel_id=1, source_target_pairs={{0,2},{1,3},{2,0},{3,1},{4,6},{5,7},{6,4},{7,5},{8,10},{9,11},{10,... | collective-permute-start | bytes 589832 | tf_op jit(solution)/shard_map/ppermute | solution.py:136
  53.5 1.8 %collective-permute-start.8 = (bf16[384,512]{1,0:T(8,128)(2,1)S(1)}, bf16[384,512]{1,0:T(8,128)(2,1)S(1)}, u32[]{:S(2)}, u32[]{:S(2)}) collective-permute-start(bf16[384,512]{1,0:T(8,128)(2,1)S(1)} %get-tuple-element.23), channel_id=1, source_target_pairs={{0,1},{1,0},{2,3},{3,2},{4,5},{5,4},{6,7},{7,6},{8,9},{9,8},{10,11... | collective-permute-start | bytes 1179656 | tf_op jit(solution)/shard_map/ppermute | solution.py:136
  56.0 1.7 %copy-start.3 = (bf16[512,512]{1,0:T(8,128)(2,1)S(1)}, bf16[512,512]{1,0:T(8,128)(2,1)}, u32[]{:S(2)}) copy-start(bf16[512,512]{1,0:T(8,128)(2,1)} %param.23) | copy-start | bytes 1572868
  58.1 4.5 %collective-permute-start.9 = (bf16[48,512]{1,0:T(8,128)(2,1)S(1)}, bf16[48,512]{1,0:T(8,128)(2,1)S(1)}, u32[]{:S(2)}, u32[]{:S(2)}) collective-permute-start(bf16[48,512]{1,0:T(8,128)(2,1)S(1)} %get-tuple-element.22), channel_id=1, source_target_pairs={{0,4},{1,5},{2,6},{3,7},{4,0},{5,1},{6,2},{7,3},{8,12},{9,13},{10,... | collective-permute-start | bytes 147464 | tf_op jit(solution)/shard_map/ppermute | solution.py:141
  58.1 5.2 %collective-permute-start.10 = (bf16[48,512]{1,0:T(8,128)(2,1)S(1)}, bf16[48,512]{1,0:T(8,128)(2,1)S(1)}, u32[]{:S(2)}, u32[]{:S(2)}) collective-permute-start(bf16[48,512]{1,0:T(8,128)(2,1)S(1)} %get-tuple-element.21), channel_id=1, source_target_pairs={{0,8},{1,9},{2,10},{3,11},{4,12},{5,13},{6,14},{7,15},{8,0},{9,1},... | collective-permute-start | bytes 147464 | tf_op jit(solution)/shard_map/ppermute | solution.py:141
  60.2 5.9 %collective-permute-start.11 = (bf16[48,512]{1,0:T(8,128)(2,1)S(1)}, bf16[48,512]{1,0:T(8,128)(2,1)S(1)}, u32[]{:S(2)}, u32[]{:S(2)}) collective-permute-start(bf16[48,512]{1,0:T(8,128)(2,1)S(1)} %get-tuple-element.20), channel_id=1, source_target_pairs={{0,12},{1,13},{2,14},{3,15},{4,8},{5,9},{6,10},{7,11},{8,4},{9,5},... | collective-permute-start | bytes 147464 | tf_op jit(solution)/shard_map/ppermute | solution.py:141

commit v2 on v1

v2 whole, which is shorter than its diff:
```python
import functools
import math

import jax
import jax.numpy as jnp
from jax import lax
from jax.experimental import pallas as pl
from jax.experimental.pallas import tpu as pltpu
from jax.sharding import PartitionSpec as P

F32 = jnp.float32
BF16 = jnp.bfloat16
AXIS = "ha"
PHASES = 4


def dot(left, right):
    return jnp.dot(left, right, preferred_element_type=F32)


def lanes(parts):
    return parts[0] if len(parts) == 1 else jnp.concatenate(parts, axis=-1)


def silu(x):
    return 0.5 * x * (1.0 + jnp.tanh(0.5 * x))


def shifted(x, step, period):
    rows = x.shape[0]
    place = lax.broadcasted_iota(jnp.int32, x.shape, 0) % period
    moved = pltpu.roll(x, step % rows, 0)
    return jnp.where(place == (0 if step == 1 else period - 1), 0.0, moved)


def place_phases(total, tap_ref, out_of):
    _, frames, cols, channels = tap_ref.shape
    count = cols // PHASES
    for tap in range(3):
        tap_ref[tap] = total[:, tap * channels : (tap + 1) * channels].reshape(
            frames, cols, channels
        )
    for frame in range(frames):
        def strided(tap, phase):
            return tap_ref[tap, frame, pl.ds(phase, count, stride=PHASES), :]

        for phase in range(PHASES):
            before = (
                shifted(strided(0, PHASES - 1), 1, count)
                if phase == 0
                else strided(0, phase - 1)
            )
            after = (
                shifted(strided(2, 0), -1, count)
                if phase == PHASES - 1
                else strided(2, phase + 1)
            )
            out_of(frame, phase, before + strided(1, phase) + after)


def tap_matrix(w_ref, row):
    return lanes([w_ref[row, tap] for tap in range(3)])


def edge_kernel(video_ref, w_ref, far_ref, near_ref, tap_ref):
    parity = lax.axis_index(AXIS) % 2
    frames, rows, cols, channels = video_ref.shape
    for ref, side in ((far_ref, parity), (near_ref, 1 - parity)):
        row = side * (rows - 1)
        weight = tap_matrix(w_ref, 2 - 2 * side)
        total = dot(video_ref[:, row].reshape(frames * cols, channels), weight)

        def store(frame, phase, value, ref=ref):
            ref[frame, phase] = value.astype(BF16)

        place_phases(total, tap_ref, store)


def inner_kernel(video_ref, w_ref, acc_ref, tap_ref):
    frames, rows, cols, channels = video_ref.shape
    for row in range(rows):
        total = None
        for tap in range(3):
            source = row + tap - 1
            if 0 <= source < rows:
                term = dot(
                    video_ref[:, source].reshape(frames * cols, channels), tap_matrix(w_ref, tap)
                )
                total = term if total is None else total + term

        def store(frame, phase, value, row=row):
            acc_ref[frame, row, phase] = value

        place_phases(total, tap_ref, store)


def first_kernel(acc_ref, far_ref, near_ref, t_ref, r_ref, d_ref, far_out, near_out, a_ref, h_ref):
    frames, rows, phases, count, channels = acc_ref.shape
    parity = lax.axis_index(AXIS) % 2
    is_even = parity == 0
    sites = rows * phases * count
    for frame in range(frames):
        far = far_ref[frame].astype(F32)
        near = near_ref[frame].astype(F32)
        above = jnp.where(is_even, far, near)
        below = jnp.where(is_even, near, far)
        for row in range(rows):
            value = acc_ref[frame, row]
            if row == 0:
                value = value + above
            if row == rows - 1:
                value = value + below
            a_ref[frame, row] = value.astype(BF16)
        taps = range(max(0, 2 - frame), 3)
        left = lanes([a_ref[frame + tap - 2].reshape(sites, channels) for tap in taps])
        weight = jnp.concatenate([t_ref[tap] for tap in taps], axis=0) if len(taps) > 1 else t_ref[2]
        h_ref[frame] = silu(dot(left, weight)).astype(BF16).reshape(h_ref.shape[1:])
    wide = r_ref.shape[-1]
    weight = r_ref[...].reshape(4 * channels, wide)
    for out_row in range(rows // 2):
        for side in range(phases // 2):
            left = lanes(
                [
                    h_ref[:, 2 * out_row + i, 2 * side + j].reshape(frames * count, channels)
                    for i in range(2)
                    for j in range(2)
                ]
            )
            value = dot(left, weight).astype(BF16).reshape(frames, count, wide)
            d_ref[:, out_row, side] = value
    last = rows // 2 - 1
    far_out[...] = d_ref[:, parity * last]
    near_out[...] = d_ref[:, (1 - parity) * last]


def place_pairs(total, sites, count, channels):
    even, odd = total[:sites], total[sites:]
    first, middle, last = (slice(tap * channels, (tap + 1) * channels) for tap in range(3))
    return (
        shifted(odd[:, first], 1, count) + even[:, middle] + odd[:, last],
        even[:, first] + odd[:, middle] + shifted(even[:, last], -1, count),
    )


def side_rows(ref, row):
    frames, _, sides, count, channels = ref.shape
    return jnp.concatenate(
        [ref[:, row, side].reshape(frames * count, channels) for side in range(sides)], axis=0
    )


def middle_kernel(d_ref, w_ref, acc_ref):
    frames, rows, sides, count, channels = d_ref.shape
    sites = frames * count
    for row in range(rows):
        total = None
        for tap in range(3):
            source = row + tap - 1
            if 0 <= source < rows:
                term = dot(side_rows(d_ref, source), tap_matrix(w_ref, tap))
                total = term if total is None else total + term
        for side, value in enumerate(place_pairs(total, sites, count, channels)):
            acc_ref[:, row, side] = value.reshape(frames, count, channels)


def second_kernel(
    acc_ref, far_ref, near_ref, d_ref, w_ref, t_ref, r_ref, gain_ref, *refs, group_size
):
    frames, rows, sides, count, channels = d_ref.shape
    h_out, *blocks = refs[: frames + 1]
    a_ref, h_ref = refs[frames + 1 :]
    index = lax.axis_index(AXIS)
    parity = index % 2
    is_even = parity == 0
    sites = frames * count
    halos = []
    for side in range(2):
        far = far_ref[:, side].reshape(sites, channels)
        near = near_ref[:, side].reshape(sites, channels)
        halos.append((far, near))
    far = jnp.concatenate([pair[0] for pair in halos], axis=0)
    near = jnp.concatenate([pair[1] for pair in halos], axis=0)
    above = jnp.where(is_even, far, near)
    below = jnp.where(is_even, near, far)
    for row in range(rows):
        values = [acc_ref[:, row, side].reshape(sites, channels) for side in range(sides)]
        for here, halo, tap in ((0, above, 0), (rows - 1, below, 2)):
            if row == here:
                more = place_pairs(dot(halo, tap_matrix(w_ref, tap)), sites, count, channels)
                values = [value + extra for value, extra in zip(values, more)]
        for side, value in enumerate(values):
            a_ref[:, row, side] = value.astype(BF16).reshape(frames, count, channels)
    frame_sites = rows * sides * count
    for frame in range(frames):
        taps = range(max(0, 2 - frame), 3)
        left = lanes([a_ref[frame + tap - 2].reshape(frame_sites, channels) for tap in taps])
        weight = jnp.concatenate([t_ref[tap] for tap in taps], axis=0) if len(taps) > 1 else t_ref[2]
        value = d_ref[frame].reshape(frame_sites, channels).astype(F32) + silu(dot(left, weight))
        h_ref[frame] = value.astype(BF16).reshape(h_ref.shape[1:])
    wide = r_ref.shape[-1]
    weight = r_ref[...].reshape(4 * channels, wide)
    gain = gain_ref[...].astype(F32)
    place = index // group_size
    for out_row in range(rows // 2):
        left = lanes(
            [
                h_ref[:, 2 * out_row + i, j].reshape(sites, channels)
                for i in range(2)
                for j in range(2)
            ]
        )
        residual = dot(left, weight).astype(BF16)
        h_out[:, out_row] = residual.reshape(frames, count, wide)
        residual = residual.astype(F32)
        mean_square = jnp.mean(residual * residual, axis=-1, keepdims=True)
        normed = (residual * lax.rsqrt(mean_square + 1e-06) * gain).astype(BF16)
        a_ref_shape = (frames, count, wide)
        refs_normed = normed.reshape(a_ref_shape)
        for frame in range(frames):
            for step, block in enumerate(blocks):

                @pl.when(place ^ step == frame)
                def _(block=block, frame=frame, out_row=out_row):
                    block[pl.ds(out_row * count, count), :] = refs_normed[frame]


def query_kernel(own_ref, q_ref, k_ref, out_ref):
    queries = dot(own_ref[...], q_ref[...]).astype(BF16)
    out_ref[...] = lax.dot_general(
        queries, k_ref[...], (((1,), (1,)), ((), ())), preferred_element_type=F32
    ).astype(BF16)


def attention_kernel(mapped_ref, sites_ref, v_ref, o_ref, *blocks):
    channels = mapped_ref.shape[-1]
    score_scale = 1.0 / math.sqrt(channels)
    scores = (
        lax.dot_general(
            mapped_ref[...], sites_ref[...], (((1,), (1,)), ((), ())), preferred_element_type=F32
        )
        * score_scale
    )
    weights = jnp.exp(scores - jnp.max(scores, axis=-1, keepdims=True))
    totals = jnp.sum(weights, axis=-1, keepdims=True)
    mixed = (dot(weights.astype(BF16), sites_ref[...]) / totals).astype(BF16)
    attended = dot(mixed, v_ref[...]).astype(BF16)
    result = dot(attended, o_ref[...]).astype(BF16)
    count = blocks[0].shape[0]
    for step, block in enumerate(blocks):
        block[...] = result[step * count : (step + 1) * count]


def sum_kernel(h_ref, *refs, group_size):
    *blocks, out_ref = refs
    frames, rows, count, channels = h_ref.shape
    place = lax.axis_index(AXIS) // group_size
    for step, block in enumerate(blocks):
        frame = place ^ step
        value = block[...].astype(F32).reshape(rows, count, channels)
        out_ref[frame] = (h_ref[frame].astype(F32) + value).astype(BF16)


def call(kernel, outs, scratch, args, flops, name):
    vmem = pl.BlockSpec(memory_space=pltpu.VMEM)
    shapes = [jax.ShapeDtypeStruct(shape, dtype) for shape, dtype in outs]
    moved = sum(math.prod(arg.shape) * arg.dtype.itemsize for arg in args)
    moved += sum(math.prod(shape) * jnp.dtype(dtype).itemsize for shape, dtype in outs)
    used = moved + sum(
        math.prod(shape) * jnp.dtype(dtype).itemsize for shape, dtype in scratch
    )
    return pl.pallas_call(
        kernel,
        out_shape=shapes,
        in_specs=[vmem] * len(args),
        out_specs=[vmem] * len(outs),
        scratch_shapes=[pltpu.VMEM(shape, dtype) for shape, dtype in scratch],
        compiler_params=pltpu.CompilerParams(vmem_limit_bytes=LIMIT),
        cost_estimate=pl.CostEstimate(flops=int(flops), bytes_accessed=int(moved), transcendentals=0),
        name=name,
    )(*args)


LIMIT = 40 * 1024 * 1024


def per_device(
    video,
    s1_weight,
    t1_weight,
    r1_weight,
    s2_weight,
    t2_weight,
    r2_weight,
    attn_gain,
    w_query,
    w_key,
    w_value,
    w_out,
):
    frames, rows, cols, c0 = video.shape
    c1, c2, c3 = s1_weight.shape[-1], s2_weight.shape[-1], w_out.shape[-1]
    count = cols // PHASES
    devices = lax.axis_size(AXIS)
    group_size = devices // frames
    inner = [(d, d ^ 1) for d in range(devices)]
    outer = [(d, d + 1) for d in range(1, devices - 1, 2)]
    outer = outer + [(target, source) for source, target in outer]
    turns = [
        [(d, (d // group_size ^ k) * group_size + d % group_size) for d in range(devices)]
        for k in range(frames)
    ]

    edge = ((frames, PHASES, count, c1), BF16)
    taps = ((3, frames, cols, c1), F32)
    site_flops = 2 * frames * cols * 3 * c0 * c1
    far, near = call(edge_kernel, [edge, edge], [taps], [video, s1_weight], 2 * site_flops, "edge")
    far = lax.ppermute(far, AXIS, outer)
    near = lax.ppermute(near, AXIS, inner)
    shape = (frames, rows, PHASES, count, c1)
    (acc,) = call(
        inner_kernel, [(shape, F32)], [taps], [video, s1_weight], 10 * site_flops, "inner"
    )
    half = (frames, rows // 2, 2, count, c2)
    edge = ((frames, 2, count, c2), BF16)
    d_first, far, near = call(
        first_kernel,
        [(half, BF16), edge, edge],
        [(shape, BF16), (shape, BF16)],
        [acc, far, near, t1_weight, r1_weight],
        5e8,
        "first",
    )
    far = lax.ppermute(far, AXIS, outer)
    near = lax.ppermute(near, AXIS, inner)
    (acc,) = call(middle_kernel, [(half, F32)], [], [d_first, s2_weight], 6e8, "middle")
    site_rows = rows // 4
    block = ((site_rows * count, c3), BF16)
    residual, *blocks = call(
        functools.partial(second_kernel, group_size=group_size),
        [((frames, site_rows, count, c3), BF16)] + [block] * frames,
        [(half, BF16), (half, BF16)],
        [acc, far, near, d_first, s2_weight, t2_weight, r2_weight, attn_gain.reshape(1, c3)],
        8e8,
        "second",
    )
    own = jnp.concatenate(
        [blocks[0]] + [lax.ppermute(blocks[k], AXIS, turns[k]) for k in range(1, frames)], axis=0
    )
    sites = own
    bit = group_size // 2
    while bit:
        sites = jnp.concatenate(
            [sites, lax.ppermute(sites, AXIS, [(d, d ^ bit) for d in range(devices)])], axis=0
        )
        bit //= 2
    (mapped,) = call(query_kernel, [(own.shape, BF16)], [], [own, w_query, w_key], 2e8, "query")
    blocks = call(
        attention_kernel, [block] * frames, [], [mapped, sites, w_value, w_out], 6e8, "attention"
    )
    blocks = [blocks[0]] + [lax.ppermute(blocks[k], AXIS, turns[k]) for k in range(1, frames)]
    (encoded,) = call(
        functools.partial(sum_kernel, group_size=group_size),
        [(residual.shape, BF16)],
        [],
        [residual, *blocks],
        1e6,
        "sum",
    )
    return encoded


def solution(mesh):
    placed = (P("groups", "ha", None, None), P(), P(), P(), P(), P(), P(), P(), P(), P(), P(), P())
    return jax.shard_map(
        per_device,
        mesh=mesh,
        in_specs=placed,
        out_specs=P("groups", "ha", None, None),
        check_vma=False,
    )
```

time: 67.2 us -> 52.8 us (0.79)
  matrix products: 15.8 us -> 0 us
  Pallas kernels: 0 us -> 8.57 us
  other arithmetic: 5.64 us -> 0 us
  starting transfers between devices: 28.6 us -> 24.8 us
  waiting for transfers between devices: 15 us -> 16.4 us
  local copies, waits for them, and re-layouts: 1.42 us -> 2.58 us
    dot_general x30 -> x0, matrix products: 15.8 us -> none  [the longest x18 8.66 us: spatial(): jnp.einsum('tywc,co->tywo', padded[:, tap_row:tap_row + row_count, tap_co...]
    pallas_call x0 -> x8, Pallas kernels: none -> 8.57 us  [call(): pl.pallas_call(kernel, out_shape=shapes, in_specs=[vmem] * len(args), out...]
    ppermute x12, starting transfers between devices: 28.6 us -> 24.8 us  [the longest x6 10.9 us: per_device(): lax.ppermute(blocks[k], AXIS, turns[k])]
    select_n x4 -> x0, other arithmetic: 3.19 us -> none  [the longest x2 2.11 us: pair_halo(): far = lax.ppermute(jnp.where(is_even, top, low), axis, outer)]
    ppermute x12, waiting for transfers between devices: 15 us -> 16.4 us  [the longest x6 9.86 us: per_device(): lax.ppermute(blocks[k], AXIS, turns[k])]
    unnamed x23 -> x28, local copies, waits for them, and re-layouts: 1.15 us -> 2.52 us
    concatenate x3 -> x0, other arithmetic: 1.3 us -> none  [the longest x2 1.29 us: pair_halo(): return jnp.concatenate([above, block, below], axis=dim)]
    convert_element_type x3 -> x0, other arithmetic: 0.85 us -> none  [the longest x1 0.74 us: per_device(): return encoded.astype(jnp.bfloat16)]
  transfers between devices with their start and end apart: 12 -> 12, of which waited for: 7 -> 8; matrix products, arithmetic and copies ran while one was open for 5% -> 0% of each run, Pallas kernels for 0% -> 7%
where the time goes in v2:
time: 52.8 us; the launch traced here: 52.6 us
  starting transfers between devices  24.8 us (47%)
  waiting for transfers between devices  16.4 us (31%)
  Pallas kernels  8.57 us (16%)
  local copies, waits for them, and re-layouts  2.58 us (5%)
    ppermute x6, starting transfers between devices, per_device(): lax.ppermute(blocks[k], AXIS, turns[k])  10.9 us
    ppermute x2, starting transfers between devices, per_device(): near = lax.ppermute(near, AXIS, inner)  10.4 us
    ppermute x6, waiting for transfers between devices, per_device(): lax.ppermute(blocks[k], AXIS, turns[k])  9.86 us
    pallas_call x8, Pallas kernels, call(): pl.pallas_call(kernel, out_shape=shapes, in_specs=[vmem] * len(args), out...  8.57 us
    ppermute x2, waiting for transfers between devices, per_device(): lax.ppermute(sites, AXIS, [(d, d ^ bit) for d in range(devices)])  6.22 us
    unnamed x28, local copies, waits for them, and re-layouts  2.52 us
    ppermute x2, starting transfers between devices, per_device(): lax.ppermute(sites, AXIS, [(d, d ^ bit) for d in range(devices)])  2.06 us
    ppermute x2, starting transfers between devices, per_device(): far = lax.ppermute(far, AXIS, outer)  1.48 us
  transfers between devices with their start and end apart: 12, of which 8 were waited for; matrix products, arithmetic and copies ran while one was open for 0% of the time, Pallas kernels for 7%

profile of v2, /device:TPU:0, one launch (start us, length us, event | category | flops | bytes accessed | tf_op | source)
XLA Modules:
  0.0 52.6 jit_solution(5511547126107622797)
XLA Ops:
  0.0 1.4 %copy-done.1 = bf16[4,4,192,192]{3,2,1,0:T(8,128)(2,1)S(1)} copy-done((bf16[4,4,192,192]{3,2,1,0:T(8,128)(2,1)S(1)}, bf16[4,4,192,192]{3,2,1,0:T(8,128)(2,1)}, u32[]{:S(2)}) %copy-start.1) | copy-done | bytes 1179672
  1.4 1.0 %copy-done.5 = bf16[3,3,192,128]{3,2,1,0:T(8,128)(2,1)S(1)} copy-done((bf16[3,3,192,128]{3,2,1,0:T(8,128)(2,1)S(1)}, bf16[3,3,192,128]{3,2,1,0:T(8,128)(2,1)}, u32[]{:S(2)}) %copy-start.5) | copy-done | bytes 442392
  2.4 0.6 %edge.1 = (bf16[4,4,48,128]{3,2,1,0:T(8,128)(2,1)S(1)}, bf16[4,4,48,128]{3,2,1,0:T(8,128)(2,1)S(1)}) custom-call(bf16[4,4,192,192]{3,2,1,0:T(8,128)(2,1)S(1)} %copy-done.1, bf16[3,3,192,128]{3,2,1,0:T(8,128)(2,1)S(1)} %copy-done.5), custom_call_target="tpu_custom_call" | custom-call | flops 226492416 | bytes 2015232 | tf_op jit(solution)/shard_map/edge/pallas_call | solution.py:271
  3.1 0.7 %collective-permute-start = (bf16[4,4,48,128]{3,2,1,0:T(8,128)(2,1)S(1)}, bf16[4,4,48,128]{3,2,1,0:T(8,128)(2,1)S(1)}, u32[]{:S(2)}, u32[]{:S(2)}) collective-permute-start(bf16[4,4,48,128]{3,2,1,0:T(8,128)(2,1)S(1)} %get-tuple-element.19), channel_id=1, source_target_pairs={{1,2},{3,4},{5,6},{7,8},{9,10},{11,12},{13,14},{2,1},{4,3},{6,5},{... | collective-permute-start | bytes 589832 | tf_op jit(solution)/shard_map/ppermute | solution.py:317
  3.8 0.0 copy-start.8
  3.8 4.4 %collective-permute-start.1 = (bf16[4,4,48,128]{3,2,1,0:T(8,128)(2,1)S(1)}, bf16[4,4,48,128]{3,2,1,0:T(8,128)(2,1)S(1)}, u32[]{:S(2)}, u32[]{:S(2)}) collective-permute-start(bf16[4,4,48,128]{3,2,1,0:T(8,128)(2,1)S(1)} %get-tuple-element.20), channel_id=1, source_target_pairs={{0,1},{1,0},{2,3},{3,2},{4,5},{5,4},{6,7},{7,6},{8,9},{9,8},{10,11... | collective-permute-start | bytes 589832 | tf_op jit(solution)/shard_map/ppermute | solution.py:318
  8.2 2.4 %inner.1.acc_ref = f32[4,4,4,48,128]{4,3,2,1,0:T(8,128)S(1)} custom-call(bf16[4,4,192,192]{3,2,1,0:T(8,128)(2,1)S(1)} %copy-done.1, bf16[3,3,192,128]{3,2,1,0:T(8,128)(2,1)S(1)} %copy-done.5), custom_call_target="tpu_custom_call" | custom-call | flops 1132462080 | bytes 3194880 | tf_op jit(solution)/shard_map/inner/pallas_call | solution.py:271
  10.6 0.0 copy-start.11
  10.6 0.0 copy-start
  10.6 0.9 %first.1 = (bf16[4,2,2,48,256]{4,3,2,1,0:T(8,128)(2,1)S(1)}, bf16[4,2,48,256]{3,2,1,0:T(8,128)(2,1)S(1)}, bf16[4,2,48,256]{3,2,1,0:T(8,128)(2,1)S(1)}) custom-call(f32[4,4,4,48,128]{4,3,2,1,0:T(8,128)S(1)} %inner.1.acc_ref, bf16[4,4,48,128]{3,2,1,0:T(8,128)(2,1)S(1)} %collective-permute-done.far_ref, ...), custom_call_target="tpu_custom_call" | custom-call | flops 500000000 | bytes 3112960 | tf_op jit(solution)/shard_map/first/pallas_call | solution.py:271
  11.6 0.8 %collective-permute-start.2 = (bf16[4,2,48,256]{3,2,1,0:T(8,128)(2,1)S(1)}, bf16[4,2,48,256]{3,2,1,0:T(8,128)(2,1)S(1)}, u32[]{:S(2)}, u32[]{:S(2)}) collective-permute-start(bf16[4,2,48,256]{3,2,1,0:T(8,128)(2,1)S(1)} %get-tuple-element.22), channel_id=1, source_target_pairs={{1,2},{3,4},{5,6},{7,8},{9,10},{11,12},{13,14},{2,1},{4,3},{6,5},{... | collective-permute-start | bytes 589832 | tf_op jit(solution)/shard_map/ppermute | solution.py:333
  12.4 6.0 %collective-permute-start.3 = (bf16[4,2,48,256]{3,2,1,0:T(8,128)(2,1)S(1)}, bf16[4,2,48,256]{3,2,1,0:T(8,128)(2,1)S(1)}, u32[]{:S(2)}, u32[]{:S(2)}) collective-permute-start(bf16[4,2,48,256]{3,2,1,0:T(8,128)(2,1)S(1)} %get-tuple-element.23), channel_id=1, source_target_pairs={{0,1},{1,0},{2,3},{3,2},{4,5},{5,4},{6,7},{7,6},{8,9},{9,8},{10,11... | collective-permute-start | bytes 589832 | tf_op jit(solution)/shard_map/ppermute | solution.py:334
  18.4 0.8 %middle.1.acc_ref = f32[4,2,2,48,256]{4,3,2,1,0:T(8,128)S(1)} custom-call(bf16[4,2,2,48,256]{4,3,2,1,0:T(8,128)(2,1)S(1)} %get-tuple-element.21.d_ref, bf16[3,3,256,256]{3,2,1,0:T(8,128)(2,1)S(1)} %copy-done), custom_call_target="tpu_custom_call" | custom-call | flops 600000000 | bytes 2359296 | tf_op jit(solution)/shard_map/middle/pallas_call | solution.py:271
  19.2 0.3 collective-permute-done.3.near_ref
  19.4 1.4 %second.1 = (bf16[4,1,48,512]{3,2,1,0:T(8,128)(2,1)S(1)}, bf16[48,512]{1,0:T(8,128)(2,1)S(1)}, bf16[48,512]{1,0:T(8,128)(2,1)S(1)}, bf16[48,512]{1,0:T(8,128)(2,1)S(1)}, bf16[48,512]{1,0:T(8,128)(2,1)S(1)}) custom-call(f32[4,2,2,48,256]{4,3,2,1,0:T(8,128)S(1)} %middle.1.acc_ref, bf16[4,2,48,256]{3,2,1,0:T(8,128)(2,1)S(1)} %collective-permute-done.2.far_ref, ...), custom_call_target="tpu_custom_call" | custom-call | flops 800000000 | bytes 4588544 | tf_op jit(solution)/shard_map/second/pallas_call | solution.py:271
  20.9 3.8 %collective-permute-start.4 = (bf16[48,512]{1,0:T(8,128)(2,1)S(1)}, bf16[48,512]{1,0:T(8,128)(2,1)S(1)}, u32[]{:S(2)}, u32[]{:S(2)}) collective-permute-start(bf16[48,512]{1,0:T(8,128)(2,1)S(1)} %get-tuple-element.26), channel_id=1, source_target_pairs={{0,4},{1,5},{2,6},{3,7},{4,0},{5,1},{6,2},{7,3},{8,12},{9,13},{10,... | collective-permute-start | bytes 147464 | tf_op jit(solution)/shard_map/ppermute | solution.py:347
  24.7 2.6 %collective-permute-start.5 = (bf16[48,512]{1,0:T(8,128)(2,1)S(1)}, bf16[48,512]{1,0:T(8,128)(2,1)S(1)}, u32[]{:S(2)}, u32[]{:S(2)}) collective-permute-start(bf16[48,512]{1,0:T(8,128)(2,1)S(1)} %get-tuple-element.27), channel_id=1, source_target_pairs={{0,8},{1,9},{2,10},{3,11},{4,12},{5,13},{6,14},{7,15},{8,0},{9,1},... | collective-permute-start | bytes 147464 | tf_op jit(solution)/shard_map/ppermute | solution.py:347
  27.3 3.7 %collective-permute-done.5 = bf16[48,512]{1,0:T(8,128)(2,1)S(1)} collective-permute-done((bf16[48,512]{1,0:T(8,128)(2,1)S(1)}, bf16[48,512]{1,0:T(8,128)(2,1)S(1)}, u32[]{:S(2)}, u32[]{:S(2)}) %collective-permute-start.5) | collective-permute-done | bytes 49184 | tf_op jit(solution)/shard_map/ppermute | solution.py:347
  31.1 2.3 %collective-permute-done.6 = bf16[48,512]{1,0:T(8,128)(2,1)S(1)} collective-permute-done((bf16[48,512]{1,0:T(8,128)(2,1)S(1)}, bf16[48,512]{1,0:T(8,128)(2,1)S(1)}, u32[]{:S(2)}, u32[]{:S(2)}) %collective-permute-start.6) | collective-permute-done | bytes 49184 | tf_op jit(solution)/shard_map/ppermute | solution.py:347
  33.4 2.0 %collective-permute-start.7 = (bf16[192,512]{1,0:T(8,128)(2,1)S(1)}, bf16[192,512]{1,0:T(8,128)(2,1)S(1)}, u32[]{:S(2)}, u32[]{:S(2)}) collective-permute-start(bf16[192,512]{1,0:T(8,128)(2,1)S(1)} %get-tuple-element.37.own_ref), channel_id=1, source_target_pairs={{0,2},{1,3},{2,0},{3,1},{4,6},{5,7},{6,4},{7,5},{8,10},{9,11},{10,... | collective-permute-start | bytes 589832 | tf_op jit(solution)/shard_map/ppermute | solution.py:353
  35.4 5.0 %collective-permute-done.7 = bf16[192,512]{1,0:T(8,128)(2,1)S(1)} collective-permute-done((bf16[192,512]{1,0:T(8,128)(2,1)S(1)}, bf16[192,512]{1,0:T(8,128)(2,1)S(1)}, u32[]{:S(2)}, u32[]{:S(2)}) %collective-permute-start.7) | collective-permute-done | bytes 196640 | tf_op jit(solution)/shard_map/ppermute | solution.py:353
  40.4 0.1 collective-permute-start.8
  40.5 0.5 query.1.mapped_ref
  41.0 1.2 %collective-permute-done.8 = bf16[384,512]{1,0:T(8,128)(2,1)S(1)} collective-permute-done((bf16[384,512]{1,0:T(8,128)(2,1)S(1)}, bf16[384,512]{1,0:T(8,128)(2,1)S(1)}, u32[]{:S(2)}, u32[]{:S(2)}) %collective-permute-start.8) | collective-permute-done | bytes 393248 | tf_op jit(solution)/shard_map/ppermute | solution.py:353
  42.3 1.3 %attention.1 = (bf16[48,512]{1,0:T(8,128)(2,1)S(1)}, bf16[48,512]{1,0:T(8,128)(2,1)S(1)}, bf16[48,512]{1,0:T(8,128)(2,1)S(1)}, bf16[48,512]{1,0:T(8,128)(2,1)S(1)}) custom-call(bf16[192,512]{1,0:T(8,128)(2,1)S(1)} %query.1.mapped_ref, bf16[768,512]{1,0:T(8,128)(2,1)S(1)} %constant_dynamic-update-slice_fusion.9.sites_ref, bf16[512,512]{1,0:T(8,128)(2,1)S(1)} %copy-done.9, ...), custom_call_target="tpu_custom_call" | custom-call | flops 600000000 | bytes 2228224 | tf_op jit(solution)/shard_map/attention/pallas_call | solution.py:271
  43.5 0.1 collective-permute-start.9
  43.6 2.2 %collective-permute-start.10 = (bf16[48,512]{1,0:T(8,128)(2,1)S(1)}, bf16[48,512]{1,0:T(8,128)(2,1)S(1)}, u32[]{:S(2)}, u32[]{:S(2)}) collective-permute-start(bf16[48,512]{1,0:T(8,128)(2,1)S(1)} %get-tuple-element.31), channel_id=1, source_target_pairs={{0,8},{1,9},{2,10},{3,11},{4,12},{5,13},{6,14},{7,15},{8,0},{9,1},... | collective-permute-start | bytes 147464 | tf_op jit(solution)/shard_map/ppermute | solution.py:360
  45.8 2.2 %collective-permute-start.11 = (bf16[48,512]{1,0:T(8,128)(2,1)S(1)}, bf16[48,512]{1,0:T(8,128)(2,1)S(1)}, u32[]{:S(2)}, u32[]{:S(2)}) collective-permute-start(bf16[48,512]{1,0:T(8,128)(2,1)S(1)} %get-tuple-element.32), channel_id=1, source_target_pairs={{0,12},{1,13},{2,14},{3,15},{4,8},{5,9},{6,10},{7,11},{8,4},{9,5},... | collective-permute-start | bytes 147464 | tf_op jit(solution)/shard_map/ppermute | solution.py:360
  48.0 0.6 %collective-permute-done.9.refs_1_ = bf16[48,512]{1,0:T(8,128)(2,1)S(1)} collective-permute-done((bf16[48,512]{1,0:T(8,128)(2,1)S(1)}, bf16[48,512]{1,0:T(8,128)(2,1)S(1)}, u32[]{:S(2)}, u32[]{:S(2)}) %collective-permute-start.9) | collective-permute-done | bytes 49184 | tf_op jit(solution)/shard_map/ppermute | solution.py:360
  48.6 0.8 %collective-permute-done.10.refs_2_ = bf16[48,512]{1,0:T(8,128)(2,1)S(1)} collective-permute-done((bf16[48,512]{1,0:T(8,128)(2,1)S(1)}, bf16[48,512]{1,0:T(8,128)(2,1)S(1)}, u32[]{:S(2)}, u32[]{:S(2)}) %collective-permute-start.10) | collective-permute-done | bytes 49184 | tf_op jit(solution)/shard_map/ppermute | solution.py:360
  49.4 2.4 %collective-permute-done.11.refs_3_ = bf16[48,512]{1,0:T(8,128)(2,1)S(1)} collective-permute-done((bf16[48,512]{1,0:T(8,128)(2,1)S(1)}, bf16[48,512]{1,0:T(8,128)(2,1)S(1)}, u32[]{:S(2)}, u32[]{:S(2)}) %collective-permute-start.11) | collective-permute-done | bytes 49184 | tf_op jit(solution)/shard_map/ppermute | solution.py:360
  51.8 0.7 %sum.1 = bf16[4,1,48,512]{3,2,1,0:T(8,128)(2,1)} custom-call(bf16[4,1,48,512]{3,2,1,0:T(8,128)(2,1)S(1)} %get-tuple-element.24.h_ref, bf16[48,512]{1,0:T(8,128)(2,1)S(1)} %get-tuple-element.29.refs_0_, bf16[48,512]{1,0:T(8,128)(2,1)S(1)} %collective-permute-done.9.refs_1_, bf16[48,512]{1,0:T(8,128)(2,1)S(1)} %collective-permute-done.10.refs_2_, ...), custom_call_target="tpu_custom_call" | custom-call | flops 1000000 | bytes 589824 | tf_op jit(solution)/shard_map/sum/pallas_call | solution.py:271
  (31 shorter events, 0.2 us)
Async XLA Ops:
  0.0 1.4 %copy-start.1 = (bf16[4,4,192,192]{3,2,1,0:T(8,128)(2,1)S(1)}, bf16[4,4,192,192]{3,2,1,0:T(8,128)(2,1)}, u32[]{:S(2)}) copy-start(bf16[4,4,192,192]{3,2,1,0:T(8,128)(2,1)} %video_ref.3) | copy-start | bytes 3538948
  1.4 1.0 %copy-start.5 = (bf16[3,3,192,128]{3,2,1,0:T(8,128)(2,1)S(1)}, bf16[3,3,192,128]{3,2,1,0:T(8,128)(2,1)}, u32[]{:S(2)}) copy-start(bf16[3,3,192,128]{3,2,1,0:T(8,128)(2,1)} %w_ref.5) | copy-start | bytes 1327108
  3.1 7.5 %collective-permute-start = (bf16[4,4,48,128]{3,2,1,0:T(8,128)(2,1)S(1)}, bf16[4,4,48,128]{3,2,1,0:T(8,128)(2,1)S(1)}, u32[]{:S(2)}, u32[]{:S(2)}) collective-permute-start(bf16[4,4,48,128]{3,2,1,0:T(8,128)(2,1)S(1)} %get-tuple-element.19), channel_id=1, source_target_pairs={{1,2},{3,4},{5,6},{7,8},{9,10},{11,12},{13,14},{2,1},{4,3},{6,5},{... | collective-permute-start | bytes 589832 | tf_op jit(solution)/shard_map/ppermute | solution.py:317
  3.8 6.9 %copy-start.7 = (bf16[2,2,128,256]{3,2,1,0:T(8,128)(2,1)S(1)}, bf16[2,2,128,256]{3,2,1,0:T(8,128)(2,1)}, u32[]{:S(2)}) copy-start(bf16[2,2,128,256]{3,2,1,0:T(8,128)(2,1)} %r_ref.2) | copy-start | bytes 786436
  3.8 6.8 %copy-start.8 = (bf16[3,128,128]{2,1,0:T(8,128)(2,1)S(1)}, bf16[3,128,128]{2,1,0:T(8,128)(2,1)}, u32[]{:S(2)}) copy-start(bf16[3,128,128]{2,1,0:T(8,128)(2,1)} %t_ref.2) | copy-start | bytes 294916
  3.8 6.8 %collective-permute-start.1 = (bf16[4,4,48,128]{3,2,1,0:T(8,128)(2,1)S(1)}, bf16[4,4,48,128]{3,2,1,0:T(8,128)(2,1)S(1)}, u32[]{:S(2)}, u32[]{:S(2)}) collective-permute-start(bf16[4,4,48,128]{3,2,1,0:T(8,128)(2,1)S(1)} %get-tuple-element.20), channel_id=1, source_target_pairs={{0,1},{1,0},{2,3},{3,2},{4,5},{5,4},{6,7},{7,6},{8,9},{9,8},{10,11... | collective-permute-start | bytes 589832 | tf_op jit(solution)/shard_map/ppermute | solution.py:318
  10.6 7.8 %copy-start.11 = (bf16[512]{0:T(512)(128)(2,1)S(1)}, bf16[512]{0:T(512)(128)(2,1)}, u32[]{:S(2)}) copy-start(bf16[512]{0:T(512)(128)(2,1)} %param.19) | copy-start | bytes 3076
  10.6 7.8 %copy-start = (bf16[3,3,256,256]{3,2,1,0:T(8,128)(2,1)S(1)}, bf16[3,3,256,256]{3,2,1,0:T(8,128)(2,1)}, u32[]{:S(2)}) copy-start(bf16[3,3,256,256]{3,2,1,0:T(8,128)(2,1)} %w_ref.7) | copy-start | bytes 3538948
  11.6 7.9 %copy-start.2 = (bf16[2,2,256,512]{3,2,1,0:T(8,128)(2,1)S(1)}, bf16[2,2,256,512]{3,2,1,0:T(8,128)(2,1)}, u32[]{:S(2)}) copy-start(bf16[2,2,256,512]{3,2,1,0:T(8,128)(2,1)} %r_ref.3) | copy-start | bytes 3145732
  11.6 7.9 %copy-start.6 = (bf16[3,256,256]{2,1,0:T(8,128)(2,1)S(1)}, bf16[3,256,256]{2,1,0:T(8,128)(2,1)}, u32[]{:S(2)}) copy-start(bf16[3,256,256]{2,1,0:T(8,128)(2,1)} %t_ref.3) | copy-start | bytes 1179652
  11.6 7.6 %collective-permute-start.2 = (bf16[4,2,48,256]{3,2,1,0:T(8,128)(2,1)S(1)}, bf16[4,2,48,256]{3,2,1,0:T(8,128)(2,1)S(1)}, u32[]{:S(2)}, u32[]{:S(2)}) collective-permute-start(bf16[4,2,48,256]{3,2,1,0:T(8,128)(2,1)S(1)} %get-tuple-element.22), channel_id=1, source_target_pairs={{1,2},{3,4},{5,6},{7,8},{9,10},{11,12},{13,14},{2,1},{4,3},{6,5},{... | collective-permute-start | bytes 589832 | tf_op jit(solution)/shard_map/ppermute | solution.py:333
  12.4 7.0 %collective-permute-start.3 = (bf16[4,2,48,256]{3,2,1,0:T(8,128)(2,1)S(1)}, bf16[4,2,48,256]{3,2,1,0:T(8,128)(2,1)S(1)}, u32[]{:S(2)}, u32[]{:S(2)}) collective-permute-start(bf16[4,2,48,256]{3,2,1,0:T(8,128)(2,1)S(1)} %get-tuple-element.23), channel_id=1, source_target_pairs={{0,1},{1,0},{2,3},{3,2},{4,5},{5,4},{6,7},{7,6},{8,9},{9,8},{10,11... | collective-permute-start | bytes 589832 | tf_op jit(solution)/shard_map/ppermute | solution.py:334
  20.8 19.7 %copy-start.3 = (bf16[512,512]{1,0:T(8,128)(2,1)S(1)}, bf16[512,512]{1,0:T(8,128)(2,1)}, u32[]{:S(2)}) copy-start(bf16[512,512]{1,0:T(8,128)(2,1)} %q_ref.1) | copy-start | bytes 1572868
  20.8 19.7 %copy-start.4 = (bf16[512,512]{1,0:T(8,128)(2,1)S(1)}, bf16[512,512]{1,0:T(8,128)(2,1)}, u32[]{:S(2)}) copy-start(bf16[512,512]{1,0:T(8,128)(2,1)} %k_ref.1) | copy-start | bytes 1572868
  20.9 6.4 %collective-permute-start.4 = (bf16[48,512]{1,0:T(8,128)(2,1)S(1)}, bf16[48,512]{1,0:T(8,128)(2,1)S(1)}, u32[]{:S(2)}, u32[]{:S(2)}) collective-permute-start(bf16[48,512]{1,0:T(8,128)(2,1)S(1)} %get-tuple-element.26), channel_id=1, source_target_pairs={{0,4},{1,5},{2,6},{3,7},{4,0},{5,1},{6,2},{7,3},{8,12},{9,13},{10,... | collective-permute-start | bytes 147464 | tf_op jit(solution)/shard_map/ppermute | solution.py:347
  24.7 6.4 %collective-permute-start.5 = (bf16[48,512]{1,0:T(8,128)(2,1)S(1)}, bf16[48,512]{1,0:T(8,128)(2,1)S(1)}, u32[]{:S(2)}, u32[]{:S(2)}) collective-permute-start(bf16[48,512]{1,0:T(8,128)(2,1)S(1)} %get-tuple-element.27), channel_id=1, source_target_pairs={{0,8},{1,9},{2,10},{3,11},{4,12},{5,13},{6,14},{7,15},{8,0},{9,1},... | collective-permute-start | bytes 147464 | tf_op jit(solution)/shard_map/ppermute | solution.py:347
  27.3 6.1 %collective-permute-start.6 = (bf16[48,512]{1,0:T(8,128)(2,1)S(1)}, bf16[48,512]{1,0:T(8,128)(2,1)S(1)}, u32[]{:S(2)}, u32[]{:S(2)}) collective-permute-start(bf16[48,512]{1,0:T(8,128)(2,1)S(1)} %get-tuple-element.28), channel_id=1, source_target_pairs={{0,12},{1,13},{2,14},{3,15},{4,8},{5,9},{6,10},{7,11},{8,4},{9,5},... | collective-permute-start | bytes 147464 | tf_op jit(solution)/shard_map/ppermute | solution.py:347
  31.1 11.2 %copy-start.9 = (bf16[512,512]{1,0:T(8,128)(2,1)S(1)}, bf16[512,512]{1,0:T(8,128)(2,1)}, u32[]{:S(2)}) copy-start(bf16[512,512]{1,0:T(8,128)(2,1)} %v_ref.1) | copy-start | bytes 1572868
  31.1 11.2 %copy-start.10 = (bf16[512,512]{1,0:T(8,128)(2,1)S(1)}, bf16[512,512]{1,0:T(8,128)(2,1)}, u32[]{:S(2)}) copy-start(bf16[512,512]{1,0:T(8,128)(2,1)} %o_ref.1) | copy-start | bytes 1572868
  33.4 7.0 %collective-permute-start.7 = (bf16[192,512]{1,0:T(8,128)(2,1)S(1)}, bf16[192,512]{1,0:T(8,128)(2,1)S(1)}, u32[]{:S(2)}, u32[]{:S(2)}) collective-permute-start(bf16[192,512]{1,0:T(8,128)(2,1)S(1)} %get-tuple-element.37.own_ref), channel_id=1, source_target_pairs={{0,2},{1,3},{2,0},{3,1},{4,6},{5,7},{6,4},{7,5},{8,10},{9,11},{10,... | collective-permute-start | bytes 589832 | tf_op jit(solution)/shard_map/ppermute | solution.py:353
  40.4 1.8 %collective-permute-start.8 = (bf16[384,512]{1,0:T(8,128)(2,1)S(1)}, bf16[384,512]{1,0:T(8,128)(2,1)S(1)}, u32[]{:S(2)}, u32[]{:S(2)}) collective-permute-start(bf16[384,512]{1,0:T(8,128)(2,1)S(1)} %get-tuple-element.33), channel_id=1, source_target_pairs={{0,1},{1,0},{2,3},{3,2},{4,5},{5,4},{6,7},{7,6},{8,9},{9,8},{10,11... | collective-permute-start | bytes 1179656 | tf_op jit(solution)/shard_map/ppermute | solution.py:353
  43.5 5.0 %collective-permute-start.9 = (bf16[48,512]{1,0:T(8,128)(2,1)S(1)}, bf16[48,512]{1,0:T(8,128)(2,1)S(1)}, u32[]{:S(2)}, u32[]{:S(2)}) collective-permute-start(bf16[48,512]{1,0:T(8,128)(2,1)S(1)} %get-tuple-element.30), channel_id=1, source_target_pairs={{0,4},{1,5},{2,6},{3,7},{4,0},{5,1},{6,2},{7,3},{8,12},{9,13},{10,... | collective-permute-start | bytes 147464 | tf_op jit(solution)/shard_map/ppermute | solution.py:360
  43.6 5.8 %collective-permute-start.10 = (bf16[48,512]{1,0:T(8,128)(2,1)S(1)}, bf16[48,512]{1,0:T(8,128)(2,1)S(1)}, u32[]{:S(2)}, u32[]{:S(2)}) collective-permute-start(bf16[48,512]{1,0:T(8,128)(2,1)S(1)} %get-tuple-element.31), channel_id=1, source_target_pairs={{0,8},{1,9},{2,10},{3,11},{4,12},{5,13},{6,14},{7,15},{8,0},{9,1},... | collective-permute-start | bytes 147464 | tf_op jit(solution)/shard_map/ppermute | solution.py:360
  45.8 6.0 %collective-permute-start.11 = (bf16[48,512]{1,0:T(8,128)(2,1)S(1)}, bf16[48,512]{1,0:T(8,128)(2,1)S(1)}, u32[]{:S(2)}, u32[]{:S(2)}) collective-permute-start(bf16[48,512]{1,0:T(8,128)(2,1)S(1)} %get-tuple-element.32), channel_id=1, source_target_pairs={{0,12},{1,13},{2,14},{3,15},{4,8},{5,9},{6,10},{7,11},{8,4},{9,5},... | collective-permute-start | bytes 147464 | tf_op jit(solution)/shard_map/ppermute | solution.py:360

commit v3 on v2

--- a/solution.py
+++ b/solution.py
@@ -11,11 +11,24 @@
 F32 = jnp.float32
 BF16 = jnp.bfloat16
 AXIS = "ha"
+BOTH = ("groups", AXIS)
 PHASES = 4
 
 
 def dot(left, right):
     return jnp.dot(left, right, preferred_element_type=F32)
+
+
+def neighbours(far, near):
+    index = lax.axis_index(AXIS)
+    is_even = index % 2 == 0
+    above = jnp.where(is_even, far, near)
+    below = jnp.where(is_even, near, far)
+    zero = jnp.zeros_like(above)
+    return (
+        jnp.where(index == 0, zero, above),
+        jnp.where(index == lax.axis_size(AXIS) - 1, zero, below),
+    )
 
 
 def lanes(parts):
@@ -62,13 +75,25 @@
     return lanes([w_ref[row, tap] for tap in range(3)])
 
 
-def edge_kernel(video_ref, w_ref, far_ref, near_ref, tap_ref):
+def edge_kernel(video_ref, w_ref, far_ref, near_ref, row_ref, weight_ref, tap_ref, row_sem, weight_sem):
     parity = lax.axis_index(AXIS) % 2
     frames, rows, cols, channels = video_ref.shape
-    for ref, side in ((far_ref, parity), (near_ref, 1 - parity)):
-        row = side * (rows - 1)
-        weight = tap_matrix(w_ref, 2 - 2 * side)
-        total = dot(video_ref[:, row].reshape(frames * cols, channels), weight)
+    sides = (parity, 1 - parity)
+    copies = []
+    for at, side in enumerate(sides):
+        pair = (
+            pltpu.make_async_copy(
+                video_ref.at[:, side * (rows - 1)], row_ref.at[at], row_sem.at[at]
+            ),
+            pltpu.make_async_copy(w_ref.at[2 - 2 * side], weight_ref.at[at], weight_sem.at[at]),
+        )
+        for copy in pair:
+            copy.start()
+        copies.append(pair)
+    for at, ref in enumerate((far_ref, near_ref)):
+        for copy in copies[at]:
+            copy.wait()
+        total = dot(row_ref[at].reshape(frames * cols, channels), tap_matrix(weight_ref, at))
 
         def store(frame, phase, value, ref=ref):
             ref[frame, phase] = value.astype(BF16)
@@ -97,13 +122,11 @@
 def first_kernel(acc_ref, far_ref, near_ref, t_ref, r_ref, d_ref, far_out, near_out, a_ref, h_ref):
     frames, rows, phases, count, channels = acc_ref.shape
     parity = lax.axis_index(AXIS) % 2
-    is_even = parity == 0
     sites = rows * phases * count
     for frame in range(frames):
         far = far_ref[frame].astype(F32)
         near = near_ref[frame].astype(F32)
-        above = jnp.where(is_even, far, near)
-        below = jnp.where(is_even, near, far)
+        above, below = neighbours(far, near)
         for row in range(rows):
             value = acc_ref[frame, row]
             if row == 0:
@@ -170,8 +193,6 @@
     h_out, *blocks = refs[: frames + 1]
     a_ref, h_ref = refs[frames + 1 :]
     index = lax.axis_index(AXIS)
-    parity = index % 2
-    is_even = parity == 0
     sites = frames * count
     halos = []
     for side in range(2):
@@ -180,8 +201,7 @@
         halos.append((far, near))
     far = jnp.concatenate([pair[0] for pair in halos], axis=0)
     near = jnp.concatenate([pair[1] for pair in halos], axis=0)
-    above = jnp.where(is_even, far, near)
-    below = jnp.where(is_even, near, far)
+    above, below = neighbours(far, near)
     for row in range(rows):
         values = [acc_ref[:, row, side].reshape(sites, channels) for side in range(sides)]
         for here, halo, tap in ((0, above, 0), (rows - 1, below, 2)):
@@ -224,6 +244,21 @@
                     block[pl.ds(out_row * count, count), :] = refs_normed[frame]
 
 
+def scored(mapped, sites):
+    scores = lax.dot_general(
+        mapped, sites, (((1,), (1,)), ((), ())), preferred_element_type=F32
+    ) * (1.0 / math.sqrt(mapped.shape[-1]))
+    top = jnp.max(scores, axis=-1, keepdims=True)
+    weights = jnp.exp(scores - top)
+    return top, jnp.sum(weights, axis=-1, keepdims=True), dot(weights.astype(BF16), sites)
+
+
+def joined(left, right):
+    top = jnp.maximum(left[0], right[0])
+    one, two = jnp.exp(left[0] - top), jnp.exp(right[0] - top)
+    return top, left[1] * one + right[1] * two, left[2] * one + right[2] * two
+
+
 def query_kernel(own_ref, q_ref, k_ref, out_ref):
     queries = dot(own_ref[...], q_ref[...]).astype(BF16)
     out_ref[...] = lax.dot_general(
@@ -231,19 +266,20 @@
     ).astype(BF16)
 
 
-def attention_kernel(mapped_ref, sites_ref, v_ref, o_ref, *blocks):
-    channels = mapped_ref.shape[-1]
-    score_scale = 1.0 / math.sqrt(channels)
-    scores = (
-        lax.dot_general(
-            mapped_ref[...], sites_ref[...], (((1,), (1,)), ((), ())), preferred_element_type=F32
-        )
-        * score_scale
-    )
-    weights = jnp.exp(scores - jnp.max(scores, axis=-1, keepdims=True))
-    totals = jnp.sum(weights, axis=-1, keepdims=True)
-    mixed = (dot(weights.astype(BF16), sites_ref[...]) / totals).astype(BF16)
-    attended = dot(mixed, v_ref[...]).astype(BF16)
+def early_kernel(mapped_ref, *refs):
+    *site_refs, top_ref, total_ref, mixed_ref = refs
+    sites = jnp.concatenate([ref[...] for ref in site_refs], axis=0)
+    top, total, mixed_ref[...] = scored(mapped_ref[...], sites)
+    top_ref[...] = jnp.broadcast_to(top, top_ref.shape)
+    total_ref[...] = jnp.broadcast_to(total, total_ref.shape)
+
+
+def late_kernel(mapped_ref, top_ref, total_ref, mixed_ref, v_ref, o_ref, *refs, parts):
+    site_refs, blocks = refs[:parts], refs[parts:]
+    sites = jnp.concatenate([ref[...] for ref in site_refs], axis=0)
+    early = top_ref[:, :1], total_ref[:, :1], mixed_ref[...]
+    _, total, mixed = joined(early, scored(mapped_ref[...], sites))
+    attended = dot((mixed / total).astype(BF16), v_ref[...]).astype(BF16)
     result = dot(attended, o_ref[...]).astype(BF16)
     count = blocks[0].shape[0]
     for step, block in enumerate(blocks):
@@ -260,27 +296,25 @@
         out_ref[frame] = (h_ref[frame].astype(F32) + value).astype(BF16)
 
 
-def call(kernel, outs, scratch, args, flops, name):
+def call(kernel, outs, scratch, args, flops, name, space=pltpu.VMEM, sems=(), limit=None):
     vmem = pl.BlockSpec(memory_space=pltpu.VMEM)
     shapes = [jax.ShapeDtypeStruct(shape, dtype) for shape, dtype in outs]
     moved = sum(math.prod(arg.shape) * arg.dtype.itemsize for arg in args)
     moved += sum(math.prod(shape) * jnp.dtype(dtype).itemsize for shape, dtype in outs)
-    used = moved + sum(
-        math.prod(shape) * jnp.dtype(dtype).itemsize for shape, dtype in scratch
-    )
     return pl.pallas_call(
         kernel,
         out_shape=shapes,
-        in_specs=[vmem] * len(args),
+        in_specs=[pl.BlockSpec(memory_space=space)] * len(args),
         out_specs=[vmem] * len(outs),
-        scratch_shapes=[pltpu.VMEM(shape, dtype) for shape, dtype in scratch],
-        compiler_params=pltpu.CompilerParams(vmem_limit_bytes=LIMIT),
+        scratch_shapes=[pltpu.VMEM(shape, dtype) for shape, dtype in scratch] + list(sems),
+        compiler_params=pltpu.CompilerParams(vmem_limit_bytes=limit or LIMIT),
         cost_estimate=pl.CostEstimate(flops=int(flops), bytes_accessed=int(moved), transcendentals=0),
         name=name,
     )(*args)
 
 
 LIMIT = 40 * 1024 * 1024
+WHOLE = 67043328
 
 
 def per_device(
@@ -303,8 +337,16 @@
     devices = lax.axis_size(AXIS)
     group_size = devices // frames
     inner = [(d, d ^ 1) for d in range(devices)]
+    groups = lax.axis_size("groups")
     outer = [(d, d + 1) for d in range(1, devices - 1, 2)]
     outer = outer + [(target, source) for source, target in outer]
+    outer = [(g * devices + a, g * devices + b) for g in range(groups) for a, b in outer]
+    if groups % 2 == 0:
+        outer += [
+            (g * devices + end, (g ^ 1) * devices + end)
+            for g in range(groups)
+            for end in (0, devices - 1)
+        ]
     turns = [
         [(d, (d // group_size ^ k) * group_size + d % group_size) for d in range(devices)]
         for k in range(frames)
@@ -313,8 +355,18 @@
     edge = ((frames, PHASES, count, c1), BF16)
     taps = ((3, frames, cols, c1), F32)
     site_flops = 2 * frames * cols * 3 * c0 * c1
-    far, near = call(edge_kernel, [edge, edge], [taps], [video, s1_weight], 2 * site_flops, "edge")
-    far = lax.ppermute(far, AXIS, outer)
+    far, near = call(
+        edge_kernel,
+        [edge, edge],
+        [((2, frames, cols, c0), BF16), ((2, 3, c0, c1), BF16), taps],
+        [video, s1_weight],
+        2 * site_flops,
+        "edge",
+        pltpu.HBM,
+        [pltpu.SemaphoreType.DMA((2,))] * 2,
+        WHOLE,
+    )
+    far = lax.ppermute(far, BOTH, outer)
     near = lax.ppermute(near, AXIS, inner)
     shape = (frames, rows, PHASES, count, c1)
     (acc,) = call(
@@ -330,7 +382,7 @@
         5e8,
         "first",
     )
-    far = lax.ppermute(far, AXIS, outer)
+    far = lax.ppermute(far, BOTH, outer)
     near = lax.ppermute(near, AXIS, inner)
     (acc,) = call(middle_kernel, [(half, F32)], [], [d_first, s2_weight], 6e8, "middle")
     site_rows = rows // 4
@@ -346,16 +398,44 @@
     own = jnp.concatenate(
         [blocks[0]] + [lax.ppermute(blocks[k], AXIS, turns[k]) for k in range(1, frames)], axis=0
     )
-    sites = own
+    site_count = own.shape[0]
+    bits = []
     bit = group_size // 2
-    while bit:
-        sites = jnp.concatenate(
-            [sites, lax.ppermute(sites, AXIS, [(d, d ^ bit) for d in range(devices)])], axis=0
-        )
+    while bit > 1:
+        bits.append(bit)
         bit //= 2
+
+    def swap(x, bit):
+        return lax.ppermute(x, AXIS, [(d, d ^ bit) for d in range(devices)])
+
+    far_sites = []
+    have = [own]
+    for bit in bits:
+        whole = jnp.concatenate(have, axis=0) if len(have) > 1 else have[0]
+        got = swap(whole, bit)
+        far_sites.append(got)
+        have = have + [got]
+    partner = swap(own, 1)
     (mapped,) = call(query_kernel, [(own.shape, BF16)], [], [own, w_query, w_key], 2e8, "query")
+    stats = ((site_count, 128), F32)
+    early = call(
+        early_kernel,
+        [stats, stats, (own.shape, F32)],
+        [],
+        [mapped, own, partner],
+        3e8,
+        "early",
+    )
+    far_sites = jnp.concatenate(far_sites, axis=0) if len(far_sites) > 1 else far_sites[0]
+    far_sites, early = lax.optimization_barrier((far_sites, early))
+    late = [far_sites, swap(far_sites, 1)]
     blocks = call(
-        attention_kernel, [block] * frames, [], [mapped, sites, w_value, w_out], 6e8, "attention"
+        functools.partial(late_kernel, parts=len(late)),
+        [block] * frames,
+        [],
+        [mapped, *early, w_value, w_out, *late],
+        6e8,
+        "late",
     )
     blocks = [blocks[0]] + [lax.ppermute(blocks[k], AXIS, turns[k]) for k in range(1, frames)]
     (encoded,) = call(

time: 52.8 us -> 48.7 us (0.922)
  starting transfers between devices: 24.8 us -> 16.9 us
  Pallas kernels: 8.57 us -> 11 us
  waiting for transfers between devices: 16.4 us -> 17.9 us
    ppermute x2, starting transfers between devices: 10.4 us -> 1.22 us  [per_device(): near = lax.ppermute(near, AXIS, inner)]
    ppermute x4 -> x5, starting transfers between devices: 3.54 us -> 6.61 us  [the longest x2 4.59 us: per_device(): far = lax.ppermute(far, BOTH, outer)]
    pallas_call x8 -> x9, Pallas kernels: 8.57 us -> 11 us  [call(): pl.pallas_call(kernel, out_shape=shapes, in_specs=[pl.BlockSpec(memory_sp...]
    ppermute x4 -> x5, waiting for transfers between devices: 6.22 us -> 8.12 us  [the longest x3 5.84 us: swap(): return lax.ppermute(x, AXIS, [(d, d ^ bit) for d in range(devices)])]
    ppermute x6, starting transfers between devices: 10.9 us -> 9.09 us  [per_device(): lax.ppermute(blocks[k], AXIS, turns[k])]
    unnamed x28 -> x27, local copies, waits for them, and re-layouts: 2.52 us -> 2.49 us
  transfers between devices with their start and end apart: 12 -> 13, of which waited for: 8 -> 8; matrix products, arithmetic and copies ran while one was open for 0% -> 0% of each run, Pallas kernels for 7% -> 9%
where the time goes in v3:
time: 48.7 us; the launch traced here: 48.5 us
  waiting for transfers between devices  17.9 us (37%)
  starting transfers between devices  16.9 us (35%)
  Pallas kernels  11 us (23%)
  local copies, waits for them, and re-layouts  2.5 us (5%)
    pallas_call x9, Pallas kernels, call(): pl.pallas_call(kernel, out_shape=shapes, in_specs=[pl.BlockSpec(memory_sp...  11 us
    ppermute x6, waiting for transfers between devices, per_device(): lax.ppermute(blocks[k], AXIS, turns[k])  9.77 us
    ppermute x6, starting transfers between devices, per_device(): lax.ppermute(blocks[k], AXIS, turns[k])  9.09 us
    ppermute x3, waiting for transfers between devices, swap(): return lax.ppermute(x, AXIS, [(d, d ^ bit) for d in range(devices)])  5.84 us
    ppermute x2, starting transfers between devices, per_device(): far = lax.ppermute(far, BOTH, outer)  4.59 us
    unnamed x27, local copies, waits for them, and re-layouts  2.49 us
    ppermute x2, waiting for transfers between devices, per_device(): far = lax.ppermute(far, BOTH, outer)  2.28 us
    ppermute x3, starting transfers between devices, swap(): return lax.ppermute(x, AXIS, [(d, d ^ bit) for d in range(devices)])  2.02 us
  transfers between devices with their start and end apart: 13, of which 8 were waited for; matrix products, arithmetic and copies ran while one was open for 0% of the time, Pallas kernels for 9%

profile of v3, /device:TPU:0, one launch (start us, length us, event | category | flops | bytes accessed | tf_op | source)
XLA Modules:
  0.0 48.5 jit_solution(14450181485355559291)
XLA Ops:
  0.0 2.5 %edge.1 = (bf16[4,4,48,128]{3,2,1,0:T(8,128)(2,1)}, bf16[4,4,48,128]{3,2,1,0:T(8,128)(2,1)}) custom-call(bf16[4,4,192,192]{3,2,1,0:T(8,128)(2,1)} %video_ref.3, bf16[3,3,192,128]{3,2,1,0:T(8,128)(2,1)} %w_ref.5), custom_call_target="tpu_custom_call" | custom-call | flops 226492416 | bytes 2015232 | tf_op jit(solution)/shard_map/edge/pallas_call | solution.py:304
  2.6 3.0 %collective-permute-start = (bf16[4,4,48,128]{3,2,1,0:T(8,128)(2,1)}, bf16[4,4,48,128]{3,2,1,0:T(8,128)(2,1)S(1)}, u32[]{:S(2)}, u32[]{:S(2)}) collective-permute-start(bf16[4,4,48,128]{3,2,1,0:T(8,128)(2,1)} %get-tuple-element.26), channel_id=1, source_target_pairs={{1,2},{3,4},{5,6},{7,8},{9,10},{11,12},{13,14},{2,1},{4,3},{6,5},{... | collective-permute-start | bytes 589832 | tf_op jit(solution)/shard_map/ppermute | solution.py:369
  5.6 0.1 collective-permute-start.1
  5.7 1.4 %copy-done.1 = bf16[4,4,192,192]{3,2,1,0:T(8,128)(2,1)S(1)} copy-done((bf16[4,4,192,192]{3,2,1,0:T(8,128)(2,1)S(1)}, bf16[4,4,192,192]{3,2,1,0:T(8,128)(2,1)}, u32[]{:S(2)}) %copy-start.1) | copy-done | bytes 1179672
  7.2 1.0 %copy-done.7 = bf16[3,3,192,128]{3,2,1,0:T(8,128)(2,1)S(1)} copy-done((bf16[3,3,192,128]{3,2,1,0:T(8,128)(2,1)S(1)}, bf16[3,3,192,128]{3,2,1,0:T(8,128)(2,1)}, u32[]{:S(2)}) %copy-start.7) | copy-done | bytes 442392
  8.2 2.4 %inner.1.acc_ref = f32[4,4,4,48,128]{4,3,2,1,0:T(8,128)S(1)} custom-call(bf16[4,4,192,192]{3,2,1,0:T(8,128)(2,1)S(1)} %copy-done.1, bf16[3,3,192,128]{3,2,1,0:T(8,128)(2,1)S(1)} %copy-done.7), custom_call_target="tpu_custom_call" | custom-call | flops 1132462080 | bytes 3194880 | tf_op jit(solution)/shard_map/inner/pallas_call | solution.py:304
  10.5 0.0 copy-start.11
  10.6 0.9 %first.1 = (bf16[4,2,2,48,256]{4,3,2,1,0:T(8,128)(2,1)S(1)}, bf16[4,2,48,256]{3,2,1,0:T(8,128)(2,1)S(1)}, bf16[4,2,48,256]{3,2,1,0:T(8,128)(2,1)S(1)}) custom-call(f32[4,4,4,48,128]{4,3,2,1,0:T(8,128)S(1)} %inner.1.acc_ref, bf16[4,4,48,128]{3,2,1,0:T(8,128)(2,1)S(1)} %collective-permute-done.far_ref, ...), custom_call_target="tpu_custom_call" | custom-call | flops 500000000 | bytes 3112960 | tf_op jit(solution)/shard_map/first/pallas_call | solution.py:304
  11.5 0.0 copy-start.8
  11.6 1.6 %collective-permute-start.2 = (bf16[4,2,48,256]{3,2,1,0:T(8,128)(2,1)S(1)}, bf16[4,2,48,256]{3,2,1,0:T(8,128)(2,1)S(1)}, u32[]{:S(2)}, u32[]{:S(2)}) collective-permute-start(bf16[4,2,48,256]{3,2,1,0:T(8,128)(2,1)S(1)} %get-tuple-element.29), channel_id=1, source_target_pairs={{1,2},{3,4},{5,6},{7,8},{9,10},{11,12},{13,14},{2,1},{4,3},{6,5},{... | collective-permute-start | bytes 589832 | tf_op jit(solution)/shard_map/ppermute | solution.py:385
  13.1 1.1 %collective-permute-start.3 = (bf16[4,2,48,256]{3,2,1,0:T(8,128)(2,1)S(1)}, bf16[4,2,48,256]{3,2,1,0:T(8,128)(2,1)S(1)}, u32[]{:S(2)}, u32[]{:S(2)}) collective-permute-start(bf16[4,2,48,256]{3,2,1,0:T(8,128)(2,1)S(1)} %get-tuple-element.30), channel_id=1, source_target_pairs={{0,1},{1,0},{2,3},{3,2},{4,5},{5,4},{6,7},{7,6},{8,9},{9,8},{10,11... | collective-permute-start | bytes 589832 | tf_op jit(solution)/shard_map/ppermute | solution.py:386
  14.2 0.8 %middle.1.acc_ref = f32[4,2,2,48,256]{4,3,2,1,0:T(8,128)S(1)} custom-call(bf16[4,2,2,48,256]{4,3,2,1,0:T(8,128)(2,1)S(1)} %get-tuple-element.28.d_ref, bf16[3,3,256,256]{3,2,1,0:T(8,128)(2,1)S(1)} %copy-done), custom_call_target="tpu_custom_call" | custom-call | flops 600000000 | bytes 2359296 | tf_op jit(solution)/shard_map/middle/pallas_call | solution.py:304
  15.0 2.3 %collective-permute-done.2.far_ref = bf16[4,2,48,256]{3,2,1,0:T(8,128)(2,1)S(1)} collective-permute-done((bf16[4,2,48,256]{3,2,1,0:T(8,128)(2,1)S(1)}, bf16[4,2,48,256]{3,2,1,0:T(8,128)(2,1)S(1)}, u32[]{:S(2)}, u32[]{:S(2)}) %collective-permute-start.2) | collective-permute-done | bytes 196640 | tf_op jit(solution)/shard_map/ppermute | solution.py:385
  17.3 1.4 %second.1 = (bf16[4,1,48,512]{3,2,1,0:T(8,128)(2,1)S(1)}, bf16[48,512]{1,0:T(8,128)(2,1)S(1)}, bf16[48,512]{1,0:T(8,128)(2,1)S(1)}, bf16[48,512]{1,0:T(8,128)(2,1)S(1)}, bf16[48,512]{1,0:T(8,128)(2,1)S(1)}) custom-call(f32[4,2,2,48,256]{4,3,2,1,0:T(8,128)S(1)} %middle.1.acc_ref, bf16[4,2,48,256]{3,2,1,0:T(8,128)(2,1)S(1)} %collective-permute-done.2.far_ref, ...), custom_call_target="tpu_custom_call" | custom-call | flops 800000000 | bytes 4588544 | tf_op jit(solution)/shard_map/second/pallas_call | solution.py:304
  18.7 2.0 %collective-permute-start.4 = (bf16[48,512]{1,0:T(8,128)(2,1)S(1)}, bf16[48,512]{1,0:T(8,128)(2,1)S(1)}, u32[]{:S(2)}, u32[]{:S(2)}) collective-permute-start(bf16[48,512]{1,0:T(8,128)(2,1)S(1)} %get-tuple-element.33), channel_id=1, source_target_pairs={{0,4},{1,5},{2,6},{3,7},{4,0},{5,1},{6,2},{7,3},{8,12},{9,13},{10,... | collective-permute-start | bytes 147464 | tf_op jit(solution)/shard_map/ppermute | solution.py:399
  20.8 2.6 %collective-permute-start.5 = (bf16[48,512]{1,0:T(8,128)(2,1)S(1)}, bf16[48,512]{1,0:T(8,128)(2,1)S(1)}, u32[]{:S(2)}, u32[]{:S(2)}) collective-permute-start(bf16[48,512]{1,0:T(8,128)(2,1)S(1)} %get-tuple-element.34), channel_id=1, source_target_pairs={{0,8},{1,9},{2,10},{3,11},{4,12},{5,13},{6,14},{7,15},{8,0},{9,1},... | collective-permute-start | bytes 147464 | tf_op jit(solution)/shard_map/ppermute | solution.py:399
  23.4 3.8 %collective-permute-done.5 = bf16[48,512]{1,0:T(8,128)(2,1)S(1)} collective-permute-done((bf16[48,512]{1,0:T(8,128)(2,1)S(1)}, bf16[48,512]{1,0:T(8,128)(2,1)S(1)}, u32[]{:S(2)}, u32[]{:S(2)}) %collective-permute-start.5) | collective-permute-done | bytes 49184 | tf_op jit(solution)/shard_map/ppermute | solution.py:399
  27.2 2.3 %collective-permute-done.6 = bf16[48,512]{1,0:T(8,128)(2,1)S(1)} collective-permute-done((bf16[48,512]{1,0:T(8,128)(2,1)S(1)}, bf16[48,512]{1,0:T(8,128)(2,1)S(1)}, u32[]{:S(2)}, u32[]{:S(2)}) %collective-permute-start.6) | collective-permute-done | bytes 49184 | tf_op jit(solution)/shard_map/ppermute | solution.py:399
  29.5 0.1 collective-permute-start.8
  29.6 1.9 %collective-permute-start.7 = (bf16[192,512]{1,0:T(8,128)(2,1)S(1)}, bf16[192,512]{1,0:T(8,128)(2,1)S(1)}, u32[]{:S(2)}, u32[]{:S(2)}) collective-permute-start(bf16[192,512]{1,0:T(8,128)(2,1)S(1)} %constant_dynamic-update-slice_fusion.own_ref.refs_0_), channel_id=1, source_target_pairs={{0,2},{1,3},{2,0},{3,1},{4,6},{5,7},{6,4},{7,5},{8,10},{9,11},{10,... | collective-permute-start | bytes 589832 | tf_op jit(solution)/shard_map/ppermute | solution.py:409
  31.5 0.5 query.1.mapped_ref
  32.0 0.6 %early.1 = (f32[192,128]{1,0:T(8,128)S(1)}, f32[192,128]{1,0:T(8,128)S(1)}, f32[192,512]{1,0:T(8,128)S(1)}) custom-call(bf16[192,512]{1,0:T(8,128)(2,1)S(1)} %query.1.mapped_ref, bf16[192,512]{1,0:T(8,128)(2,1)S(1)} %constant_dynamic-update-slice_fusion.own_ref.refs_0_, bf16[192,512]{1,0:T(8,128)(2,1)S(1)} %collective-permute-done.8.refs_1_), custom_call_target="tpu_custom_call" | custom-call | flops 300000000 | bytes 1179648 | tf_op jit(solution)/shard_map/early/pallas_call | solution.py:304
  32.6 4.4 %collective-permute-done.7.refs_0_ = bf16[192,512]{1,0:T(8,128)(2,1)S(1)} collective-permute-done((bf16[192,512]{1,0:T(8,128)(2,1)S(1)}, bf16[192,512]{1,0:T(8,128)(2,1)S(1)}, u32[]{:S(2)}, u32[]{:S(2)}) %collective-permute-start.7) | collective-permute-done | bytes 196640 | tf_op jit(solution)/shard_map/ppermute | solution.py:409
  37.0 1.4 %collective-permute-done.9.refs_1_ = bf16[192,512]{1,0:T(8,128)(2,1)S(1)} collective-permute-done((bf16[192,512]{1,0:T(8,128)(2,1)S(1)}, bf16[192,512]{1,0:T(8,128)(2,1)S(1)}, u32[]{:S(2)}, u32[]{:S(2)}) %collective-permute-start.9) | collective-permute-done | bytes 196640 | tf_op jit(solution)/shard_map/ppermute | solution.py:409
  38.5 1.2 %late.1 = (bf16[48,512]{1,0:T(8,128)(2,1)S(1)}, bf16[48,512]{1,0:T(8,128)(2,1)S(1)}, bf16[48,512]{1,0:T(8,128)(2,1)S(1)}, bf16[48,512]{1,0:T(8,128)(2,1)S(1)}) custom-call(bf16[192,512]{1,0:T(8,128)(2,1)S(1)} %query.1.mapped_ref, f32[192,128]{1,0:T(8,128)S(1)} %get-tuple-element.39.top_ref, f32[192,128]{1,0:T(8,128)S(1)} %get-tuple-element.40.total_ref, ...), custom_call_target="tpu_custom_call" | custom-call | flops 600000000 | bytes 2424832 | tf_op jit(solution)/shard_map/late/pallas_call | solution.py:304
  39.7 0.1 collective-permute-start.10
  39.8 2.1 %collective-permute-start.11 = (bf16[48,512]{1,0:T(8,128)(2,1)S(1)}, bf16[48,512]{1,0:T(8,128)(2,1)S(1)}, u32[]{:S(2)}, u32[]{:S(2)}) collective-permute-start(bf16[48,512]{1,0:T(8,128)(2,1)S(1)} %get-tuple-element.45), channel_id=1, source_target_pairs={{0,8},{1,9},{2,10},{3,11},{4,12},{5,13},{6,14},{7,15},{8,0},{9,1},... | collective-permute-start | bytes 147464 | tf_op jit(solution)/shard_map/ppermute | solution.py:440
  41.9 2.2 %collective-permute-start.12 = (bf16[48,512]{1,0:T(8,128)(2,1)S(1)}, bf16[48,512]{1,0:T(8,128)(2,1)S(1)}, u32[]{:S(2)}, u32[]{:S(2)}) collective-permute-start(bf16[48,512]{1,0:T(8,128)(2,1)S(1)} %get-tuple-element.46), channel_id=1, source_target_pairs={{0,12},{1,13},{2,14},{3,15},{4,8},{5,9},{6,10},{7,11},{8,4},{9,5},... | collective-permute-start | bytes 147464 | tf_op jit(solution)/shard_map/ppermute | solution.py:440
  44.1 0.3 collective-permute-done.10.refs_1_
  44.4 1.3 %collective-permute-done.11.refs_2_ = bf16[48,512]{1,0:T(8,128)(2,1)S(1)} collective-permute-done((bf16[48,512]{1,0:T(8,128)(2,1)S(1)}, bf16[48,512]{1,0:T(8,128)(2,1)S(1)}, u32[]{:S(2)}, u32[]{:S(2)}) %collective-permute-start.11) | collective-permute-done | bytes 49184 | tf_op jit(solution)/shard_map/ppermute | solution.py:440
  45.7 2.1 %collective-permute-done.12.refs_3_ = bf16[48,512]{1,0:T(8,128)(2,1)S(1)} collective-permute-done((bf16[48,512]{1,0:T(8,128)(2,1)S(1)}, bf16[48,512]{1,0:T(8,128)(2,1)S(1)}, u32[]{:S(2)}, u32[]{:S(2)}) %collective-permute-start.12) | collective-permute-done | bytes 49184 | tf_op jit(solution)/shard_map/ppermute | solution.py:440
  47.8 0.7 %sum.1 = bf16[4,1,48,512]{3,2,1,0:T(8,128)(2,1)} custom-call(bf16[4,1,48,512]{3,2,1,0:T(8,128)(2,1)S(1)} %get-tuple-element.31.h_ref, bf16[48,512]{1,0:T(8,128)(2,1)S(1)} %get-tuple-element.43.refs_0_, bf16[48,512]{1,0:T(8,128)(2,1)S(1)} %collective-permute-done.10.refs_1_, bf16[48,512]{1,0:T(8,128)(2,1)S(1)} %collective-permute-done.11.refs_2_, ...), custom_call_target="tpu_custom_call" | custom-call | flops 1000000 | bytes 589824 | tf_op jit(solution)/shard_map/sum/pallas_call | solution.py:304
  (32 shorter events, 0.1 us)
Async XLA Ops:
  2.6 8.0 %collective-permute-start = (bf16[4,4,48,128]{3,2,1,0:T(8,128)(2,1)}, bf16[4,4,48,128]{3,2,1,0:T(8,128)(2,1)S(1)}, u32[]{:S(2)}, u32[]{:S(2)}) collective-permute-start(bf16[4,4,48,128]{3,2,1,0:T(8,128)(2,1)} %get-tuple-element.26), channel_id=1, source_target_pairs={{1,2},{3,4},{5,6},{7,8},{9,10},{11,12},{13,14},{2,1},{4,3},{6,5},{... | collective-permute-start | bytes 589832 | tf_op jit(solution)/shard_map/ppermute | solution.py:369
  5.6 5.0 %collective-permute-start.1 = (bf16[4,4,48,128]{3,2,1,0:T(8,128)(2,1)}, bf16[4,4,48,128]{3,2,1,0:T(8,128)(2,1)S(1)}, u32[]{:S(2)}, u32[]{:S(2)}) collective-permute-start(bf16[4,4,48,128]{3,2,1,0:T(8,128)(2,1)} %get-tuple-element.27), channel_id=1, source_target_pairs={{0,1},{1,0},{2,3},{3,2},{4,5},{5,4},{6,7},{7,6},{8,9},{9,8},{10,11... | collective-permute-start | bytes 589832 | tf_op jit(solution)/shard_map/ppermute | solution.py:370
  5.7 1.4 %copy-start.1 = (bf16[4,4,192,192]{3,2,1,0:T(8,128)(2,1)S(1)}, bf16[4,4,192,192]{3,2,1,0:T(8,128)(2,1)}, u32[]{:S(2)}) copy-start(bf16[4,4,192,192]{3,2,1,0:T(8,128)(2,1)} %video_ref.3) | copy-start | bytes 3538948
  7.1 1.0 %copy-start.7 = (bf16[3,3,192,128]{3,2,1,0:T(8,128)(2,1)S(1)}, bf16[3,3,192,128]{3,2,1,0:T(8,128)(2,1)}, u32[]{:S(2)}) copy-start(bf16[3,3,192,128]{3,2,1,0:T(8,128)(2,1)} %w_ref.5) | copy-start | bytes 1327108
  8.2 2.4 %copy-start.9 = (bf16[2,2,128,256]{3,2,1,0:T(8,128)(2,1)S(1)}, bf16[2,2,128,256]{3,2,1,0:T(8,128)(2,1)}, u32[]{:S(2)}) copy-start(bf16[2,2,128,256]{3,2,1,0:T(8,128)(2,1)} %r_ref.2) | copy-start | bytes 786436
  8.2 2.4 %copy-start.10 = (bf16[3,128,128]{2,1,0:T(8,128)(2,1)S(1)}, bf16[3,128,128]{2,1,0:T(8,128)(2,1)}, u32[]{:S(2)}) copy-start(bf16[3,128,128]{2,1,0:T(8,128)(2,1)} %t_ref.2) | copy-start | bytes 294916
  10.5 3.7 %copy-start.11 = (bf16[512]{0:T(512)(128)(2,1)S(1)}, bf16[512]{0:T(512)(128)(2,1)}, u32[]{:S(2)}) copy-start(bf16[512]{0:T(512)(128)(2,1)} %param.19) | copy-start | bytes 3076
  10.5 3.7 %copy-start = (bf16[3,3,256,256]{3,2,1,0:T(8,128)(2,1)S(1)}, bf16[3,3,256,256]{3,2,1,0:T(8,128)(2,1)}, u32[]{:S(2)}) copy-start(bf16[3,3,256,256]{3,2,1,0:T(8,128)(2,1)} %w_ref.7) | copy-start | bytes 3538948
  11.5 5.8 %copy-start.2 = (bf16[2,2,256,512]{3,2,1,0:T(8,128)(2,1)S(1)}, bf16[2,2,256,512]{3,2,1,0:T(8,128)(2,1)}, u32[]{:S(2)}) copy-start(bf16[2,2,256,512]{3,2,1,0:T(8,128)(2,1)} %r_ref.3) | copy-start | bytes 3145732
  11.5 5.8 %copy-start.8 = (bf16[3,256,256]{2,1,0:T(8,128)(2,1)S(1)}, bf16[3,256,256]{2,1,0:T(8,128)(2,1)}, u32[]{:S(2)}) copy-start(bf16[3,256,256]{2,1,0:T(8,128)(2,1)} %t_ref.3) | copy-start | bytes 1179652
  11.6 5.7 %collective-permute-start.2 = (bf16[4,2,48,256]{3,2,1,0:T(8,128)(2,1)S(1)}, bf16[4,2,48,256]{3,2,1,0:T(8,128)(2,1)S(1)}, u32[]{:S(2)}, u32[]{:S(2)}) collective-permute-start(bf16[4,2,48,256]{3,2,1,0:T(8,128)(2,1)S(1)} %get-tuple-element.29), channel_id=1, source_target_pairs={{1,2},{3,4},{5,6},{7,8},{9,10},{11,12},{13,14},{2,1},{4,3},{6,5},{... | collective-permute-start | bytes 589832 | tf_op jit(solution)/shard_map/ppermute | solution.py:385
  13.1 4.2 %collective-permute-start.3 = (bf16[4,2,48,256]{3,2,1,0:T(8,128)(2,1)S(1)}, bf16[4,2,48,256]{3,2,1,0:T(8,128)(2,1)S(1)}, u32[]{:S(2)}, u32[]{:S(2)}) collective-permute-start(bf16[4,2,48,256]{3,2,1,0:T(8,128)(2,1)S(1)} %get-tuple-element.30), channel_id=1, source_target_pairs={{0,1},{1,0},{2,3},{3,2},{4,5},{5,4},{6,7},{7,6},{8,9},{9,8},{10,11... | collective-permute-start | bytes 589832 | tf_op jit(solution)/shard_map/ppermute | solution.py:386
  15.0 16.5 %copy-start.5 = (bf16[512,512]{1,0:T(8,128)(2,1)S(1)}, bf16[512,512]{1,0:T(8,128)(2,1)}, u32[]{:S(2)}) copy-start(bf16[512,512]{1,0:T(8,128)(2,1)} %q_ref.1) | copy-start | bytes 1572868
  15.0 16.5 %copy-start.6 = (bf16[512,512]{1,0:T(8,128)(2,1)S(1)}, bf16[512,512]{1,0:T(8,128)(2,1)}, u32[]{:S(2)}) copy-start(bf16[512,512]{1,0:T(8,128)(2,1)} %k_ref.1) | copy-start | bytes 1572868
  18.7 19.8 %copy-start.3 = (bf16[512,512]{1,0:T(8,128)(2,1)S(1)}, bf16[512,512]{1,0:T(8,128)(2,1)}, u32[]{:S(2)}) copy-start(bf16[512,512]{1,0:T(8,128)(2,1)} %v_ref.1) | copy-start | bytes 1572868
  18.7 19.7 %copy-start.4 = (bf16[512,512]{1,0:T(8,128)(2,1)S(1)}, bf16[512,512]{1,0:T(8,128)(2,1)}, u32[]{:S(2)}) copy-start(bf16[512,512]{1,0:T(8,128)(2,1)} %o_ref.1) | copy-start | bytes 1572868
  18.7 4.7 %collective-permute-start.4 = (bf16[48,512]{1,0:T(8,128)(2,1)S(1)}, bf16[48,512]{1,0:T(8,128)(2,1)S(1)}, u32[]{:S(2)}, u32[]{:S(2)}) collective-permute-start(bf16[48,512]{1,0:T(8,128)(2,1)S(1)} %get-tuple-element.33), channel_id=1, source_target_pairs={{0,4},{1,5},{2,6},{3,7},{4,0},{5,1},{6,2},{7,3},{8,12},{9,13},{10,... | collective-permute-start | bytes 147464 | tf_op jit(solution)/shard_map/ppermute | solution.py:399
  20.8 6.4 %collective-permute-start.5 = (bf16[48,512]{1,0:T(8,128)(2,1)S(1)}, bf16[48,512]{1,0:T(8,128)(2,1)S(1)}, u32[]{:S(2)}, u32[]{:S(2)}) collective-permute-start(bf16[48,512]{1,0:T(8,128)(2,1)S(1)} %get-tuple-element.34), channel_id=1, source_target_pairs={{0,8},{1,9},{2,10},{3,11},{4,12},{5,13},{6,14},{7,15},{8,0},{9,1},... | collective-permute-start | bytes 147464 | tf_op jit(solution)/shard_map/ppermute | solution.py:399
  23.4 6.1 %collective-permute-start.6 = (bf16[48,512]{1,0:T(8,128)(2,1)S(1)}, bf16[48,512]{1,0:T(8,128)(2,1)S(1)}, u32[]{:S(2)}, u32[]{:S(2)}) collective-permute-start(bf16[48,512]{1,0:T(8,128)(2,1)S(1)} %get-tuple-element.35), channel_id=1, source_target_pairs={{0,12},{1,13},{2,14},{3,15},{4,8},{5,9},{6,10},{7,11},{8,4},{9,5},... | collective-permute-start | bytes 147464 | tf_op jit(solution)/shard_map/ppermute | solution.py:399
  29.5 2.5 %collective-permute-start.8 = (bf16[192,512]{1,0:T(8,128)(2,1)S(1)}, bf16[192,512]{1,0:T(8,128)(2,1)S(1)}, u32[]{:S(2)}, u32[]{:S(2)}) collective-permute-start(bf16[192,512]{1,0:T(8,128)(2,1)S(1)} %constant_dynamic-update-slice_fusion.own_ref.refs_0_), channel_id=1, source_target_pairs={{0,1},{1,0},{2,3},{3,2},{4,5},{5,4},{6,7},{7,6},{8,9},{9,8},{10,11... | collective-permute-start | bytes 589832 | tf_op jit(solution)/shard_map/ppermute | solution.py:409
  29.6 7.4 %collective-permute-start.7 = (bf16[192,512]{1,0:T(8,128)(2,1)S(1)}, bf16[192,512]{1,0:T(8,128)(2,1)S(1)}, u32[]{:S(2)}, u32[]{:S(2)}) collective-permute-start(bf16[192,512]{1,0:T(8,128)(2,1)S(1)} %constant_dynamic-update-slice_fusion.own_ref.refs_0_), channel_id=1, source_target_pairs={{0,2},{1,3},{2,0},{3,1},{4,6},{5,7},{6,4},{7,5},{8,10},{9,11},{10,... | collective-permute-start | bytes 589832 | tf_op jit(solution)/shard_map/ppermute | solution.py:409
  37.0 1.4 %collective-permute-start.9 = (bf16[192,512]{1,0:T(8,128)(2,1)S(1)}, bf16[192,512]{1,0:T(8,128)(2,1)S(1)}, u32[]{:S(2)}, u32[]{:S(2)}) collective-permute-start(bf16[192,512]{1,0:T(8,128)(2,1)S(1)} %collective-permute-done.7.refs_0_), channel_id=1, source_target_pairs={{0,1},{1,0},{2,3},{3,2},{4,5},{5,4},{6,7},{7,6},{8,9},{9,8},{10,11... | collective-permute-start | bytes 589832 | tf_op jit(solution)/shard_map/ppermute | solution.py:409
  39.7 4.8 %collective-permute-start.10 = (bf16[48,512]{1,0:T(8,128)(2,1)S(1)}, bf16[48,512]{1,0:T(8,128)(2,1)S(1)}, u32[]{:S(2)}, u32[]{:S(2)}) collective-permute-start(bf16[48,512]{1,0:T(8,128)(2,1)S(1)} %get-tuple-element.44), channel_id=1, source_target_pairs={{0,4},{1,5},{2,6},{3,7},{4,0},{5,1},{6,2},{7,3},{8,12},{9,13},{10,... | collective-permute-start | bytes 147464 | tf_op jit(solution)/shard_map/ppermute | solution.py:440
  39.8 5.9 %collective-permute-start.11 = (bf16[48,512]{1,0:T(8,128)(2,1)S(1)}, bf16[48,512]{1,0:T(8,128)(2,1)S(1)}, u32[]{:S(2)}, u32[]{:S(2)}) collective-permute-start(bf16[48,512]{1,0:T(8,128)(2,1)S(1)} %get-tuple-element.45), channel_id=1, source_target_pairs={{0,8},{1,9},{2,10},{3,11},{4,12},{5,13},{6,14},{7,15},{8,0},{9,1},... | collective-permute-start | bytes 147464 | tf_op jit(solution)/shard_map/ppermute | solution.py:440
  41.9 5.9 %collective-permute-start.12 = (bf16[48,512]{1,0:T(8,128)(2,1)S(1)}, bf16[48,512]{1,0:T(8,128)(2,1)S(1)}, u32[]{:S(2)}, u32[]{:S(2)}) collective-permute-start(bf16[48,512]{1,0:T(8,128)(2,1)S(1)} %get-tuple-element.46), channel_id=1, source_target_pairs={{0,12},{1,13},{2,14},{3,15},{4,8},{5,9},{6,10},{7,11},{8,4},{9,5},... | collective-permute-start | bytes 147464 | tf_op jit(solution)/shard_map/ppermute | solution.py:440

commit v4 on v3

v4 whole, which is shorter than its diff:
```python
import functools
import math

import jax
import jax.numpy as jnp
from jax import lax
from jax.experimental import pallas as pl
from jax.experimental.pallas import tpu as pltpu
from jax.sharding import PartitionSpec as P


F32 = jnp.float32
BF16 = jnp.bfloat16
AXIS = "ha"
BOTH = ("groups", AXIS)
PHASES = 4


def dot(left, right):
    return jnp.dot(left, right, preferred_element_type=F32)


def turn():
    return lax.axis_index(AXIS) % 2


def whole_row(row, count):
    return row + turn() * (count - 1 - 2 * row)


def inside(far):
    index = lax.axis_index(AXIS)
    at_end = (index == 0) | (index == lax.axis_size(AXIS) - 1)
    return jnp.where(at_end, jnp.zeros_like(far), far)


def causal(a, t_ref):
    frames, sites, channels = a.shape
    total = None
    for lag in range(3):
        count = frames - lag
        term = dot(a[:count].reshape(count * sites, channels), t_ref[2 - lag]).reshape(
            count, sites, -1
        )
        total = (
            term if total is None else jnp.concatenate([total[:lag], total[lag:] + term], axis=0)
        )
    return total


def reduction(r_ref):
    first = turn()
    return jnp.concatenate(
        [r_ref[first, 0], r_ref[first, 1], r_ref[1 - first, 0], r_ref[1 - first, 1]], axis=0
    )


def lanes(parts):
    return parts[0] if len(parts) == 1 else jnp.concatenate(parts, axis=-1)


def silu(x):
    return 0.5 * x * (1.0 + jnp.tanh(0.5 * x))


def shifted(x, step, period):
    rows = x.shape[0]
    place = lax.broadcasted_iota(jnp.int32, x.shape, 0) % period
    moved = pltpu.roll(x, step % rows, 0)
    return jnp.where(place == (0 if step == 1 else period - 1), 0.0, moved)


def place_phases(total, tap_ref, out_of):
    _, frames, cols, channels = tap_ref.shape
    count = cols // PHASES
    for tap in range(3):
        tap_ref[tap] = total[:, tap * channels : (tap + 1) * channels].reshape(
            frames, cols, channels
        )
    for frame in range(frames):
        def strided(tap, phase):
            return tap_ref[tap, frame, pl.ds(phase, count, stride=PHASES), :]

        for phase in range(PHASES):
            before = (
                shifted(strided(0, PHASES - 1), 1, count)
                if phase == 0
                else strided(0, phase - 1)
            )
            after = (
                shifted(strided(2, 0), -1, count)
                if phase == PHASES - 1
                else strided(2, phase + 1)
            )
            out_of(frame, phase, before + strided(1, phase) + after)


def tap_matrix(w_ref, row):
    return lanes([w_ref[row, tap] for tap in range(3)])


def edge_kernel(
    video_ref, w_ref, far_ref, near_ref, row_ref, weight_ref, tap_ref, row_sem, weight_sem
):
    frames, rows, cols, channels = video_ref.shape
    side = turn()
    copies = []
    for at, (row, tap) in enumerate((((rows - 1) * side, 2 - 2 * side), ((rows - 1) * (1 - side), 2 * side))):
        group = [
            pltpu.make_async_copy(
                video_ref.at[frame, row], row_ref.at[at, frame], row_sem.at[at, frame]
            )
            for frame in range(frames)
        ] + [
            pltpu.make_async_copy(
                w_ref.at[tap, column], weight_ref.at[at, column], weight_sem.at[at, column]
            )
            for column in range(3)
        ]
        for copy in group:
            copy.start()
        copies.append(group)
    for at, ref in enumerate((far_ref, near_ref)):
        for copy in copies[at]:
            copy.wait()
        total = dot(row_ref[at].reshape(frames * cols, channels), tap_matrix(weight_ref, at))

        def store(frame, phase, value, ref=ref):
            ref[frame, phase] = value.astype(BF16)

        place_phases(total, tap_ref, store)


def inner_kernel(
    video_ref, w_ref, edge_ref, weight_ref, acc_ref, row_ref, middle_ref, tap_ref, row_sem, w_sem
):
    frames, rows, cols, channels = video_ref.shape
    w_copies = [
        pltpu.make_async_copy(w_ref.at[1, column], middle_ref.at[0, column], w_sem.at[column])
        for column in range(3)
    ]
    copies = {
        row: [
            pltpu.make_async_copy(
                video_ref.at[frame, whole_row(row, rows)],
                row_ref.at[row - 1, frame],
                row_sem.at[row - 1, frame],
            )
            for frame in range(frames)
        ]
        for row in range(1, rows - 1)
    }
    for copy in w_copies + [copy for group in copies.values() for copy in group]:
        copy.start()
    for copy in w_copies:
        copy.wait()

    def source_row(row):
        ref, at = (
            (edge_ref, 0) if row == 0 else (edge_ref, 1) if row == rows - 1 else (row_ref, row - 1)
        )
        return ref[at].reshape(frames * cols, channels)

    waited = set()
    for row in range(rows):
        total = None
        for step, (ref, at) in ((0, (middle_ref, 0)), (-1, (weight_ref, 1)), (1, (weight_ref, 0))):
            source = row + step
            if 0 <= source < rows:
                if source in copies and source not in waited:
                    waited.add(source)
                    for copy in copies[source]:
                        copy.wait()
                term = dot(source_row(source), tap_matrix(ref, at))
                total = term if total is None else total + term

        def store(frame, phase, value, row=row):
            acc_ref[row, frame, phase] = value

        place_phases(total, tap_ref, store)


def to_half(h, weight, frames, phases, count):
    return [
        dot(lanes([h(row, 2 * side + j) for row in range(2) for j in range(2)]), weight)
        .astype(BF16)
        .reshape(frames, count, -1)
        for side in range(phases // 2)
    ]


def near_kernel(acc_ref, near_ref, t_ref, r_ref, d_ref, h_out, h_ref):
    rows, frames, phases, count, channels = acc_ref.shape
    for row in range(1, rows):
        value = acc_ref[row]
        if row == rows - 1:
            value = value + near_ref[...].astype(F32)
        a = value.astype(BF16).reshape(frames, phases * count, channels)
        h_ref[row - 1] = silu(causal(a, t_ref)).astype(BF16).reshape(h_ref.shape[1:])
    h_out[...] = h_ref[0]
    weight = reduction(r_ref)
    for half in range(1, rows // 2):
        parts = to_half(
            lambda row, phase: h_ref[2 * half + row - 1, :, phase].reshape(
                frames * count, channels
            ),
            weight,
            frames,
            phases,
            count,
        )
        for side, part in enumerate(parts):
            d_ref[half - 1, :, side] = part


def far_kernel(acc_ref, far_ref, h_in, t_ref, r_ref, d_ref):
    _, frames, phases, count, channels = acc_ref.shape
    value = acc_ref[0] + inside(far_ref[...].astype(F32))
    a = value.astype(BF16).reshape(frames, phases * count, channels)
    h = silu(causal(a, t_ref)).astype(BF16).reshape(frames, phases, count, channels)
    parts = to_half(
        lambda row, phase: (h_in[:, phase] if row else h[:, phase]).reshape(
            frames * count, channels
        ),
        reduction(r_ref),
        frames,
        phases,
        count,
    )
    for side, part in enumerate(parts):
        d_ref[:, side] = part


def place_pairs(total, sites, count, channels):
    even, odd = total[:sites], total[sites:]
    first, middle, last = (slice(tap * channels, (tap + 1) * channels) for tap in range(3))
    return (
        shifted(odd[:, first], 1, count) + even[:, middle] + odd[:, last],
        even[:, first] + odd[:, middle] + shifted(even[:, last], -1, count),
    )


def flat(d):
    frames, sides, count, channels = d.shape
    return jnp.concatenate(
        [d[:, side].reshape(frames * count, channels) for side in range(sides)], axis=0
    )


def by_side(pair, shape):
    frames, _, count, channels = shape
    return jnp.stack([value.reshape(frames, count, channels) for value in pair], axis=1)


def second_rows(a, d, t_ref):
    frames, sides, count, channels = d.shape
    mixed = silu(causal(a.astype(BF16).reshape(frames, sides * count, channels), t_ref))
    return (d.astype(F32) + mixed.reshape(d.shape)).astype(BF16)


def middle_kernel(far_ref, rest_ref, near_ref, w_ref, t_ref, acc_ref, h_ref):
    shape = far_ref.shape
    frames, _, count, channels = shape
    sites = frames * count
    rows = rest_ref.shape[0] + 1
    side = turn()
    taps = {-1: 2 * side, 0: 1, 1: 2 - 2 * side}
    held = [far_ref[...]] + [rest_ref[row] for row in range(rows - 1)] + [near_ref[...]]
    for row in range(rows):
        total = None
        for step, tap in taps.items():
            if row + step >= 0:
                term = dot(flat(held[row + step]), tap_matrix(w_ref, tap))
                total = term if total is None else total + term
        a = by_side(place_pairs(total, sites, count, channels), shape)
        if row == 0:
            acc_ref[...] = a
        else:
            h_ref[row - 1] = second_rows(a, held[row], t_ref)


def second_kernel(
    acc_ref, far_ref, d_ref, rest_ref, w_ref, t_ref, r_ref, gain_ref, h_out, *blocks, group_size
):
    shape = d_ref.shape
    frames, _, count, channels = shape
    sites = frames * count
    more = dot(flat(inside(far_ref[...])), tap_matrix(w_ref, 2 * turn()))
    a = acc_ref[...] + by_side(place_pairs(more, sites, count, channels), shape)
    held = [second_rows(a, d_ref[...], t_ref)] + [rest_ref[row] for row in range(rest_ref.shape[0])]
    weight = reduction(r_ref)
    wide = weight.shape[-1]
    gain = gain_ref[...].astype(F32)
    place = lax.axis_index(AXIS) // group_size
    halves = len(held) // 2
    for half in range(halves):
        left = lanes(
            [held[2 * half + i][:, j].reshape(sites, channels) for i in range(2) for j in range(2)]
        )
        out_row = whole_row(half, halves) if halves > 1 else 0
        residual = dot(left, weight).astype(BF16)
        h_out[:, out_row] = residual.reshape(frames, count, wide)
        residual = residual.astype(F32)
        mean_square = jnp.mean(residual * residual, axis=-1, keepdims=True)
        normed = (residual * lax.rsqrt(mean_square + 1e-06) * gain).astype(BF16)
        normed = normed.reshape(frames, count, wide)
        for frame in range(frames):
            for step, block in enumerate(blocks):

                @pl.when(place ^ step == frame)
                def _(block=block, frame=frame, half=half, normed=normed):
                    at = out_row * count if halves > 1 else 0
                    block[pl.ds(at, count), :] = normed[frame]


def scored(mapped, sites):
    scores = lax.dot_general(
        mapped, sites, (((1,), (1,)), ((), ())), preferred_element_type=F32
    ) * (1.0 / math.sqrt(mapped.shape[-1]))
    top = jnp.max(scores, axis=-1, keepdims=True)
    weights = jnp.exp(scores - top)
    return top, jnp.sum(weights, axis=-1, keepdims=True), dot(weights.astype(BF16), sites)


def joined(left, right):
    top = jnp.maximum(left[0], right[0])
    one, two = jnp.exp(left[0] - top), jnp.exp(right[0] - top)
    return top, left[1] * one + right[1] * two, left[2] * one + right[2] * two


def query_kernel(own_ref, q_ref, k_ref, out_ref):
    queries = dot(own_ref[...], q_ref[...]).astype(BF16)
    out_ref[...] = lax.dot_general(
        queries, k_ref[...], (((1,), (1,)), ((), ())), preferred_element_type=F32
    ).astype(BF16)


def early_kernel(mapped_ref, *refs):
    *site_refs, top_ref, total_ref, mixed_ref = refs
    sites = jnp.concatenate([ref[...] for ref in site_refs], axis=0)
    top, total, mixed_ref[...] = scored(mapped_ref[...], sites)
    top_ref[...] = jnp.broadcast_to(top, top_ref.shape)
    total_ref[...] = jnp.broadcast_to(total, total_ref.shape)


def late_kernel(mapped_ref, top_ref, total_ref, mixed_ref, v_ref, o_ref, *refs, parts):
    site_refs, blocks = refs[:parts], refs[parts:]
    sites = jnp.concatenate([ref[...] for ref in site_refs], axis=0)
    early = top_ref[:, :1], total_ref[:, :1], mixed_ref[...]
    _, total, mixed = joined(early, scored(mapped_ref[...], sites))
    attended = dot((mixed / total).astype(BF16), v_ref[...]).astype(BF16)
    result = dot(attended, o_ref[...]).astype(BF16)
    count = blocks[0].shape[0]
    for step, block in enumerate(blocks):
        block[...] = result[step * count : (step + 1) * count]


def sum_kernel(h_ref, *refs, group_size):
    *blocks, out_ref = refs
    _, rows, count, channels = h_ref.shape
    place = lax.axis_index(AXIS) // group_size
    for step, block in enumerate(blocks):
        frame = place ^ step
        value = block[...].astype(F32).reshape(rows, count, channels)
        out_ref[frame] = (h_ref[frame].astype(F32) + value).astype(BF16)


def call(kernel, outs, scratch, args, flops, spaces=None, sems=(), limit=None):
    vmem = pl.BlockSpec(memory_space=pltpu.VMEM)
    shapes = [jax.ShapeDtypeStruct(shape, dtype) for shape, dtype in outs]
    moved = sum(math.prod(arg.shape) * arg.dtype.itemsize for arg in args)
    moved += sum(math.prod(shape) * jnp.dtype(dtype).itemsize for shape, dtype in outs)
    return pl.pallas_call(
        kernel,
        out_shape=shapes,
        in_specs=[pl.BlockSpec(memory_space=space) for space in spaces or [pltpu.VMEM] * len(args)],
        out_specs=[vmem] * len(outs),
        scratch_shapes=[pltpu.VMEM(shape, dtype) for shape, dtype in scratch] + list(sems),
        compiler_params=pltpu.CompilerParams(vmem_limit_bytes=limit or LIMIT),
        cost_estimate=pl.CostEstimate(flops=int(flops), bytes_accessed=int(moved), transcendentals=0),
    )(*args)


LIMIT = 40 * 1024 * 1024
WHOLE = 40 << 20


def per_device(
    video,
    s1_weight,
    t1_weight,
    r1_weight,
    s2_weight,
    t2_weight,
    r2_weight,
    attn_gain,
    w_query,
    w_key,
    w_value,
    w_out,
):
    frames, rows, cols, c0 = video.shape
    c1, c2, c3 = s1_weight.shape[-1], s2_weight.shape[-1], w_out.shape[-1]
    count = cols // PHASES
    devices = lax.axis_size(AXIS)
    group_size = devices // frames
    inner = [(d, d ^ 1) for d in range(devices)]
    groups = lax.axis_size("groups")
    outer = [(d, d + 1) for d in range(1, devices - 1, 2)]
    outer = outer + [(target, source) for source, target in outer]
    outer = [(g * devices + a, g * devices + b) for g in range(groups) for a, b in outer]
    if groups % 2 == 0:
        outer += [
            (g * devices + end, (g ^ 1) * devices + end)
            for g in range(groups)
            for end in (0, devices - 1)
        ]
    turns = [
        [(d, (d // group_size ^ k) * group_size + d % group_size) for d in range(devices)]
        for k in range(frames)
    ]

    edge = ((frames, PHASES, count, c1), BF16)
    taps = ((3, frames, cols, c1), F32)
    dma = pltpu.SemaphoreType.DMA
    site_flops = 2 * frames * cols * 3 * c0 * c1
    video = pltpu.with_memory_space_constraint(video, pltpu.HBM)
    s1_weight = pltpu.with_memory_space_constraint(s1_weight, pltpu.HBM)
    far, near, edge_rows, edge_weight = call(
        edge_kernel,
        [edge, edge, ((2, frames, cols, c0), BF16), ((2, 3, c0, c1), BF16)],
        [taps],
        [video, s1_weight],
        2 * site_flops,
        [pltpu.HBM] * 2,
        [dma((2, frames)), dma((2, 3))],
        WHOLE,
    )
    far = lax.ppermute(far, BOTH, outer)
    near = lax.ppermute(near, AXIS, inner)
    (acc,) = call(
        inner_kernel,
        [((rows, frames, PHASES, count, c1), F32)],
        [((rows - 2, frames, cols, c0), BF16), ((1, 3, c0, c1), BF16), taps],
        [video, s1_weight, edge_rows, edge_weight],
        10 * site_flops,
        [pltpu.HBM] * 2 + [pltpu.VMEM] * 2,
        [dma((rows - 2, frames)), dma((3,))],
        WHOLE,
    )
    half = (frames, 2, count, c2)
    rest = ((rows // 2 - 1, *half), BF16)
    rest_of, h_next = call(
        near_kernel,
        [rest, edge],
        [((rows - 1, frames, PHASES, count, c1), BF16)],
        [acc, near, t1_weight, r1_weight],
        4e8,
    )
    near = lax.ppermute(rest_of[-1], AXIS, inner)
    (d_far,) = call(far_kernel, [(half, BF16)], [], [acc, far, h_next, t1_weight, r1_weight], 2e8)
    far = lax.ppermute(d_far, BOTH, outer)
    acc, h_rest = call(
        middle_kernel, [(half, F32), rest], [], [d_far, rest_of, near, s2_weight, t2_weight], 9e8
    )
    site_rows = rows // 4
    block = ((site_rows * count, c3), BF16)
    residual, *blocks = call(
        functools.partial(second_kernel, group_size=group_size),
        [((frames, site_rows, count, c3), BF16)] + [block] * frames,
        [],
        [acc, far, d_far, h_rest, s2_weight, t2_weight, r2_weight, attn_gain.reshape(1, c3)],
        6e8,
    )
    own = jnp.concatenate(
        [blocks[0]] + [lax.ppermute(blocks[k], AXIS, turns[k]) for k in range(1, frames)], axis=0
    )
    site_count = own.shape[0]
    bits = []
    bit = group_size // 2
    while bit > 1:
        bits.append(bit)
        bit //= 2

    def swap(x, bit):
        return lax.ppermute(x, AXIS, [(d, d ^ bit) for d in range(devices)])

    far_sites = []
    have = [own]
    for bit in bits:
        whole = jnp.concatenate(have, axis=0) if len(have) > 1 else have[0]
        got = swap(whole, bit)
        far_sites.append(got)
        have = have + [got]
    (mapped,) = call(query_kernel, [(own.shape, BF16)], [], [own, w_query, w_key], 2e8)
    own, mapped = lax.optimization_barrier((own, mapped))
    partner = swap(own, 1)
    stats = ((site_count, 128), F32)
    early = call(early_kernel, [stats, stats, (own.shape, F32)], [], [mapped, own, partner], 3e8)
    far_sites = jnp.concatenate(far_sites, axis=0) if len(far_sites) > 1 else far_sites[0]
    far_sites, early = lax.optimization_barrier((far_sites, early))
    late = [far_sites, swap(far_sites, 1)]
    blocks = call(
        functools.partial(late_kernel, parts=len(late)),
        [block] * frames,
        [],
        [mapped, *early, w_value, w_out, *late],
        6e8,
    )
    blocks = [blocks[0]] + [lax.ppermute(blocks[k], AXIS, turns[k]) for k in range(1, frames)]
    (encoded,) = call(
        functools.partial(sum_kernel, group_size=group_size),
        [(residual.shape, BF16)],
        [],
        [residual, *blocks],
        1e6,
    )
    return encoded


def solution(mesh):
    placed = (P("groups", "ha", None, None), P(), P(), P(), P(), P(), P(), P(), P(), P(), P(), P())
    return jax.shard_map(
        per_device,
        mesh=mesh,
        in_specs=placed,
        out_specs=P("groups", "ha", None, None),
        check_vma=False,
    )
```

time: 48.7 us -> 48.2 us (0.990)
  local copies, waits for them, and re-layouts: 2.5 us -> 0.07 us
  Pallas kernels: 11 us -> 12.9 us
  waiting for transfers between devices: 17.9 us -> 19 us
  starting transfers between devices: 16.9 us -> 15.9 us
    ppermute x0 -> x2, waiting for transfers between devices: none -> 2.78 us  [the longest x1 2.78 us: per_device(): far = lax.ppermute(d_far, BOTH, outer)]
    unnamed x27 -> x23, local copies, waits for them, and re-layouts: 2.49 us -> 0.06 us
    ppermute x2 -> x1, waiting for transfers between devices: 2.28 us -> 0.01 us  [per_device(): far = lax.ppermute(far, BOTH, outer)]
    ppermute x2 -> x1, starting transfers between devices: 4.59 us -> 2.56 us  [per_device(): far = lax.ppermute(far, BOTH, outer)]
    pallas_call x9 -> x10, Pallas kernels: 11 us -> 12.9 us  [call(): pl.pallas_call(kernel, out_shape=shapes, in_specs=[pl.BlockSpec(memory_sp...]
    ppermute x0 -> x2, starting transfers between devices: none -> 1.77 us  [the longest x1 1.56 us: per_device(): far = lax.ppermute(d_far, BOTH, outer)]
    ppermute x2 -> x1, starting transfers between devices: 1.22 us -> 0.56 us  [per_device(): near = lax.ppermute(near, AXIS, inner)]
  transfers between devices with their start and end apart: 13 -> 13, of which waited for: 8 -> 8; matrix products, arithmetic and copies ran while one was open for 0% -> 0% of each run, Pallas kernels for 9% -> 15%
where the time goes in v4:
time: 48.2 us; the launch traced here: 48 us
  waiting for transfers between devices  19 us (39%)
  starting transfers between devices  15.9 us (33%)
  Pallas kernels  12.9 us (27%)
    pallas_call x10, Pallas kernels, call(): pl.pallas_call(kernel, out_shape=shapes, in_specs=[pl.BlockSpec(memory_sp...  12.9 us
    ppermute x6, waiting for transfers between devices, per_device(): lax.ppermute(blocks[k], AXIS, turns[k])  9.87 us
    ppermute x6, starting transfers between devices, per_device(): lax.ppermute(blocks[k], AXIS, turns[k])  9.11 us
    ppermute x3, waiting for transfers between devices, swap(): return lax.ppermute(x, AXIS, [(d, d ^ bit) for d in range(devices)])  6.32 us
    ppermute x1, waiting for transfers between devices, per_device(): far = lax.ppermute(d_far, BOTH, outer)  2.78 us
    ppermute x1, starting transfers between devices, per_device(): far = lax.ppermute(far, BOTH, outer)  2.56 us
    ppermute x3, starting transfers between devices, swap(): return lax.ppermute(x, AXIS, [(d, d ^ bit) for d in range(devices)])  1.94 us
    ppermute x1, starting transfers between devices, per_device(): far = lax.ppermute(d_far, BOTH, outer)  1.56 us
  transfers between devices with their start and end apart: 13, of which 8 were waited for; matrix products, arithmetic and copies ran while one was open for 0% of the time, Pallas kernels for 15%

profile of v4, /device:TPU:0, one launch (start us, length us, event | category | flops | bytes accessed | tf_op | source)
XLA Modules:
  0.0 48.0 jit_solution(8658853006920529843)
XLA Ops:
  0.0 2.0 %shard_map.118 = (bf16[4,4,48,128]{3,2,1,0:T(8,128)(2,1)S(1)}, bf16[4,4,48,128]{3,2,1,0:T(8,128)(2,1)S(1)}, bf16[2,4,192,192]{3,2,1,0:T(8,128)(2,1)S(1)}, bf16[2,3,192,128]{3,2,1,0:T(8,128)(2,1)S(1)}) custom-call(bf16[4,4,192,192]{3,2,1,0:T(8,128)(2,1)} %video_ref.3, bf16[3,3,192,128]{3,2,1,0:T(8,128)(2,1)} %w_ref.5), custom_call_target="tpu_custom_call" | custom-call | flops 226492416 | bytes 2899968 | tf_op jit(solution)/shard_map/pallas_call | solution.py:373
  2.0 0.6 %collective-permute-start.1 = (bf16[4,4,48,128]{3,2,1,0:T(8,128)(2,1)S(1)}, bf16[4,4,48,128]{3,2,1,0:T(8,128)(2,1)S(1)}, u32[]{:S(2)}, u32[]{:S(2)}) collective-permute-start(bf16[4,4,48,128]{3,2,1,0:T(8,128)(2,1)S(1)} %get-tuple-element.34), channel_id=1, source_target_pairs={{0,1},{1,0},{2,3},{3,2},{4,5},{5,4},{6,7},{7,6},{8,9},{9,8},{10,11... | collective-permute-start | bytes 589832 | tf_op jit(solution)/shard_map/ppermute | solution.py:440
  2.6 2.6 %collective-permute-start = (bf16[4,4,48,128]{3,2,1,0:T(8,128)(2,1)S(1)}, bf16[4,4,48,128]{3,2,1,0:T(8,128)(2,1)S(1)}, u32[]{:S(2)}, u32[]{:S(2)}) collective-permute-start(bf16[4,4,48,128]{3,2,1,0:T(8,128)(2,1)S(1)} %get-tuple-element.33), channel_id=1, source_target_pairs={{1,2},{3,4},{5,6},{7,8},{9,10},{11,12},{13,14},{2,1},{4,3},{6,5},{... | collective-permute-start | bytes 589832 | tf_op jit(solution)/shard_map/ppermute | solution.py:439
  5.1 3.7 %shard_map.119.acc_ref = f32[4,4,4,48,128]{4,3,2,1,0:T(8,128)S(1)} custom-call(bf16[4,4,192,192]{3,2,1,0:T(8,128)(2,1)} %video_ref.3, bf16[3,3,192,128]{3,2,1,0:T(8,128)(2,1)} %w_ref.5, bf16[2,4,192,192]{3,2,1,0:T(8,128)(2,1)S(1)} %get-tuple-element.31.edge_ref, bf16[2,3,192,128]{3,2,1,0:T(8,128)(2,1)S(1)} %get-tuple-element.32.weight_ref), custom_call_target="tpu_custom_call" | custom-call | flops 1132462080 | bytes 4079616 | tf_op jit(solution)/shard_map/pallas_call | solution.py:373
  8.9 0.9 %shard_map.120 = (bf16[1,4,2,48,256]{4,3,2,1,0:T(8,128)(2,1)S(1)}, bf16[4,4,48,128]{3,2,1,0:T(8,128)(2,1)S(1)}) custom-call(f32[4,4,4,48,128]{4,3,2,1,0:T(8,128)S(1)} %shard_map.119.acc_ref, bf16[4,4,48,128]{3,2,1,0:T(8,128)(2,1)S(1)} %collective-permute-done.1.near_ref, bf16[3,128,128]{2,1,0:T(8,128)(2,1)S(1)} %copy-done.7, ...), custom_call_target="tpu_custom_call" | custom-call | flops 400000000 | bytes 2523136 | tf_op jit(solution)/shard_map/pallas_call | solution.py:373
  9.8 0.0 copy-start.9
  9.8 0.0 copy-start.8
  9.8 0.2 collective-permute-start.2
  10.0 0.6 %shard_map.121.far_ref.d_ref = bf16[4,2,48,256]{3,2,1,0:T(8,128)(2,1)S(1)} custom-call(f32[4,4,4,48,128]{4,3,2,1,0:T(8,128)S(1)} %shard_map.119.acc_ref, bf16[4,4,48,128]{3,2,1,0:T(8,128)(2,1)S(1)} %collective-permute-done.far_ref, bf16[4,4,48,128]{3,2,1,0:T(8,128)(2,1)S(1)} %get-tuple-element.35.h_in, bf16[3,128,128]{2,1,0:T(8,128)(2,1)S(1)} %copy-done.7, ...), custom_call_target="tpu_custom_call" | custom-call | flops 200000000 | bytes 2523136 | tf_op jit(solution)/shard_map/pallas_call | solution.py:373
  10.7 1.6 %collective-permute-start.3 = (bf16[4,2,48,256]{3,2,1,0:T(8,128)(2,1)S(1)}, bf16[4,2,48,256]{3,2,1,0:T(8,128)(2,1)S(1)}, u32[]{:S(2)}, u32[]{:S(2)}) collective-permute-start(bf16[4,2,48,256]{3,2,1,0:T(8,128)(2,1)S(1)} %shard_map.121.far_ref.d_ref), channel_id=1, source_target_pairs={{1,2},{3,4},{5,6},{7,8},{9,10},{11,12},{13,14},{2,1},{4,3},{6,5},{... | collective-permute-start | bytes 589832 | tf_op jit(solution)/shard_map/ppermute | solution.py:462
  12.3 1.3 %shard_map.122 = (f32[4,2,48,256]{3,2,1,0:T(8,128)S(1)}, bf16[1,4,2,48,256]{4,3,2,1,0:T(8,128)(2,1)S(1)}) custom-call(bf16[4,2,48,256]{3,2,1,0:T(8,128)(2,1)S(1)} %shard_map.121.far_ref.d_ref, bf16[1,4,2,48,256]{4,3,2,1,0:T(8,128)(2,1)S(1)} %get-tuple-element.36.rest_ref, bf16[4,2,48,256]{3,2,1,0:T(8,128)(2,1)S(1)} %collective-permute-done.2.near_ref, ...), custom_call_target="tpu_custom_call" | custom-call | flops 900000000 | bytes 2752512 | tf_op jit(solution)/shard_map/pallas_call | solution.py:373
  13.6 2.8 %collective-permute-done.3.far_ref = bf16[4,2,48,256]{3,2,1,0:T(8,128)(2,1)S(1)} collective-permute-done((bf16[4,2,48,256]{3,2,1,0:T(8,128)(2,1)S(1)}, bf16[4,2,48,256]{3,2,1,0:T(8,128)(2,1)S(1)}, u32[]{:S(2)}, u32[]{:S(2)}) %collective-permute-start.3) | collective-permute-done | bytes 196640 | tf_op jit(solution)/shard_map/ppermute | solution.py:462
  16.4 1.2 %shard_map.123 = (bf16[4,1,48,512]{3,2,1,0:T(8,128)(2,1)S(1)}, bf16[48,512]{1,0:T(8,128)(2,1)S(1)}, bf16[48,512]{1,0:T(8,128)(2,1)S(1)}, bf16[48,512]{1,0:T(8,128)(2,1)S(1)}, bf16[48,512]{1,0:T(8,128)(2,1)S(1)}) custom-call(f32[4,2,48,256]{3,2,1,0:T(8,128)S(1)} %get-tuple-element.37.acc_ref, bf16[4,2,48,256]{3,2,1,0:T(8,128)(2,1)S(1)} %collective-permute-done.3.far_ref, ...), custom_call_target="tpu_custom_call" | custom-call | flops 600000000 | bytes 3998720 | tf_op jit(solution)/shard_map/pallas_call | solution.py:373
  17.7 0.0 copy-start.4
  17.7 2.1 %collective-permute-start.4 = (bf16[48,512]{1,0:T(8,128)(2,1)S(1)}, bf16[48,512]{1,0:T(8,128)(2,1)S(1)}, u32[]{:S(2)}, u32[]{:S(2)}) collective-permute-start(bf16[48,512]{1,0:T(8,128)(2,1)S(1)} %get-tuple-element.41), channel_id=1, source_target_pairs={{0,4},{1,5},{2,6},{3,7},{4,0},{5,1},{6,2},{7,3},{8,12},{9,13},{10,... | collective-permute-start | bytes 147464 | tf_op jit(solution)/shard_map/ppermute | solution.py:476
  19.8 2.6 %collective-permute-start.5 = (bf16[48,512]{1,0:T(8,128)(2,1)S(1)}, bf16[48,512]{1,0:T(8,128)(2,1)S(1)}, u32[]{:S(2)}, u32[]{:S(2)}) collective-permute-start(bf16[48,512]{1,0:T(8,128)(2,1)S(1)} %get-tuple-element.42), channel_id=1, source_target_pairs={{0,8},{1,9},{2,10},{3,11},{4,12},{5,13},{6,14},{7,15},{8,0},{9,1},... | collective-permute-start | bytes 147464 | tf_op jit(solution)/shard_map/ppermute | solution.py:476
  22.4 3.8 %collective-permute-done.5 = bf16[48,512]{1,0:T(8,128)(2,1)S(1)} collective-permute-done((bf16[48,512]{1,0:T(8,128)(2,1)S(1)}, bf16[48,512]{1,0:T(8,128)(2,1)S(1)}, u32[]{:S(2)}, u32[]{:S(2)}) %collective-permute-start.5) | collective-permute-done | bytes 49184 | tf_op jit(solution)/shard_map/ppermute | solution.py:476
  26.2 2.3 %collective-permute-done.6 = bf16[48,512]{1,0:T(8,128)(2,1)S(1)} collective-permute-done((bf16[48,512]{1,0:T(8,128)(2,1)S(1)}, bf16[48,512]{1,0:T(8,128)(2,1)S(1)}, u32[]{:S(2)}, u32[]{:S(2)}) %collective-permute-start.6) | collective-permute-done | bytes 49184 | tf_op jit(solution)/shard_map/ppermute | solution.py:476
  28.5 0.5 shard_map.124.mapped_ref
  29.0 0.2 collective-permute-start.8
  29.2 1.8 %collective-permute-start.7 = (bf16[192,512]{1,0:T(8,128)(2,1)S(1)}, bf16[192,512]{1,0:T(8,128)(2,1)S(1)}, u32[]{:S(2)}, u32[]{:S(2)}) collective-permute-start(bf16[192,512]{1,0:T(8,128)(2,1)S(1)} %constant_dynamic-update-slice_fusion.own_ref.refs_0_), channel_id=1, source_target_pairs={{0,2},{1,3},{2,0},{3,1},{4,6},{5,7},{6,4},{7,5},{8,10},{9,11},{10,... | collective-permute-start | bytes 589832 | tf_op jit(solution)/shard_map/ppermute | solution.py:486
  30.9 0.6 %shard_map.125 = (f32[192,128]{1,0:T(8,128)S(1)}, f32[192,128]{1,0:T(8,128)S(1)}, f32[192,512]{1,0:T(8,128)S(1)}) custom-call(bf16[192,512]{1,0:T(8,128)(2,1)S(1)} %shard_map.124.mapped_ref, bf16[192,512]{1,0:T(8,128)(2,1)S(1)} %constant_dynamic-update-slice_fusion.own_ref.refs_0_, bf16[192,512]{1,0:T(8,128)(2,1)S(1)} %collective-permute-done.8.refs_1_), custom_call_target="tpu_custom_call" | custom-call | flops 300000000 | bytes 1179648 | tf_op jit(solution)/shard_map/pallas_call | solution.py:373
  31.5 4.9 %collective-permute-done.7.refs_0_ = bf16[192,512]{1,0:T(8,128)(2,1)S(1)} collective-permute-done((bf16[192,512]{1,0:T(8,128)(2,1)S(1)}, bf16[192,512]{1,0:T(8,128)(2,1)S(1)}, u32[]{:S(2)}, u32[]{:S(2)}) %collective-permute-start.7) | collective-permute-done | bytes 196640 | tf_op jit(solution)/shard_map/ppermute | solution.py:486
  36.4 1.4 %collective-permute-done.9.refs_1_ = bf16[192,512]{1,0:T(8,128)(2,1)S(1)} collective-permute-done((bf16[192,512]{1,0:T(8,128)(2,1)S(1)}, bf16[192,512]{1,0:T(8,128)(2,1)S(1)}, u32[]{:S(2)}, u32[]{:S(2)}) %collective-permute-start.9) | collective-permute-done | bytes 196640 | tf_op jit(solution)/shard_map/ppermute | solution.py:486
  37.8 1.2 %shard_map.126 = (bf16[48,512]{1,0:T(8,128)(2,1)S(1)}, bf16[48,512]{1,0:T(8,128)(2,1)S(1)}, bf16[48,512]{1,0:T(8,128)(2,1)S(1)}, bf16[48,512]{1,0:T(8,128)(2,1)S(1)}) custom-call(bf16[192,512]{1,0:T(8,128)(2,1)S(1)} %shard_map.124.mapped_ref, f32[192,128]{1,0:T(8,128)S(1)} %get-tuple-element.49.top_ref, f32[192,128]{1,0:T(8,128)S(1)} %get-tuple-element.50.total_ref, ...), custom_call_target="tpu_custom_call" | custom-call | flops 600000000 | bytes 2424832 | tf_op jit(solution)/shard_map/pallas_call | solution.py:373
  39.1 0.1 collective-permute-start.10
  39.2 2.1 %collective-permute-start.11 = (bf16[48,512]{1,0:T(8,128)(2,1)S(1)}, bf16[48,512]{1,0:T(8,128)(2,1)S(1)}, u32[]{:S(2)}, u32[]{:S(2)}) collective-permute-start(bf16[48,512]{1,0:T(8,128)(2,1)S(1)} %get-tuple-element.55), channel_id=1, source_target_pairs={{0,8},{1,9},{2,10},{3,11},{4,12},{5,13},{6,14},{7,15},{8,0},{9,1},... | collective-permute-start | bytes 147464 | tf_op jit(solution)/shard_map/ppermute | solution.py:510
  41.3 2.2 %collective-permute-start.12 = (bf16[48,512]{1,0:T(8,128)(2,1)S(1)}, bf16[48,512]{1,0:T(8,128)(2,1)S(1)}, u32[]{:S(2)}, u32[]{:S(2)}) collective-permute-start(bf16[48,512]{1,0:T(8,128)(2,1)S(1)} %get-tuple-element.56), channel_id=1, source_target_pairs={{0,12},{1,13},{2,14},{3,15},{4,8},{5,9},{6,10},{7,11},{8,4},{9,5},... | collective-permute-start | bytes 147464 | tf_op jit(solution)/shard_map/ppermute | solution.py:510
  43.5 0.3 collective-permute-done.10.refs_1_
  43.8 2.5 %collective-permute-done.11.refs_2_ = bf16[48,512]{1,0:T(8,128)(2,1)S(1)} collective-permute-done((bf16[48,512]{1,0:T(8,128)(2,1)S(1)}, bf16[48,512]{1,0:T(8,128)(2,1)S(1)}, u32[]{:S(2)}, u32[]{:S(2)}) %collective-permute-start.11) | collective-permute-done | bytes 49184 | tf_op jit(solution)/shard_map/ppermute | solution.py:510
  46.3 1.0 %collective-permute-done.12.refs_3_ = bf16[48,512]{1,0:T(8,128)(2,1)S(1)} collective-permute-done((bf16[48,512]{1,0:T(8,128)(2,1)S(1)}, bf16[48,512]{1,0:T(8,128)(2,1)S(1)}, u32[]{:S(2)}, u32[]{:S(2)}) %collective-permute-start.12) | collective-permute-done | bytes 49184 | tf_op jit(solution)/shard_map/ppermute | solution.py:510
  47.3 0.7 %shard_map.127 = bf16[4,1,48,512]{3,2,1,0:T(8,128)(2,1)} custom-call(bf16[4,1,48,512]{3,2,1,0:T(8,128)(2,1)S(1)} %get-tuple-element.39.h_ref, bf16[48,512]{1,0:T(8,128)(2,1)S(1)} %get-tuple-element.53.refs_0_, bf16[48,512]{1,0:T(8,128)(2,1)S(1)} %collective-permute-done.10.refs_1_, bf16[48,512]{1,0:T(8,128)(2,1)S(1)} %collective-permute-done.11.refs_2_, ...), custom_call_target="tpu_custom_call" | custom-call | flops 1000000 | bytes 589824 | tf_op jit(solution)/shard_map/pallas_call | solution.py:373
  (29 shorter events, 0.1 us)
Async XLA Ops:
  2.0 6.9 %collective-permute-start.1 = (bf16[4,4,48,128]{3,2,1,0:T(8,128)(2,1)S(1)}, bf16[4,4,48,128]{3,2,1,0:T(8,128)(2,1)S(1)}, u32[]{:S(2)}, u32[]{:S(2)}) collective-permute-start(bf16[4,4,48,128]{3,2,1,0:T(8,128)(2,1)S(1)} %get-tuple-element.34), channel_id=1, source_target_pairs={{0,1},{1,0},{2,3},{3,2},{4,5},{5,4},{6,7},{7,6},{8,9},{9,8},{10,11... | collective-permute-start | bytes 589832 | tf_op jit(solution)/shard_map/ppermute | solution.py:440
  2.6 7.5 %collective-permute-start = (bf16[4,4,48,128]{3,2,1,0:T(8,128)(2,1)S(1)}, bf16[4,4,48,128]{3,2,1,0:T(8,128)(2,1)S(1)}, u32[]{:S(2)}, u32[]{:S(2)}) collective-permute-start(bf16[4,4,48,128]{3,2,1,0:T(8,128)(2,1)S(1)} %get-tuple-element.33), channel_id=1, source_target_pairs={{1,2},{3,4},{5,6},{7,8},{9,10},{11,12},{13,14},{2,1},{4,3},{6,5},{... | collective-permute-start | bytes 589832 | tf_op jit(solution)/shard_map/ppermute | solution.py:439
  5.1 3.8 %copy-start.2 = (bf16[2,2,128,256]{3,2,1,0:T(8,128)(2,1)S(1)}, bf16[2,2,128,256]{3,2,1,0:T(8,128)(2,1)}, u32[]{:S(2)}) copy-start(bf16[2,2,128,256]{3,2,1,0:T(8,128)(2,1)} %r_ref.4) | copy-start | bytes 786436
  5.1 3.8 %copy-start.7 = (bf16[3,128,128]{2,1,0:T(8,128)(2,1)S(1)}, bf16[3,128,128]{2,1,0:T(8,128)(2,1)}, u32[]{:S(2)}) copy-start(bf16[3,128,128]{2,1,0:T(8,128)(2,1)} %t_ref.5) | copy-start | bytes 294916
  9.8 2.4 %copy-start.9 = (bf16[512]{0:T(512)(128)(2,1)S(1)}, bf16[512]{0:T(512)(128)(2,1)}, u32[]{:S(2)}) copy-start(bf16[512]{0:T(512)(128)(2,1)} %param.19) | copy-start | bytes 3076
  9.8 2.5 %copy-start = (bf16[3,3,256,256]{3,2,1,0:T(8,128)(2,1)S(1)}, bf16[3,3,256,256]{3,2,1,0:T(8,128)(2,1)}, u32[]{:S(2)}) copy-start(bf16[3,3,256,256]{3,2,1,0:T(8,128)(2,1)} %w_ref.7) | copy-start | bytes 3538948
  9.8 2.5 %copy-start.8 = (bf16[3,256,256]{2,1,0:T(8,128)(2,1)S(1)}, bf16[3,256,256]{2,1,0:T(8,128)(2,1)}, u32[]{:S(2)}) copy-start(bf16[3,256,256]{2,1,0:T(8,128)(2,1)} %t_ref.7) | copy-start | bytes 1179652
  9.8 2.4 %collective-permute-start.2 = (bf16[4,2,48,256]{3,2,1,0:T(8,128)(2,1)S(1)}, bf16[4,2,48,256]{3,2,1,0:T(8,128)(2,1)S(1)}, u32[]{:S(2)}, u32[]{:S(2)}) collective-permute-start(bf16[4,2,48,256]{3,2,1,0:T(8,128)(2,1)S(1)} %bitcast.1), channel_id=1, source_target_pairs={{0,1},{1,0},{2,3},{3,2},{4,5},{5,4},{6,7},{7,6},{8,9},{9,8},{10,11... | collective-permute-start | bytes 589832 | tf_op jit(solution)/shard_map/ppermute | solution.py:460
  10.7 5.7 %collective-permute-start.3 = (bf16[4,2,48,256]{3,2,1,0:T(8,128)(2,1)S(1)}, bf16[4,2,48,256]{3,2,1,0:T(8,128)(2,1)S(1)}, u32[]{:S(2)}, u32[]{:S(2)}) collective-permute-start(bf16[4,2,48,256]{3,2,1,0:T(8,128)(2,1)S(1)} %shard_map.121.far_ref.d_ref), channel_id=1, source_target_pairs={{1,2},{3,4},{5,6},{7,8},{9,10},{11,12},{13,14},{2,1},{4,3},{6,5},{... | collective-permute-start | bytes 589832 | tf_op jit(solution)/shard_map/ppermute | solution.py:462
  12.2 4.2 %copy-start.1 = (bf16[2,2,256,512]{3,2,1,0:T(8,128)(2,1)S(1)}, bf16[2,2,256,512]{3,2,1,0:T(8,128)(2,1)}, u32[]{:S(2)}) copy-start(bf16[2,2,256,512]{3,2,1,0:T(8,128)(2,1)} %r_ref.5) | copy-start | bytes 3145732
  16.4 12.1 %copy-start.5 = (bf16[512,512]{1,0:T(8,128)(2,1)S(1)}, bf16[512,512]{1,0:T(8,128)(2,1)}, u32[]{:S(2)}) copy-start(bf16[512,512]{1,0:T(8,128)(2,1)} %q_ref.1) | copy-start | bytes 1572868
  16.4 12.1 %copy-start.6 = (bf16[512,512]{1,0:T(8,128)(2,1)S(1)}, bf16[512,512]{1,0:T(8,128)(2,1)}, u32[]{:S(2)}) copy-start(bf16[512,512]{1,0:T(8,128)(2,1)} %k_ref.1) | copy-start | bytes 1572868
  17.7 20.2 %copy-start.3 = (bf16[512,512]{1,0:T(8,128)(2,1)S(1)}, bf16[512,512]{1,0:T(8,128)(2,1)}, u32[]{:S(2)}) copy-start(bf16[512,512]{1,0:T(8,128)(2,1)} %v_ref.1) | copy-start | bytes 1572868
  17.7 20.2 %copy-start.4 = (bf16[512,512]{1,0:T(8,128)(2,1)S(1)}, bf16[512,512]{1,0:T(8,128)(2,1)}, u32[]{:S(2)}) copy-start(bf16[512,512]{1,0:T(8,128)(2,1)} %o_ref.1) | copy-start | bytes 1572868
  17.7 4.7 %collective-permute-start.4 = (bf16[48,512]{1,0:T(8,128)(2,1)S(1)}, bf16[48,512]{1,0:T(8,128)(2,1)S(1)}, u32[]{:S(2)}, u32[]{:S(2)}) collective-permute-start(bf16[48,512]{1,0:T(8,128)(2,1)S(1)} %get-tuple-element.41), channel_id=1, source_target_pairs={{0,4},{1,5},{2,6},{3,7},{4,0},{5,1},{6,2},{7,3},{8,12},{9,13},{10,... | collective-permute-start | bytes 147464 | tf_op jit(solution)/shard_map/ppermute | solution.py:476
  19.8 6.4 %collective-permute-start.5 = (bf16[48,512]{1,0:T(8,128)(2,1)S(1)}, bf16[48,512]{1,0:T(8,128)(2,1)S(1)}, u32[]{:S(2)}, u32[]{:S(2)}) collective-permute-start(bf16[48,512]{1,0:T(8,128)(2,1)S(1)} %get-tuple-element.42), channel_id=1, source_target_pairs={{0,8},{1,9},{2,10},{3,11},{4,12},{5,13},{6,14},{7,15},{8,0},{9,1},... | collective-permute-start | bytes 147464 | tf_op jit(solution)/shard_map/ppermute | solution.py:476
  22.4 6.1 %collective-permute-start.6 = (bf16[48,512]{1,0:T(8,128)(2,1)S(1)}, bf16[48,512]{1,0:T(8,128)(2,1)S(1)}, u32[]{:S(2)}, u32[]{:S(2)}) collective-permute-start(bf16[48,512]{1,0:T(8,128)(2,1)S(1)} %get-tuple-element.43), channel_id=1, source_target_pairs={{0,12},{1,13},{2,14},{3,15},{4,8},{5,9},{6,10},{7,11},{8,4},{9,5},... | collective-permute-start | bytes 147464 | tf_op jit(solution)/shard_map/ppermute | solution.py:476
  29.0 1.9 %collective-permute-start.8 = (bf16[192,512]{1,0:T(8,128)(2,1)S(1)}, bf16[192,512]{1,0:T(8,128)(2,1)S(1)}, u32[]{:S(2)}, u32[]{:S(2)}) collective-permute-start(bf16[192,512]{1,0:T(8,128)(2,1)S(1)} %constant_dynamic-update-slice_fusion.own_ref.refs_0_), channel_id=1, source_target_pairs={{0,1},{1,0},{2,3},{3,2},{4,5},{5,4},{6,7},{7,6},{8,9},{9,8},{10,11... | collective-permute-start | bytes 589832 | tf_op jit(solution)/shard_map/ppermute | solution.py:486
  29.2 7.2 %collective-permute-start.7 = (bf16[192,512]{1,0:T(8,128)(2,1)S(1)}, bf16[192,512]{1,0:T(8,128)(2,1)S(1)}, u32[]{:S(2)}, u32[]{:S(2)}) collective-permute-start(bf16[192,512]{1,0:T(8,128)(2,1)S(1)} %constant_dynamic-update-slice_fusion.own_ref.refs_0_), channel_id=1, source_target_pairs={{0,2},{1,3},{2,0},{3,1},{4,6},{5,7},{6,4},{7,5},{8,10},{9,11},{10,... | collective-permute-start | bytes 589832 | tf_op jit(solution)/shard_map/ppermute | solution.py:486
  36.4 1.4 %collective-permute-start.9 = (bf16[192,512]{1,0:T(8,128)(2,1)S(1)}, bf16[192,512]{1,0:T(8,128)(2,1)S(1)}, u32[]{:S(2)}, u32[]{:S(2)}) collective-permute-start(bf16[192,512]{1,0:T(8,128)(2,1)S(1)} %collective-permute-done.7.refs_0_), channel_id=1, source_target_pairs={{0,1},{1,0},{2,3},{3,2},{4,5},{5,4},{6,7},{7,6},{8,9},{9,8},{10,11... | collective-permute-start | bytes 589832 | tf_op jit(solution)/shard_map/ppermute | solution.py:486
  39.1 4.8 %collective-permute-start.10 = (bf16[48,512]{1,0:T(8,128)(2,1)S(1)}, bf16[48,512]{1,0:T(8,128)(2,1)S(1)}, u32[]{:S(2)}, u32[]{:S(2)}) collective-permute-start(bf16[48,512]{1,0:T(8,128)(2,1)S(1)} %get-tuple-element.54), channel_id=1, source_target_pairs={{0,4},{1,5},{2,6},{3,7},{4,0},{5,1},{6,2},{7,3},{8,12},{9,13},{10,... | collective-permute-start | bytes 147464 | tf_op jit(solution)/shard_map/ppermute | solution.py:510
  39.2 7.1 %collective-permute-start.11 = (bf16[48,512]{1,0:T(8,128)(2,1)S(1)}, bf16[48,512]{1,0:T(8,128)(2,1)S(1)}, u32[]{:S(2)}, u32[]{:S(2)}) collective-permute-start(bf16[48,512]{1,0:T(8,128)(2,1)S(1)} %get-tuple-element.55), channel_id=1, source_target_pairs={{0,8},{1,9},{2,10},{3,11},{4,12},{5,13},{6,14},{7,15},{8,0},{9,1},... | collective-permute-start | bytes 147464 | tf_op jit(solution)/shard_map/ppermute | solution.py:510
  41.3 6.0 %collective-permute-start.12 = (bf16[48,512]{1,0:T(8,128)(2,1)S(1)}, bf16[48,512]{1,0:T(8,128)(2,1)S(1)}, u32[]{:S(2)}, u32[]{:S(2)}) collective-permute-start(bf16[48,512]{1,0:T(8,128)(2,1)S(1)} %get-tuple-element.56), channel_id=1, source_target_pairs={{0,12},{1,13},{2,14},{3,15},{4,8},{5,9},{6,10},{7,11},{8,4},{9,5},... | collective-permute-start | bytes 147464 | tf_op jit(solution)/shard_map/ppermute | solution.py:510
